TPU v7x, 32 devices: a whole 2x2x4 slice. The times are simulated.
32 devices in a mesh: members: 2 (over y), comp: 4 (over z), lat: 2 (over x), sub: 2 (over core).
Axes of the slice: x: 2, y: 2, z: 4, core: 2. Of those that a mesh axis runs over, the one named last changes fastest.
Arguments:
- spectrum: float32 [1920, 4096], P('comp', ('members', 'lat', 'sub')), parts along dimension 1, may hold values from 0.05 to 2
- sea_mask: int32 [4096], P(('members', 'lat', 'sub')), parts along dimension 0, may hold values 0 or 1
- neighbours: int32 [4, 4096], P(None, ('members', 'lat', 'sub')), parts along dimension 1, may hold values from 0 to 2047, as said below
- substeps: int32 [30], replicated, may hold values from 1 to 6, as said below
- courant: float32 [30], replicated, may hold values from 0.2 to 0.7
- source_operator: bfloat16 [1920, 1920], P('sub'), may hold values from -0.125 to 0.125
Outputs:
- new_spectrum: float32 [1920, 4096], P('comp', ('members', 'lat', 'sub')), parts along dimension 1
There are 2 independent parts, one for each index of `members`. A program takes and returns all parts, laid end to end along the dimension named above; an argument that names none is the same for every part. Nothing has to cross between parts.
Inputs may be any that keep to these rules, and one draw needn't show every extreme that they name: Non-increasing with the band; the first band takes 6 substeps and the last band one. Points are numbered row by row, 256 to a row. The west and east neighbours lie in the same row, one or two columns away, wrapping around the row. The south neighbour lies in the row before and the north neighbour in the row after, within one column (wrapping); on the first and last row of the member's grid that neighbour is the point itself.
All inputs are finite; a program needn't handle non-finite values. No bound on the sum of `sea_mask` on one device may be relied on, other than what follows from the above.
Results may differ from a plain program's by a relative error of at most 0.0015.
Values may be sent and summed in bfloat16 or wider, within the bound.
No kernel may reach another device: no remote copies, remote signals or barrier semaphores. Data moves between devices by JAX's collectives and lax.ppermute only.
A program may use at most 64 MiB of HBM per device.

v0:
```python
import math

import jax
import jax.numpy as jnp
from jax import lax
from jax.sharding import PartitionSpec as P

NF = 30
ND = 64
NLON = 256
MAXSTEPS = 6
SRC_STEPS = 4


STEP_SIZE = 0.1


def extended(cells, sides, width):
    for axis, dim in sides:
        count = lax.axis_size(axis)
        ends = count - 1
        head = lax.slice_in_dim(cells, 0, width, axis=dim)
        tail = lax.slice_in_dim(cells, cells.shape[dim] - width, cells.shape[dim], axis=dim)
        cells = jnp.concatenate(
            [
                lax.ppermute(tail, axis, [(i, (i + 1) % count) for i in range(ends)]),
                cells,
                lax.ppermute(head, axis, [((i + 1) % count, i) for i in range(ends)]),
            ],
            axis=dim,
        )
    return cells


def bin_tables(global_bins, substeps, courant):
    frequency = global_bins // ND
    direction = global_bins % ND
    chosen = frequency[:, None] == jnp.arange(NF, dtype=jnp.int32)[None, :]
    bin_steps = jnp.sum(jnp.where(chosen, substeps[None, :], 0), axis=1)
    bin_speed = jnp.sum(jnp.where(chosen, courant[None, :], 0.0), axis=1)
    angles = (direction.astype(jnp.float32) + 0.5) * (2.0 * math.pi / ND)
    cosine = jnp.cos(angles)
    sine_dir = jnp.sin(angles)
    return (
        bin_steps,
        bin_speed * jnp.abs(cosine),
        bin_speed * jnp.abs(sine_dir),
        cosine > 0,
        sine_dir > 0,
    )


def offset_codes(neighbours, sea_float, points_local):
    position = lax.axis_index(("lat", "sub")) * points_local + jnp.arange(
        points_local, dtype=jnp.int32
    )
    column = position % NLON
    west_gap = (column - neighbours[0] % NLON) % NLON
    east_gap = (neighbours[1] % NLON - column) % NLON

    def vertical_code(index_row):
        column_move = (index_row % NLON - column + 1) % NLON - 1
        return jnp.where(index_row == position, 2, column_move)

    stacked = jnp.stack(
        [west_gap, east_gap, vertical_code(neighbours[2]), vertical_code(neighbours[3])]
    ).astype(jnp.float32)
    return jnp.concatenate([stacked, sea_float[None, :]], axis=0).reshape(
        5, points_local // NLON, NLON
    )


def column_roll(values, amount):
    return jnp.roll(values, amount, axis=-1)


def vertical_pick(other_rows, code_row, center):
    moved = jnp.where(
        code_row == -1.0,
        column_roll(other_rows, 1),
        jnp.where(code_row == 1.0, column_roll(other_rows, -1), other_rows),
    )
    return jnp.where(code_row == 2.0, center, moved)


def advance(substep, center, below, above, point_codes, tables):
    bin_steps, weight_x, weight_y, from_west, from_south = tables
    west_vals = jnp.where(
        point_codes[0][None] == 1.0, column_roll(center, 1), column_roll(center, 2)
    )
    east_vals = jnp.where(
        point_codes[1][None] == 1.0, column_roll(center, -1), column_roll(center, -2)
    )
    upwind_lon = jnp.where(from_west[:, None, None], west_vals, east_vals)
    south_vals = vertical_pick(below, point_codes[2][None], center)
    north_vals = vertical_pick(above, point_codes[3][None], center)
    upwind_lat = jnp.where(from_south[:, None, None], south_vals, north_vals)
    advanced = point_codes[4][None] * (
        center
        - weight_x[:, None, None] * (center - upwind_lon)
        - weight_y[:, None, None] * (center - upwind_lat)
    )
    return jnp.where((substep < bin_steps)[:, None, None], advanced, center)


def propagate(spec_part, global_bins, substeps, courant, point_codes):
    tables = bin_tables(global_bins, substeps, courant)
    bin_count = spec_part.shape[0]
    points_local = spec_part.shape[1]
    row_count = points_local // NLON
    field_now = spec_part.reshape(bin_count, row_count, NLON)
    for substep in range(MAXSTEPS):
        padded = extended(field_now, ((("lat", "sub"), 1),), 1)
        field_now = advance(substep, field_now, padded[:, :-2], padded[:, 2:], point_codes, tables)
    return field_now.reshape(bin_count, points_local)


def per_device(spectrum, sea_mask, neighbours, substeps, courant, source_operator):
    comp_index = lax.axis_index("comp")
    bins_local = spectrum.shape[0]
    points_local = spectrum.shape[1]
    sea_float = sea_mask.astype(jnp.float32)
    point_codes = offset_codes(neighbours, sea_float, points_local)
    field_start = sea_float[None, :] * spectrum
    first_bin = comp_index * bins_local
    held_bins = first_bin + jnp.arange(bins_local, dtype=jnp.int32)
    propagated = propagate(field_start, held_bins, substeps, courant, point_codes)
    outgoing = propagated.astype(jnp.bfloat16)
    owned_cols = lax.all_to_all(outgoing, "comp", split_axis=1, concat_axis=0, tiled=True)
    whole_operator = lax.all_gather(source_operator, "sub", axis=0, tiled=True)
    point_rows = owned_cols.T
    start_state = point_rows.astype(jnp.float32)
    state_now = start_state
    full_rows = point_rows
    for source_step in range(SRC_STEPS):
        driving = lax.dot_general(
            full_rows, whole_operator, (((1,), (1,)), ((), ())), preferred_element_type=jnp.float32
        )
        state_now = state_now + STEP_SIZE * state_now * driving
        if source_step + 1 < SRC_STEPS:
            full_rows = state_now.astype(jnp.bfloat16)
    returned = (state_now - start_state).astype(jnp.bfloat16).T
    home_bins = lax.all_to_all(returned, "comp", split_axis=0, concat_axis=1, tiled=True)
    return sea_float[None, :] * (propagated + home_bins.astype(jnp.float32))


def solution(mesh):
    placed = (
        P("comp", ("members", "lat", "sub")),
        P(("members", "lat", "sub")),
        P(None, ("members", "lat", "sub")),
        P(),
        P(),
        P("sub", None),
    )
    return jax.shard_map(
        per_device,
        mesh=mesh,
        in_specs=placed,
        out_specs=P("comp", ("members", "lat", "sub")),
        check_vma=False,
    )
```

profile of v0, /device:TPU:2, one launch (start us, length us, event | category | flops | bytes accessed | tf_op | source)
XLA Modules:
  0.0 158.7 jit_solution(9278967915208655400)
XLA Ops:
  6.5 0.7 convert_element_type.60
  7.2 1.3 broadcast_multiply_fusion
  8.5 0.3 copy.100
  8.9 0.1 fusion.208
  9.0 1.9 %collective-permute-start.1 = (f32[480,1,256]{0,2,1:T(8,128)S(1)}, f32[480,1,256]{0,2,1:T(8,128)S(1)}, u32[]{:S(2)}, u32[]{:S(2)}) collective-permute-start(f32[480,1,256]{0,2,1:T(8,128)S(1)} %get-tuple-element.124), channel_id=1, source_target_pairs={{1,0},{2,1},{3,2},{5,4},{6,5},{7,6},{9,8},{10,9},{11,10},{13,12},{... | collective-permute-start | bytes 1474568 | tf_op jit(solution)/shard_map/ppermute | solution.py:28
  10.9 2.6 %collective-permute-start = (f32[480,1,256]{0,2,1:T(8,128)S(1)}, f32[480,1,256]{0,2,1:T(8,128)S(1)}, u32[]{:S(2)}, u32[]{:S(2)}) collective-permute-start(f32[480,1,256]{0,2,1:T(8,128)S(1)} %get-tuple-element.123), channel_id=1, source_target_pairs={{0,1},{1,2},{2,3},{4,5},{5,6},{6,7},{8,9},{9,10},{10,11},{12,13},{... | collective-permute-start | bytes 1474568 | tf_op jit(solution)/shard_map/ppermute | solution.py:26
  13.7 0.1 select_reduce_fusion
  13.8 0.1 and_select_fusion.6
  14.1 0.1 select_reduce_fusion.1
  14.2 0.2 fusion.206
  14.5 3.1 %collective-permute-done.1 = f32[480,1,256]{0,2,1:T(8,128)S(1)} collective-permute-done((f32[480,1,256]{0,2,1:T(8,128)S(1)}, f32[480,1,256]{0,2,1:T(8,128)S(1)}, u32[]{:S(2)}, u32[]{:S(2)}) %collective-permute-start.1) | collective-permute-done | bytes 491552 | tf_op jit(solution)/shard_map/ppermute | solution.py:28
  17.6 4.0 %collective-permute-done = f32[480,1,256]{0,2,1:T(8,128)S(1)} collective-permute-done((f32[480,1,256]{0,2,1:T(8,128)S(1)}, f32[480,1,256]{0,2,1:T(8,128)S(1)}, u32[]{:S(2)}, u32[]{:S(2)}) %collective-permute-start) | collective-permute-done | bytes 491552 | tf_op jit(solution)/shard_map/ppermute | solution.py:26
  21.6 0.8 fusion.27
  22.4 3.3 %fusion.108 = f32[480,2,256]{0,2,1:T(8,128)S(1)} fusion(f32[480,2,256]{0,2,1:T(8,128)S(1)} %bitcast.72, f32[480,1,256]{0,2,1:T(8,128)S(1)} %collective-permute-done.1, f32[480,1,256]{0,2,1:T(8,128)S(1)} %collective-permute-done, f32[480,2,255]{0,2,1:T(8,128)S(1)} %get-tuple-element.112, f32[480,2,1]{0,2,1:T(1,128)S(1)} %get-tuple-element.118, ...), kind=kLoop, calls=%fused_computation.205 | loop fusion | flops 7372800 | bytes 10817184 | tf_op jit(solution)/shard_map/jit(_where)/select_n | solution.py:103
  25.7 0.1 fusion.205
  25.7 1.9 %collective-permute-start.3 = (f32[480,1,256]{0,2,1:T(8,128)S(1)}, f32[480,1,256]{0,2,1:T(8,128)S(1)}, u32[]{:S(2)}, u32[]{:S(2)}) collective-permute-start(f32[480,1,256]{0,2,1:T(8,128)S(1)} %get-tuple-element.110), channel_id=1, source_target_pairs={{1,0},{2,1},{3,2},{5,4},{6,5},{7,6},{9,8},{10,9},{11,10},{13,12},{... | collective-permute-start | bytes 1474568 | tf_op jit(solution)/shard_map/ppermute | solution.py:28
  27.7 2.4 %collective-permute-start.2 = (f32[480,1,256]{0,2,1:T(8,128)S(1)}, f32[480,1,256]{0,2,1:T(8,128)S(1)}, u32[]{:S(2)}, u32[]{:S(2)}) collective-permute-start(f32[480,1,256]{0,2,1:T(8,128)S(1)} %get-tuple-element.109), channel_id=1, source_target_pairs={{0,1},{1,2},{2,3},{4,5},{5,6},{6,7},{8,9},{9,10},{10,11},{12,13},{... | collective-permute-start | bytes 1474568 | tf_op jit(solution)/shard_map/ppermute | solution.py:26
  30.1 0.2 fusion.203
  30.4 4.0 %collective-permute-done.3 = f32[480,1,256]{0,2,1:T(8,128)S(1)} collective-permute-done((f32[480,1,256]{0,2,1:T(8,128)S(1)}, f32[480,1,256]{0,2,1:T(8,128)S(1)}, u32[]{:S(2)}, u32[]{:S(2)}) %collective-permute-start.3) | collective-permute-done | bytes 491552 | tf_op jit(solution)/shard_map/ppermute | solution.py:28
  34.3 3.8 %collective-permute-done.2 = f32[480,1,256]{0,2,1:T(8,128)S(1)} collective-permute-done((f32[480,1,256]{0,2,1:T(8,128)S(1)}, f32[480,1,256]{0,2,1:T(8,128)S(1)}, u32[]{:S(2)}, u32[]{:S(2)}) %collective-permute-start.2) | collective-permute-done | bytes 491552 | tf_op jit(solution)/shard_map/ppermute | solution.py:26
  38.2 0.8 fusion.23
  39.0 3.3 %fusion.94 = f32[480,2,256]{0,2,1:T(8,128)S(1)} fusion(f32[480,2,256]{0,2,1:T(8,128)S(1)} %fusion.108, f32[480,1,256]{0,2,1:T(8,128)S(1)} %collective-permute-done.3, f32[480,1,256]{0,2,1:T(8,128)S(1)} %collective-permute-done.2, f32[480,2,255]{0,2,1:T(8,128)S(1)} %get-tuple-element.100, f32[480,2,1]{0,2,1:T(1,128)S(1)} %get-tuple-element.104, ...), kind=kLoop, calls=%fused_computation.187 | loop fusion | flops 7372800 | bytes 10817184 | tf_op jit(solution)/shard_map/jit(_where)/select_n | solution.py:103
  42.3 0.1 fusion.202
  42.4 1.9 %collective-permute-start.5 = (f32[480,1,256]{0,2,1:T(8,128)S(1)}, f32[480,1,256]{0,2,1:T(8,128)S(1)}, u32[]{:S(2)}, u32[]{:S(2)}) collective-permute-start(f32[480,1,256]{0,2,1:T(8,128)S(1)} %get-tuple-element.96), channel_id=1, source_target_pairs={{1,0},{2,1},{3,2},{5,4},{6,5},{7,6},{9,8},{10,9},{11,10},{13,12},{... | collective-permute-start | bytes 1474568 | tf_op jit(solution)/shard_map/ppermute | solution.py:28
  44.3 2.4 %collective-permute-start.4 = (f32[480,1,256]{0,2,1:T(8,128)S(1)}, f32[480,1,256]{0,2,1:T(8,128)S(1)}, u32[]{:S(2)}, u32[]{:S(2)}) collective-permute-start(f32[480,1,256]{0,2,1:T(8,128)S(1)} %get-tuple-element.95), channel_id=1, source_target_pairs={{0,1},{1,2},{2,3},{4,5},{5,6},{6,7},{8,9},{9,10},{10,11},{12,13},{... | collective-permute-start | bytes 1474568 | tf_op jit(solution)/shard_map/ppermute | solution.py:26
  46.8 0.2 fusion.200
  47.0 4.0 %collective-permute-done.5 = f32[480,1,256]{0,2,1:T(8,128)S(1)} collective-permute-done((f32[480,1,256]{0,2,1:T(8,128)S(1)}, f32[480,1,256]{0,2,1:T(8,128)S(1)}, u32[]{:S(2)}, u32[]{:S(2)}) %collective-permute-start.5) | collective-permute-done | bytes 491552 | tf_op jit(solution)/shard_map/ppermute | solution.py:28
  51.0 3.8 %collective-permute-done.4 = f32[480,1,256]{0,2,1:T(8,128)S(1)} collective-permute-done((f32[480,1,256]{0,2,1:T(8,128)S(1)}, f32[480,1,256]{0,2,1:T(8,128)S(1)}, u32[]{:S(2)}, u32[]{:S(2)}) %collective-permute-start.4) | collective-permute-done | bytes 491552 | tf_op jit(solution)/shard_map/ppermute | solution.py:26
  54.8 0.8 fusion.19
  55.7 3.3 %fusion.80 = f32[480,2,256]{0,2,1:T(8,128)S(1)} fusion(f32[480,2,256]{0,2,1:T(8,128)S(1)} %fusion.94, f32[480,1,256]{0,2,1:T(8,128)S(1)} %collective-permute-done.5, f32[480,1,256]{0,2,1:T(8,128)S(1)} %collective-permute-done.4, f32[480,2,255]{0,2,1:T(8,128)S(1)} %get-tuple-element.86, f32[480,2,1]{0,2,1:T(1,128)S(1)} %get-tuple-element.90, ...), kind=kLoop, calls=%fused_computation.169 | loop fusion | flops 7372800 | bytes 10817184 | tf_op jit(solution)/shard_map/jit(_where)/select_n | solution.py:103
  59.0 0.1 fusion.199
  59.1 1.9 %collective-permute-start.7 = (f32[480,1,256]{0,2,1:T(8,128)S(1)}, f32[480,1,256]{0,2,1:T(8,128)S(1)}, u32[]{:S(2)}, u32[]{:S(2)}) collective-permute-start(f32[480,1,256]{0,2,1:T(8,128)S(1)} %get-tuple-element.82), channel_id=1, source_target_pairs={{1,0},{2,1},{3,2},{5,4},{6,5},{7,6},{9,8},{10,9},{11,10},{13,12},{... | collective-permute-start | bytes 1474568 | tf_op jit(solution)/shard_map/ppermute | solution.py:28
  61.0 2.4 %collective-permute-start.6 = (f32[480,1,256]{0,2,1:T(8,128)S(1)}, f32[480,1,256]{0,2,1:T(8,128)S(1)}, u32[]{:S(2)}, u32[]{:S(2)}) collective-permute-start(f32[480,1,256]{0,2,1:T(8,128)S(1)} %get-tuple-element.81), channel_id=1, source_target_pairs={{0,1},{1,2},{2,3},{4,5},{5,6},{6,7},{8,9},{9,10},{10,11},{12,13},{... | collective-permute-start | bytes 1474568 | tf_op jit(solution)/shard_map/ppermute | solution.py:26
  63.5 0.2 fusion.197
  63.7 4.0 %collective-permute-done.7 = f32[480,1,256]{0,2,1:T(8,128)S(1)} collective-permute-done((f32[480,1,256]{0,2,1:T(8,128)S(1)}, f32[480,1,256]{0,2,1:T(8,128)S(1)}, u32[]{:S(2)}, u32[]{:S(2)}) %collective-permute-start.7) | collective-permute-done | bytes 491552 | tf_op jit(solution)/shard_map/ppermute | solution.py:28
  67.7 3.8 %collective-permute-done.6 = f32[480,1,256]{0,2,1:T(8,128)S(1)} collective-permute-done((f32[480,1,256]{0,2,1:T(8,128)S(1)}, f32[480,1,256]{0,2,1:T(8,128)S(1)}, u32[]{:S(2)}, u32[]{:S(2)}) %collective-permute-start.6) | collective-permute-done | bytes 491552 | tf_op jit(solution)/shard_map/ppermute | solution.py:26
  71.5 0.8 fusion.15
  72.3 3.3 %fusion.66 = f32[480,2,256]{0,2,1:T(8,128)S(1)} fusion(f32[480,2,256]{0,2,1:T(8,128)S(1)} %fusion.80, f32[480,1,256]{0,2,1:T(8,128)S(1)} %collective-permute-done.7, f32[480,1,256]{0,2,1:T(8,128)S(1)} %collective-permute-done.6, f32[480,2,255]{0,2,1:T(8,128)S(1)} %get-tuple-element.72, f32[480,2,1]{0,2,1:T(1,128)S(1)} %get-tuple-element.76, ...), kind=kLoop, calls=%fused_computation.151 | loop fusion | flops 7372800 | bytes 10817184 | tf_op jit(solution)/shard_map/jit(_where)/select_n | solution.py:103
  75.7 1.9 %collective-permute-start.9 = (f32[480,1,256]{0,2,1:T(8,128)S(1)}, f32[480,1,256]{0,2,1:T(8,128)S(1)}, u32[]{:S(2)}, u32[]{:S(2)}) collective-permute-start(f32[480,1,256]{0,2,1:T(8,128)S(1)} %get-tuple-element.68), channel_id=1, source_target_pairs={{1,0},{2,1},{3,2},{5,4},{6,5},{7,6},{9,8},{10,9},{11,10},{13,12},{... | collective-permute-start | bytes 1474568 | tf_op jit(solution)/shard_map/ppermute | solution.py:28
  77.7 2.4 %collective-permute-start.8 = (f32[480,1,256]{0,2,1:T(8,128)S(1)}, f32[480,1,256]{0,2,1:T(8,128)S(1)}, u32[]{:S(2)}, u32[]{:S(2)}) collective-permute-start(f32[480,1,256]{0,2,1:T(8,128)S(1)} %get-tuple-element.67), channel_id=1, source_target_pairs={{0,1},{1,2},{2,3},{4,5},{5,6},{6,7},{8,9},{9,10},{10,11},{12,13},{... | collective-permute-start | bytes 1474568 | tf_op jit(solution)/shard_map/ppermute | solution.py:26
  80.1 0.2 fusion.194
  80.4 4.0 %collective-permute-done.9 = f32[480,1,256]{0,2,1:T(8,128)S(1)} collective-permute-done((f32[480,1,256]{0,2,1:T(8,128)S(1)}, f32[480,1,256]{0,2,1:T(8,128)S(1)}, u32[]{:S(2)}, u32[]{:S(2)}) %collective-permute-start.9) | collective-permute-done | bytes 491552 | tf_op jit(solution)/shard_map/ppermute | solution.py:28
  84.3 3.8 %collective-permute-done.8 = f32[480,1,256]{0,2,1:T(8,128)S(1)} collective-permute-done((f32[480,1,256]{0,2,1:T(8,128)S(1)}, f32[480,1,256]{0,2,1:T(8,128)S(1)}, u32[]{:S(2)}, u32[]{:S(2)}) %collective-permute-start.8) | collective-permute-done | bytes 491552 | tf_op jit(solution)/shard_map/ppermute | solution.py:26
  88.2 0.8 fusion.11
  89.0 3.3 %fusion.52 = f32[480,2,256]{0,2,1:T(8,128)S(1)} fusion(f32[480,2,256]{0,2,1:T(8,128)S(1)} %fusion.66, f32[480,1,256]{0,2,1:T(8,128)S(1)} %collective-permute-done.9, f32[480,1,256]{0,2,1:T(8,128)S(1)} %collective-permute-done.8, f32[480,2,255]{0,2,1:T(8,128)S(1)} %get-tuple-element.58, f32[480,2,1]{0,2,1:T(1,128)S(1)} %get-tuple-element.62, ...), kind=kLoop, calls=%fused_computation.133 | loop fusion | flops 7372800 | bytes 10817184 | tf_op jit(solution)/shard_map/jit(_where)/select_n | solution.py:103
  92.4 1.9 %collective-permute-start.11 = (f32[480,1,256]{0,2,1:T(8,128)S(1)}, f32[480,1,256]{0,2,1:T(8,128)S(1)}, u32[]{:S(2)}, u32[]{:S(2)}) collective-permute-start(f32[480,1,256]{0,2,1:T(8,128)S(1)} %get-tuple-element.54), channel_id=1, source_target_pairs={{1,0},{2,1},{3,2},{5,4},{6,5},{7,6},{9,8},{10,9},{11,10},{13,12},{... | collective-permute-start | bytes 1474568 | tf_op jit(solution)/shard_map/ppermute | solution.py:28
  94.3 2.6 %collective-permute-start.10 = (f32[480,1,256]{0,2,1:T(8,128)S(1)}, f32[480,1,256]{0,2,1:T(8,128)S(1)}, u32[]{:S(2)}, u32[]{:S(2)}) collective-permute-start(f32[480,1,256]{0,2,1:T(8,128)S(1)} %get-tuple-element.53), channel_id=1, source_target_pairs={{0,1},{1,2},{2,3},{4,5},{5,6},{6,7},{8,9},{9,10},{10,11},{12,13},{... | collective-permute-start | bytes 1474568 | tf_op jit(solution)/shard_map/ppermute | solution.py:26
  97.0 0.2 fusion.192
  97.2 3.8 %collective-permute-done.11 = f32[480,1,256]{0,2,1:T(8,128)S(1)} collective-permute-done((f32[480,1,256]{0,2,1:T(8,128)S(1)}, f32[480,1,256]{0,2,1:T(8,128)S(1)}, u32[]{:S(2)}, u32[]{:S(2)}) %collective-permute-start.11) | collective-permute-done | bytes 491552 | tf_op jit(solution)/shard_map/ppermute | solution.py:28
  101.0 3.8 %collective-permute-done.10 = f32[480,1,256]{0,2,1:T(8,128)S(1)} collective-permute-done((f32[480,1,256]{0,2,1:T(8,128)S(1)}, f32[480,1,256]{0,2,1:T(8,128)S(1)}, u32[]{:S(2)}, u32[]{:S(2)}) %collective-permute-start.10) | collective-permute-done | bytes 491552 | tf_op jit(solution)/shard_map/ppermute | solution.py:26
  104.8 0.8 fusion.8
  105.6 3.4 %fusion.188 = (bf16[480,2,256]{0,2,1:T(8,128)(2,1)S(1)}, f32[480,2,256]{0,2,1:T(8,128)S(1)}) fusion(f32[480,2,256]{0,2,1:T(8,128)S(1)} %fusion.52, f32[480,1,256]{0,2,1:T(8,128)S(1)} %collective-permute-done.11, f32[480,2,1]{0,2,1:T(1,128)S(1)} %get-tuple-element.40, f32[480,2,255]{0,2,1:T(8,128)S(1)} %get-tuple-element.51, pred[2,256]{1,0:T(4,128)(4,1)S(1)} %eq.181, ...), kind=kLoop, calls=%fused_computation.365 | loop fusion | flops 7618560 | bytes 11308704 | tf_op jit(solution)/shard_map/convert_element_type | solution.py:128
  109.0 0.3 copy.95
  109.3 14.6 %all_to_all.29 = bf16[480,4,128]{2,0,1:T(8,128)(2,1)S(1)} all-to-all(bf16[480,4,128]{2,0,1:T(8,128)(2,1)S(1)} %copy.95), channel_id=1, replica_groups=mesh['members'=2,'comp'=4,'lat'=2,'sub'=2] {'comp'}, dimensions={1} | all-to-all | bytes 983040 | tf_op jit(solution)/shard_map/all_to_all | solution.py:129
  123.9 0.3 copy.96
  124.2 5.5 %fusion.209 = f32[128,1920]{1,0:T(8,128)S(1)} fusion(bf16[1920,128]{1,0:T(8,128)(2,1)S(1)} %bitcast.74, bf16[1920,1920]{1,0:T(8,128)(2,1)} %all-gather.2.cloned.1.call-done), kind=kOutput, calls=%fused_computation.385 | convolution fusion | flops 943718400 | bytes 8847360 | tf_op jit(solution)/shard_map/dot_general | solution.py:136
  129.7 2.2 %fusion.144 = f32[128,1920]{1,0:T(8,128)S(1)} fusion(bf16[1920,1920]{1,0:T(8,128)(2,1)S(1)} %copy-done, f32[128,1920]{1,0:T(8,128)S(1)} %fusion.209, bf16[1920,128]{0,1:T(8,128)(2,1)S(1)} %copy.96), kind=kOutput, calls=%fused_computation.262 | convolution fusion | flops 944947200 | bytes 9830400 | tf_op jit(solution)/shard_map/dot_general | solution.py:136
  132.0 2.2 %fusion.146 = f32[128,1920]{1,0:T(8,128)S(1)} fusion(bf16[1920,1920]{1,0:T(8,128)(2,1)S(1)} %copy-done, f32[128,1920]{1,0:T(8,128)S(1)} %fusion.144, f32[128,1920]{1,0:T(8,128)S(1)} %fusion.209, bf16[1920,128]{0,1:T(8,128)(2,1)S(1)} %copy.96), kind=kOutput, calls=%fused_computation.263 | convolution fusion | flops 945684480 | bytes 10813440 | tf_op jit(solution)/shard_map/dot_general | solution.py:136
  134.2 2.2 %fusion.3 = bf16[1920,128]{0,1:T(8,128)(2,1)S(1)} fusion(bf16[1920,1920]{1,0:T(8,128)(2,1)S(1)} %copy-done, bf16[1920,128]{0,1:T(8,128)(2,1)S(1)} %copy.96, f32[128,1920]{1,0:T(8,128)S(1)} %fusion.146, f32[128,1920]{1,0:T(8,128)S(1)} %fusion.144, f32[128,1920]{1,0:T(8,128)S(1)} %fusion.209), kind=kOutput, calls=%fused_computation.40 | convolution fusion | flops 950108160 | bytes 11304960 | tf_op jit(solution)/shard_map/dot_general | solution.py:136
  136.4 1.0 copy.97
  137.4 3.5 %all-to-all-start.1 = ((bf16[4,480,128]{2,1,0:T(8,128)(2,1)}), bf16[4,480,128]{2,1,0:T(8,128)(2,1)S(1)}, u32[]{:S(2)}, u32[]{:S(2)}) async-start(bf16[4,480,128]{2,1,0:T(8,128)(2,1)} %bitcast.10), calls=%async_computation.1 | async-start | bytes 983040 | tf_op jit(solution)/shard_map/all_to_all | solution.py:143
  140.9 0.3 copy.99
  141.2 9.6 %all-to-all-done.1 = bf16[4,480,128]{2,1,0:T(8,128)(2,1)S(1)} async-done(((bf16[4,480,128]{2,1,0:T(8,128)(2,1)}), bf16[4,480,128]{2,1,0:T(8,128)(2,1)S(1)}, u32[]{:S(2)}, u32[]{:S(2)}) %all-to-all-start.1) | async-done | bytes 491552 | tf_op jit(solution)/shard_map/all_to_all | solution.py:143
  150.8 1.1 fusion.140
  (40 shorter events, 0.7 us)
Async XLA Ops:
  6.5 117.7 %all-gather.2.cloned.1.call-start = ((), (), s32[]{:S(2)}) async-start(), calls=%async_computation.2 | async-start | bytes 11059200 | tf_op jit(solution)/shard_map/all_gather | solution.py:130
  9.0 8.6 %collective-permute-start.1 = (f32[480,1,256]{0,2,1:T(8,128)S(1)}, f32[480,1,256]{0,2,1:T(8,128)S(1)}, u32[]{:S(2)}, u32[]{:S(2)}) collective-permute-start(f32[480,1,256]{0,2,1:T(8,128)S(1)} %get-tuple-element.124), channel_id=1, source_target_pairs={{1,0},{2,1},{3,2},{5,4},{6,5},{7,6},{9,8},{10,9},{11,10},{13,12},{... | collective-permute-start | bytes 1474568 | tf_op jit(solution)/shard_map/ppermute | solution.py:28
  10.9 2.7 %copy-start.2 = (f32[30]{0:T(128)S(1)}, f32[30]{0:T(128)}, u32[]{:S(2)}) copy-start(f32[30]{0:T(128)} %param.10) | copy-start | bytes 364
  10.9 2.9 %copy-start.1 = (s32[4,512]{1,0:T(4,128)S(1)}, s32[4,512]{1,0:T(4,128)}, u32[]{:S(2)}) copy-start(s32[4,512]{1,0:T(4,128)} %param.8) | copy-start | bytes 24580
  10.9 3.2 %copy-start.3 = (s32[30]{0:T(128)S(1)}, s32[30]{0:T(128)}, u32[]{:S(2)}) copy-start(s32[30]{0:T(128)} %param.9) | copy-start | bytes 364
  10.9 10.6 %collective-permute-start = (f32[480,1,256]{0,2,1:T(8,128)S(1)}, f32[480,1,256]{0,2,1:T(8,128)S(1)}, u32[]{:S(2)}, u32[]{:S(2)}) collective-permute-start(f32[480,1,256]{0,2,1:T(8,128)S(1)} %get-tuple-element.123), channel_id=1, source_target_pairs={{0,1},{1,2},{2,3},{4,5},{5,6},{6,7},{8,9},{9,10},{10,11},{12,13},{... | collective-permute-start | bytes 1474568 | tf_op jit(solution)/shard_map/ppermute | solution.py:26
  25.7 8.6 %collective-permute-start.3 = (f32[480,1,256]{0,2,1:T(8,128)S(1)}, f32[480,1,256]{0,2,1:T(8,128)S(1)}, u32[]{:S(2)}, u32[]{:S(2)}) collective-permute-start(f32[480,1,256]{0,2,1:T(8,128)S(1)} %get-tuple-element.110), channel_id=1, source_target_pairs={{1,0},{2,1},{3,2},{5,4},{6,5},{7,6},{9,8},{10,9},{11,10},{13,12},{... | collective-permute-start | bytes 1474568 | tf_op jit(solution)/shard_map/ppermute | solution.py:28
  27.7 10.5 %collective-permute-start.2 = (f32[480,1,256]{0,2,1:T(8,128)S(1)}, f32[480,1,256]{0,2,1:T(8,128)S(1)}, u32[]{:S(2)}, u32[]{:S(2)}) collective-permute-start(f32[480,1,256]{0,2,1:T(8,128)S(1)} %get-tuple-element.109), channel_id=1, source_target_pairs={{0,1},{1,2},{2,3},{4,5},{5,6},{6,7},{8,9},{9,10},{10,11},{12,13},{... | collective-permute-start | bytes 1474568 | tf_op jit(solution)/shard_map/ppermute | solution.py:26
  42.4 8.6 %collective-permute-start.5 = (f32[480,1,256]{0,2,1:T(8,128)S(1)}, f32[480,1,256]{0,2,1:T(8,128)S(1)}, u32[]{:S(2)}, u32[]{:S(2)}) collective-permute-start(f32[480,1,256]{0,2,1:T(8,128)S(1)} %get-tuple-element.96), channel_id=1, source_target_pairs={{1,0},{2,1},{3,2},{5,4},{6,5},{7,6},{9,8},{10,9},{11,10},{13,12},{... | collective-permute-start | bytes 1474568 | tf_op jit(solution)/shard_map/ppermute | solution.py:28
  44.3 10.5 %collective-permute-start.4 = (f32[480,1,256]{0,2,1:T(8,128)S(1)}, f32[480,1,256]{0,2,1:T(8,128)S(1)}, u32[]{:S(2)}, u32[]{:S(2)}) collective-permute-start(f32[480,1,256]{0,2,1:T(8,128)S(1)} %get-tuple-element.95), channel_id=1, source_target_pairs={{0,1},{1,2},{2,3},{4,5},{5,6},{6,7},{8,9},{9,10},{10,11},{12,13},{... | collective-permute-start | bytes 1474568 | tf_op jit(solution)/shard_map/ppermute | solution.py:26
  59.1 8.6 %collective-permute-start.7 = (f32[480,1,256]{0,2,1:T(8,128)S(1)}, f32[480,1,256]{0,2,1:T(8,128)S(1)}, u32[]{:S(2)}, u32[]{:S(2)}) collective-permute-start(f32[480,1,256]{0,2,1:T(8,128)S(1)} %get-tuple-element.82), channel_id=1, source_target_pairs={{1,0},{2,1},{3,2},{5,4},{6,5},{7,6},{9,8},{10,9},{11,10},{13,12},{... | collective-permute-start | bytes 1474568 | tf_op jit(solution)/shard_map/ppermute | solution.py:28
  61.0 10.5 %collective-permute-start.6 = (f32[480,1,256]{0,2,1:T(8,128)S(1)}, f32[480,1,256]{0,2,1:T(8,128)S(1)}, u32[]{:S(2)}, u32[]{:S(2)}) collective-permute-start(f32[480,1,256]{0,2,1:T(8,128)S(1)} %get-tuple-element.81), channel_id=1, source_target_pairs={{0,1},{1,2},{2,3},{4,5},{5,6},{6,7},{8,9},{9,10},{10,11},{12,13},{... | collective-permute-start | bytes 1474568 | tf_op jit(solution)/shard_map/ppermute | solution.py:26
  75.7 8.6 %collective-permute-start.9 = (f32[480,1,256]{0,2,1:T(8,128)S(1)}, f32[480,1,256]{0,2,1:T(8,128)S(1)}, u32[]{:S(2)}, u32[]{:S(2)}) collective-permute-start(f32[480,1,256]{0,2,1:T(8,128)S(1)} %get-tuple-element.68), channel_id=1, source_target_pairs={{1,0},{2,1},{3,2},{5,4},{6,5},{7,6},{9,8},{10,9},{11,10},{13,12},{... | collective-permute-start | bytes 1474568 | tf_op jit(solution)/shard_map/ppermute | solution.py:28
  77.7 10.5 %collective-permute-start.8 = (f32[480,1,256]{0,2,1:T(8,128)S(1)}, f32[480,1,256]{0,2,1:T(8,128)S(1)}, u32[]{:S(2)}, u32[]{:S(2)}) collective-permute-start(f32[480,1,256]{0,2,1:T(8,128)S(1)} %get-tuple-element.67), channel_id=1, source_target_pairs={{0,1},{1,2},{2,3},{4,5},{5,6},{6,7},{8,9},{9,10},{10,11},{12,13},{... | collective-permute-start | bytes 1474568 | tf_op jit(solution)/shard_map/ppermute | solution.py:26
  92.4 8.6 %collective-permute-start.11 = (f32[480,1,256]{0,2,1:T(8,128)S(1)}, f32[480,1,256]{0,2,1:T(8,128)S(1)}, u32[]{:S(2)}, u32[]{:S(2)}) collective-permute-start(f32[480,1,256]{0,2,1:T(8,128)S(1)} %get-tuple-element.54), channel_id=1, source_target_pairs={{1,0},{2,1},{3,2},{5,4},{6,5},{7,6},{9,8},{10,9},{11,10},{13,12},{... | collective-permute-start | bytes 1474568 | tf_op jit(solution)/shard_map/ppermute | solution.py:28
  94.3 10.5 %collective-permute-start.10 = (f32[480,1,256]{0,2,1:T(8,128)S(1)}, f32[480,1,256]{0,2,1:T(8,128)S(1)}, u32[]{:S(2)}, u32[]{:S(2)}) collective-permute-start(f32[480,1,256]{0,2,1:T(8,128)S(1)} %get-tuple-element.53), channel_id=1, source_target_pairs={{0,1},{1,2},{2,3},{4,5},{5,6},{6,7},{8,9},{9,10},{10,11},{12,13},{... | collective-permute-start | bytes 1474568 | tf_op jit(solution)/shard_map/ppermute | solution.py:26
  124.2 5.5 %copy-start = (bf16[1920,1920]{1,0:T(8,128)(2,1)S(1)}, bf16[1920,1920]{1,0:T(8,128)(2,1)}, u32[]{:S(2)}) copy-start(bf16[1920,1920]{1,0:T(8,128)(2,1)} %all-gather.2.cloned.1.call-done) | copy-start | bytes 22118404
  137.4 13.4 %all-to-all-start.1 = ((bf16[4,480,128]{2,1,0:T(8,128)(2,1)}), bf16[4,480,128]{2,1,0:T(8,128)(2,1)S(1)}, u32[]{:S(2)}, u32[]{:S(2)}) async-start(bf16[4,480,128]{2,1,0:T(8,128)(2,1)} %bitcast.10), calls=%async_computation.1 | async-start | bytes 983040 | tf_op jit(solution)/shard_map/all_to_all | solution.py:143
Sparse Core Ops, SparseCore 0:
  13.7 20.5 all-gather.1
where the time goes:
time: 159 us
  waiting for transfers between devices  55.5 us (35%)
  starting transfers between devices  29.9 us (19%)
  other arithmetic  28.4 us (18%)
  blocking collectives  14.6 us (9%)
  between operations  13.9 us (9%)
  matrix products  12.2 us (8%)
  local copies, waits for them, and re-layouts  4.18 us (3%)
    ppermute x6, waiting for transfers between devices, extended(): lax.ppermute(tail, axis, [(i, (i + 1) % count) for i in range(ends)])  23.1 us
    ppermute x6, waiting for transfers between devices, extended(): lax.ppermute(head, axis, [((i + 1) % count, i) for i in range(ends)])  22.8 us
    select_n x5, other arithmetic, advance(): return jnp.where((substep < bin_steps)[:, None, None], advanced, center)  16.6 us
    ppermute x6, starting transfers between devices, extended(): lax.ppermute(tail, axis, [(i, (i + 1) % count) for i in range(ends)])  14.9 us
    all_to_all x1, blocking collectives, per_device(): lax.all_to_all(outgoing, 'comp', split_axis=1, concat_axis=0, tiled=True)  14.6 us
    dot_general x4, matrix products, per_device(): lax.dot_general(full_rows, whole_operator, (((1,), (1,)), ((), ())), pref...  12.2 us
    ppermute x6, starting transfers between devices, extended(): lax.ppermute(head, axis, [((i + 1) % count, i) for i in range(ends)])  11.5 us
    all_to_all x1, waiting for transfers between devices, per_device(): lax.all_to_all(returned, 'comp', split_axis=0, concat_axis=1, tiled=True)  9.57 us
  transfers between devices with their start and end apart: 14, of which 13 were waited for; matrix products, arithmetic and copies ran while one was open for 18% of the time, Pallas kernels for 0%

commit v1 on v0

--- a/solution.py
+++ b/solution.py
@@ -1,8 +1,11 @@
+import functools
 import math
 
 import jax
 import jax.numpy as jnp
 from jax import lax
+from jax.experimental import pallas as pl
+from jax.experimental.pallas import tpu as pltpu
 from jax.sharding import PartitionSpec as P
 
 NF = 30
@@ -13,6 +16,8 @@
 
 
 STEP_SIZE = 0.1
+
+HALO_TYPE = jnp.float16
 
 
 def extended(cells, sides, width):
@@ -144,6 +149,330 @@
     return sea_float[None, :] * (propagated + home_bins.astype(jnp.float32))
 
 
+LANES = 128
+QUAD = 16
+SECTOR = 32
+
+
+def lane_pick(values, index):
+    return jnp.take_along_axis(values, index, axis=1, mode="promise_in_bounds")
+
+
+def make_tables(tab_ref, u, codes_of, north):
+    lane = lax.broadcasted_iota(jnp.int32, (QUAD, LANES), 1)
+    for half in range(2):
+        code = lambda i: jnp.broadcast_to(codes_of(i, half), (QUAD, LANES))
+        column = lane + LANES * half
+        west = (column + NLON - code(0).astype(jnp.int32)) % NLON
+        east = (column + code(1).astype(jnp.int32)) % NLON
+        move = jnp.where(north, code(3), code(2)).astype(jnp.int32)
+        lat_from = (column + NLON + move) % NLON
+        for slot, source in enumerate((west, east, lat_from)):
+            tab_ref[u, half, 2 * slot] = source % LANES
+            tab_ref[u, half, 2 * slot + 1] = (source // LANES == half).astype(jnp.int32)
+        tab_ref[u, half, 6] = code(4).astype(jnp.int32)
+
+
+def stencil_kernel(sizes, *refs):
+    bins_local, half_bins, rows_local, dependent = sizes
+    if dependent:
+        place, steps_ref, courant_ref, trig, own, own_codes, pair, near, far, start_out, field_out, tab = refs
+    else:
+        place, steps_ref, courant_ref, trig, own, own_codes, pair, start_out, field_out, tab = refs
+    lat, sub, parity, first_group = place[0], place[1], place[2], place[3]
+    chip_rows = 2 * rows_local
+    halo = chip_rows if dependent else 0
+    north = lat == (0 if dependent else 1)
+    flip = north.astype(jnp.int32)
+    pair_codes = half_bins
+    near_codes = half_bins // 2
+
+    def where_is(v):
+        core = (v // rows_local + flip) % 2
+        local = v % rows_local
+        local = local + flip * (rows_local - 1 - 2 * local)
+        return core, local, core == sub
+
+    for u in range(halo + chip_rows):
+        core, local, mine = where_is(u % chip_rows)
+
+        def codes_of(i, half):
+            at = pl.ds(pl.multiple_of(local * NLON + half * LANES, LANES), LANES)
+            if u < halo:
+                return jnp.where(
+                    mine,
+                    near[pl.ds(near_codes + i, 1), at],
+                    far[pl.ds(near_codes + i, 1), at],
+                )
+            return jnp.where(mine, own_codes[i : i + 1, at], pair[pl.ds(pair_codes + i, 1), at])
+
+        make_tables(tab, u, codes_of, north)
+
+    def block(index, carry):
+        sector, side = index // 2, index % 2
+        east = (side + flip) % 2
+        group = 2 * sector + parity
+        band = jnp.minimum((first_group + group) // 2, courant_ref.shape[0] - 1)
+        speed, count = courant_ref[band], steps_ref[band]
+        trig_row = pl.ds(pl.multiple_of(SECTOR * flip + QUAD * side, QUAD), QUAD)
+        part_row = pl.multiple_of(group * SECTOR + side * QUAD, QUAD)
+        own_row = jnp.minimum(sub * half_bins + part_row, bins_local - QUAD)
+        own_row = pl.multiple_of(own_row, QUAD)
+        sent_row = pl.multiple_of(sector * SECTOR + side * QUAD, QUAD)
+        field = []
+        for u in range(halo + chip_rows):
+            core, local, mine = where_is(u % chip_rows)
+            both = []
+            for half in range(2):
+                at = pl.ds(pl.multiple_of(local * NLON + half * LANES, LANES), LANES)
+                if u < halo:
+                    value = jnp.where(
+                        mine,
+                        near[pl.ds(sent_row, QUAD), at],
+                        far[pl.ds(sent_row, QUAD), at],
+                    )
+                else:
+                    value = jnp.where(
+                        mine,
+                        own[pl.ds(own_row, QUAD), at] * tab[u, half, 6].astype(jnp.float32),
+                        pair[pl.ds(part_row, QUAD), at],
+                    )
+                both.append(value)
+            field.append(both)
+        for t in range(MAXSTEPS):
+            now = jnp.where(t < count, speed, 0.0)
+            weight_x = now * trig[0, trig_row, :]
+            weight_y = now * trig[1, trig_row, :]
+            lowest = max(0, halo - (MAXSTEPS - 1 - t))
+            for u in reversed(range(lowest, halo + chip_rows)):
+                centre, behind = field[u], field[max(u - 1, 0)]
+                moved = []
+                for half in range(2):
+                    index_x = tab[u, half, 2 * east]
+                    same_x = tab[u, half, 2 * east + 1] == 1
+                    index_y = tab[u, half, 4]
+                    same_y = tab[u, half, 5] == 1
+                    sea = tab[u, half, 6].astype(jnp.float32)
+                    upwind_x = jnp.where(same_x, lane_pick(centre[half], index_x), lane_pick(centre[1 - half], index_x))
+                    upwind_y = jnp.where(same_y, lane_pick(behind[half], index_y), lane_pick(behind[1 - half], index_y))
+                    here = centre[half]
+                    moved.append(sea * (here - weight_x * (here - upwind_x) - weight_y * (here - upwind_y)))
+                field[u] = moved
+        for v in range(chip_rows):
+            core, local, mine = where_is(v)
+            for half in range(2):
+                value = field[halo + v][half]
+                quarter = local * 2 + half
+                start_out[quarter * 2 + core, pl.ds(sent_row, QUAD), :] = value.astype(jnp.bfloat16)
+                at = pl.ds(pl.multiple_of(local * NLON + half * LANES, LANES), LANES)
+                field_out[1 - mine.astype(jnp.int32), pl.ds(sent_row, QUAD), at] = value
+        return carry
+
+    lax.fori_loop(0, half_bins // (2 * QUAD), block, 0)
+
+
+def stencil(sizes, place, substeps, courant, trig, own, own_codes, pair, halos=()):
+    bins_local, half_bins, rows_local, dependent = sizes
+    blocks = 4 * rows_local
+    rows = (4 if dependent else 2) * rows_local
+    smem = pl.BlockSpec(memory_space=pltpu.SMEM)
+    vmem = pl.BlockSpec(memory_space=pltpu.VMEM)
+    cells = half_bins // 2 * rows_local * 2 * NLON
+    return pl.pallas_call(
+        functools.partial(stencil_kernel, sizes),
+        name="stencil_dependent" if dependent else "stencil_free",
+        in_specs=[smem] * 3 + [vmem] * (4 + len(halos)),
+        out_specs=[vmem, vmem],
+        out_shape=[
+            jax.ShapeDtypeStruct((blocks, half_bins // 2, LANES), jnp.bfloat16),
+            jax.ShapeDtypeStruct((2, half_bins // 2, rows_local * NLON), jnp.float32),
+        ],
+        scratch_shapes=[pltpu.VMEM((rows, 2, 7, QUAD, LANES), jnp.int32)],
+        cost_estimate=pl.CostEstimate(flops=cells * MAXSTEPS * 100, bytes_accessed=cells * 16, transcendentals=0),
+    )(place, substeps, courant, trig, own, own_codes, pair, *halos)
+
+
+def integrate_kernel(sizes, place, free, dependent, own_w, other_w, out, w_ref, state, driver, sem):
+    bins_local, half_bins, comps = sizes
+    lat, sub = place[0], place[1]
+    w_rows = own_w.shape[0]
+    pieces = 3
+    piece = w_rows // pieces
+    copies = []
+    for which, source in enumerate((own_w, other_w)):
+        for p in range(pieces):
+            at = pl.ds(p * piece, piece)
+            copy = pltpu.make_async_copy(source.at[at], w_ref.at[which, at], sem.at[which, p])
+            copy.start()
+            copies.append(copy)
+    sectors = half_bins // (2 * SECTOR)
+    groups = bins_local // SECTOR
+    for c in range(comps):
+        first = (c * groups) % 2
+        for s in range(2):
+            for k in range(sectors):
+                for dep, source in enumerate((free, dependent)):
+                    parity = (first + lat + dep) % 2
+                    row = c * bins_local + s * half_bins + (2 * k + parity) * SECTOR
+                    row = pl.ds(pl.multiple_of(row, SECTOR), SECTOR)
+                    block = source[2 * c + s, k * SECTOR : (k + 1) * SECTOR, :]
+                    driver[0, row, :] = block
+                    state[row, :] = block.astype(jnp.float32)
+    total = comps * bins_local
+    for step in range(SRC_STEPS):
+        read, write = step % 2, (step + 1) % 2
+        base = (0 if step == 0 else 2)
+        for which in range(2):
+            half_at = (sub + which) % 2 * w_rows
+            for p in range(pieces):
+                if step == 0:
+                    copies[which * pieces + p].wait()
+                drive = jnp.dot(
+                    w_ref[which, p * piece : (p + 1) * piece, :],
+                    driver[0 if step == 0 else 1 + step % 2, :total, :],
+                    preferred_element_type=jnp.float32,
+                )
+                row = pl.ds(pl.multiple_of(half_at + p * piece, 64), piece)
+                value = state[row, :]
+                value = value + STEP_SIZE * value * drive
+                if step + 1 < SRC_STEPS:
+                    state[row, :] = value
+                    driver[1 + (step + 1) % 2, row, :] = value.astype(jnp.bfloat16)
+                else:
+                    begun = driver[0, row, :].astype(jnp.float32)
+                    out[row, :] = (value - begun).astype(jnp.bfloat16)
+
+
+def integrate(sizes, place, free, dependent, own_w, other_w):
+    bins_local, half_bins, comps = sizes
+    total = comps * bins_local
+    spare = total + SECTOR
+    smem = pl.BlockSpec(memory_space=pltpu.SMEM)
+    vmem = pl.BlockSpec(memory_space=pltpu.VMEM)
+    hbm = pl.BlockSpec(memory_space=pl.ANY)
+    return pl.pallas_call(
+        functools.partial(integrate_kernel, sizes),
+        name="integrate",
+        in_specs=[smem, vmem, vmem, hbm, hbm],
+        out_specs=vmem,
+        out_shape=jax.ShapeDtypeStruct((total, LANES), jnp.bfloat16),
+        scratch_shapes=[
+            pltpu.VMEM((2,) + own_w.shape, jnp.bfloat16),
+            pltpu.VMEM((spare, LANES), jnp.float32),
+            pltpu.VMEM((3, spare, LANES), jnp.bfloat16),
+            pltpu.SemaphoreType.DMA((2, 3)),
+        ],
+        compiler_params=pltpu.CompilerParams(vmem_limit_bytes=40 << 20),
+        cost_estimate=pl.CostEstimate(
+            flops=2 * SRC_STEPS * total * total * LANES, bytes_accessed=2 * total * total, transcendentals=0
+        ),
+    )(place, free, dependent, own_w, other_w)
+
+
+def finish_kernel(sizes, place, mine_free, mine_dep, got_free, got_dep, raised, sea, out):
+    bins_local, half_bins = sizes
+    sub, parity = place[1], place[2]
+    for other, pair in enumerate(((mine_free, mine_dep), (got_free, got_dep))):
+        for k in range(half_bins // (2 * SECTOR)):
+            for dep, source in enumerate(pair):
+                row = (sub + other) % 2 * half_bins + (2 * k + (parity + dep) % 2) * SECTOR
+
+                @pl.when(row < bins_local)
+                def _():
+                    rows = pl.ds(pl.multiple_of(row, SECTOR), SECTOR)
+                    for j in range(out.shape[1] // LANES):
+                        at = slice(j * LANES, (j + 1) * LANES)
+                        value = source[0, k * SECTOR : (k + 1) * SECTOR, at]
+                        value = value + raised[j, rows, :].astype(jnp.float32)
+                        out[rows, at] = sea[0:1, at] * value
+
+
+def finish(sizes, place, mine_free, mine_dep, got_free, got_dep, raised, sea):
+    bins_local, half_bins = sizes
+    points = sea.shape[1]
+    smem = pl.BlockSpec(memory_space=pltpu.SMEM)
+    vmem = pl.BlockSpec(memory_space=pltpu.VMEM)
+    first = pl.BlockSpec((1, half_bins // 2, points), lambda i: (0, 0, 0))
+    return pl.pallas_call(
+        functools.partial(finish_kernel, sizes),
+        name="finish",
+        grid=(1,),
+        in_specs=[smem, first, first, first, first, vmem, vmem],
+        out_specs=vmem,
+        out_shape=jax.ShapeDtypeStruct((bins_local, points), jnp.float32),
+    )(place, mine_free, mine_dep, got_free, got_dep, raised, sea)
+
+
+def swap(values, bits):
+    count = lax.axis_size("lat") * lax.axis_size("sub")
+    return lax.ppermute(values, ("lat", "sub"), [(i, i ^ bits) for i in range(count)])
+
+
+def two_chip_device(spectrum, sea_mask, neighbours, substeps, courant, source_operator):
+    comp, lat, sub = (lax.axis_index(name) for name in ("comp", "lat", "sub"))
+    comps = lax.axis_size("comp")
+    bins_local, points_local = spectrum.shape
+    rows_local = points_local // NLON
+    groups = bins_local // SECTOR
+    half_bins = (groups + 3) // 4 * 2 * SECTOR
+    sea = sea_mask.astype(jnp.float32)
+    codes = offset_codes(neighbours, sea, points_local).reshape(5, points_local)
+    codes = codes.at[2:4].set(jnp.where(codes[2:4] == 2.0, 0.0, codes[2:4]))
+    codes = jnp.pad(codes, ((0, 3), (0, 0)))
+    first_group = comp * groups
+    parity = (first_group + lat) % 2
+    place_free = jnp.stack([lat, sub, parity, first_group + sub * (half_bins // SECTOR)])
+    place_dep = jnp.stack([lat, sub, 1 - parity, first_group + sub * (half_bins // SECTOR)])
+    angles = (jnp.arange(ND, dtype=jnp.float32) + 0.5) * (2.0 * math.pi / ND)
+    trig = jnp.abs(jnp.stack([jnp.cos(angles), jnp.sin(angles)]))
+    trig = jnp.broadcast_to(trig[:, :, None], (2, ND, LANES))
+
+    padded = jnp.pad(spectrum, ((0, 2 * half_bins - bins_local), (0, 0)))
+    to_pair = lax.dynamic_slice_in_dim(padded, (1 - sub) * half_bins, half_bins, 0) * sea[None, :]
+    to_pair = jnp.concatenate([to_pair, codes], axis=0)
+    sectors = padded.reshape(2, half_bins // (2 * SECTOR), 2, SECTOR, points_local)
+
+    def to_chip(core):
+        part = lax.dynamic_slice(
+            sectors,
+            (core, 0, parity, 0, 0),
+            (1, half_bins // (2 * SECTOR), 1, SECTOR, points_local),
+        ).reshape(half_bins // 2, points_local)
+        part = part * sea[None, :]
+        return jnp.concatenate([part, codes, codes], axis=0).astype(HALO_TYPE)
+
+    pair = swap(to_pair, 1)
+    near = swap(to_chip(sub), 2).astype(jnp.float32)
+    far = swap(to_chip(1 - sub), 3).astype(jnp.float32)
+    other_w = swap(source_operator, 1)
+
+    sizes = (bins_local, half_bins, rows_local)
+    free_start, free_field = stencil(sizes + (False,), place_free, substeps, courant, trig, spectrum, codes, pair)
+    free_state = lax.all_to_all(free_start, ("comp", "sub"), split_axis=0, concat_axis=0, tiled=True)
+    dep_start, dep_field = stencil(
+        sizes + (True,), place_dep, substeps, courant, trig, spectrum, codes, pair, (near, far)
+    )
+    dep_state = lax.all_to_all(dep_start, ("comp", "sub"), split_axis=0, concat_axis=0, tiled=True)
+    got_free = swap(free_field[1:], 1)
+    got_dep = swap(dep_field[1:], 1)
+    raised = integrate((bins_local, half_bins, comps), place_free, free_state, dep_state, source_operator, other_w)
+    raised = raised.reshape(comps, bins_local, LANES)
+    home = lax.all_to_all(raised, "comp", split_axis=0, concat_axis=0, tiled=True)
+    return finish((bins_local, half_bins), place_free, free_field, dep_field, got_free, got_dep, home, sea[None, :])
+
+
+def device_step(*arrays):
+    bins_local, points_local = arrays[0].shape
+    two_chips = (
+        lax.axis_size("lat") == 2
+        and lax.axis_size("sub") == 2
+        and bins_local % SECTOR == 0
+        and points_local % NLON == 0
+        and points_local == lax.axis_size("comp") * LANES
+    )
+    return (two_chip_device if two_chips else per_device)(*arrays)
+
+
 def solution(mesh):
     placed = (
         P("comp", ("members", "lat", "sub")),
@@ -154,7 +483,7 @@
         P("sub", None),
     )
     return jax.shard_map(
-        per_device,
+        device_step,
         mesh=mesh,
         in_specs=placed,
         out_specs=P("comp", ("members", "lat", "sub")),

time: 159 us -> 102 us (0.64)
  the two profiles are of different devices: /device:TPU:2 before, /device:TPU:0 now
where the time goes in v1:
time: 102 us; the launch traced here: 101 us
  Pallas kernels  43.7 us (43%)
  waiting for transfers between devices  18.2 us (18%)
  blocking collectives  14.8 us (15%)
  starting transfers between devices  12.9 us (13%)
  local copies, waits for them, and re-layouts  5.66 us (6%)
  other arithmetic  5.62 us (6%)
    pallas_call x2, Pallas kernels, stencil(): pl.pallas_call(functools.partial(stencil_kernel, sizes), name='stencil_de...  26.4 us
    all_to_all x1, blocking collectives, two_chip_device(): lax.all_to_all(free_start, ('comp', 'sub'), split_axis=0, concat_axis=0,...  14.8 us
    pallas_call x1, Pallas kernels, integrate(): pl.pallas_call(functools.partial(integrate_kernel, sizes), name='integrat...  14.8 us
    all_to_all x1, waiting for transfers between devices, two_chip_device(): lax.all_to_all(raised, 'comp', split_axis=0, concat_axis=0, tiled=True)  11.7 us
    ppermute x6, waiting for transfers between devices, swap(): lax.ppermute(values, ('lat', 'sub'), [(i, i ^ bits) for i in range(count)])  6.47 us
    all_to_all x1, starting transfers between devices, two_chip_device(): lax.all_to_all(dep_start, ('comp', 'sub'), split_axis=0, concat_axis=0, t...  5.21 us
    ppermute x6, starting transfers between devices, swap(): lax.ppermute(values, ('lat', 'sub'), [(i, i ^ bits) for i in range(count)])  4.25 us
    all_to_all x1, starting transfers between devices, two_chip_device(): lax.all_to_all(raised, 'comp', split_axis=0, concat_axis=0, tiled=True)  3.48 us
  transfers between devices with their start and end apart: 8, of which 5 were waited for; matrix products, arithmetic and copies ran while one was open for 8% of the time, Pallas kernels for 26%

profile of v1, /device:TPU:0, one launch (start us, length us, event | category | flops | bytes accessed | tf_op | source)
XLA Modules:
  0.0 101.2 jit_solution(15071133698981722215)
XLA Ops:
  0.0 0.5 collective-permute-start.5
  0.5 0.7 convert_element_type.19
  1.2 0.0 copy-start.9
  1.2 0.9 and_select_fusion.6
  2.2 0.0 copy-start.6
  2.2 1.1 %dynamic-slice_multiply_fusion = f32[256,512]{1,0:T(8,128)S(1)} fusion(s32[]{:T(128)S(6)} %select_n.102, f32[512]{0:T(512)S(1)} %convert_element_type.19, f32[480,512]{1,0:T(8,128)} %refs_4_.3), kind=kLoop, calls=%fused_computation.1 | loop fusion | flops 131072 | bytes 1509380 | tf_op jit(solution)/shard_map/mul | solution.py:431
  3.3 0.1 collective-permute-start
  3.4 1.3 %pad.11 = f32[512,512]{1,0:T(8,128)S(1)} pad(f32[480,512]{1,0:T(8,128)} %refs_4_.3, f32[]{:T(128)} %constant.126.clone.1), padding=0_32x0_0 | pad | bytes 2031620 | tf_op jit(solution)/shard_map/jit(_pad)/pad | solution.py:430
  4.7 0.1 constant_dynamic-slice_fusion
  4.8 0.1 fusion
  4.8 0.1 pad_maximum_fusion.1
  4.9 3.0 %collective-permute-start.1 = (f16[144,512]{1,0:T(8,128)(2,1)S(1)}, f16[144,512]{1,0:T(8,128)(2,1)S(1)}, u32[]{:S(2)}, u32[]{:S(2)}) collective-permute-start(f16[144,512]{1,0:T(8,128)(2,1)S(1)} %get-tuple-element.30), channel_id=1, source_target_pairs={{0,2},{1,3},{2,0},{3,1},{4,6},{5,7},{6,4},{7,5},{8,10},{9,11},{10,... | collective-permute-start | bytes 442376 | tf_op jit(solution)/shard_map/ppermute | solution.py:408
  8.0 0.0 collective-permute-start.2
  8.0 0.6 add_add_fusion.1.refs_0_
  8.6 4.1 %collective-permute-done.1 = f16[144,512]{1,0:T(8,128)(2,1)S(1)} collective-permute-done((f16[144,512]{1,0:T(8,128)(2,1)S(1)}, f16[144,512]{1,0:T(8,128)(2,1)S(1)}, u32[]{:S(2)}, u32[]{:S(2)}) %collective-permute-start.1) | collective-permute-done | bytes 147488 | tf_op jit(solution)/shard_map/ppermute | solution.py:408
  12.7 0.7 convert_element_type.20.refs_7_
  13.4 0.0 copy-done.9
  13.4 0.0 copy-done.6
  13.4 1.1 %collective-permute-done.2 = f16[144,512]{1,0:T(8,128)(2,1)S(1)} collective-permute-done((f16[144,512]{1,0:T(8,128)(2,1)S(1)}, f16[144,512]{1,0:T(8,128)(2,1)S(1)}, u32[]{:S(2)}, u32[]{:S(2)}) %collective-permute-start.2) | collective-permute-done | bytes 147488 | tf_op jit(solution)/shard_map/ppermute | solution.py:408
  14.5 0.8 convert_element_type.21.refs_8_
  15.3 0.0 collective-permute-done.refs_6_
  15.3 0.0 copy-start.2
  15.3 0.8 broadcast_in_dim.22.refs_3_
  16.1 0.0 copy-done.2
  16.1 15.4 %stencil_dependent.1 = (bf16[8,128,128]{2,1,0:T(8,128)(2,1)}, f32[2,128,512]{2,1,0:T(8,128)}) custom-call(s32[4]{0:T(128)} %add_add_fusion.1.refs_0_, s32[30]{0:T(128)} %refs_1_.3, f32[30]{0:T(128)} %refs_2_.3, f32[2,64,128]{2,1,0:T(8,128)} %broadcast_in_dim.22.refs_3_, f32[480,512]{1,0:T(8,128)} %refs_4_.3, f32[8,512]{1,0:T(8,128)} %copy-done.6, ...), custom_call_target="tpu_custom_call" | custom-call | flops 78643200 | bytes 2097152 | tf_op jit(solution)/shard_map/stencil_dependent/pallas_call | solution.py:281
  31.5 5.2 %all-to-all-start.1 = ((bf16[8,128,128]{2,1,0:T(8,128)(2,1)}), bf16[8,128,128]{2,1,0:T(8,128)(2,1)S(1)}, u32[]{:S(2)}, u32[]{:S(2)}) async-start(bf16[8,128,128]{2,1,0:T(8,128)(2,1)} %get-tuple-element.24), calls=%async_computation.1 | async-start | bytes 524288 | tf_op jit(solution)/shard_map/all_to_all | solution.py:455
  36.7 0.6 add_add_fusion.refs_0_.place
  37.3 11.0 %stencil_free.1 = (bf16[8,128,128]{2,1,0:T(8,128)(2,1)}, f32[2,128,512]{2,1,0:T(8,128)}) custom-call(s32[4]{0:T(128)} %add_add_fusion.refs_0_.place, s32[30]{0:T(128)} %refs_1_.3, f32[30]{0:T(128)} %refs_2_.3, f32[2,64,128]{2,1,0:T(8,128)} %broadcast_in_dim.22.refs_3_, f32[480,512]{1,0:T(8,128)} %refs_4_.3, f32[8,512]{1,0:T(8,128)} %copy-done.6, ...), custom_call_target="tpu_custom_call" | custom-call | flops 78643200 | bytes 2097152 | tf_op jit(solution)/shard_map/stencil_free/pallas_call | solution.py:281
  48.3 0.0 all-to-all-done.1.dependent
  48.3 14.8 %all_to_all.15.free = bf16[8,128,128]{2,1,0:T(8,128)(2,1)S(1)} all-to-all(bf16[8,128,128]{2,1,0:T(8,128)(2,1)} %get-tuple-element.23), channel_id=1, replica_groups=mesh['members'=2,'comp'=4,'lat'=2,'sub'=2] {'comp','sub'}, dimensions={0} | all-to-all | bytes 524288 | tf_op jit(solution)/shard_map/all_to_all | solution.py:451
  63.1 0.0 collective-permute-done.5.other_w
  63.1 0.0 copy-start
  63.1 0.6 copy-done
  63.7 0.0 copy-start.1
  63.7 2.0 %copy-done.1 = bf16[960,1920]{1,0:T(8,128)(2,1)S(1)} copy-done((bf16[960,1920]{1,0:T(8,128)(2,1)S(1)}, bf16[960,1920]{1,0:T(8,128)(2,1)}, u32[]{:S(2)}) %copy-start.1) | copy-done | bytes 3686424
  65.8 0.0 copy-start.4
  65.8 0.0 copy-start.5
  65.8 14.8 %integrate.1 = bf16[1920,128]{1,0:T(8,128)(2,1)} custom-call(s32[4]{0:T(128)S(1)} %copy-done, bf16[8,128,128]{2,1,0:T(8,128)(2,1)S(1)} %all_to_all.15.free, bf16[8,128,128]{2,1,0:T(8,128)(2,1)S(1)} %all-to-all-done.1.dependent, bf16[960,1920]{1,0:T(8,128)(2,1)S(1)} %copy-done.1, bf16[960,1920]{1,0:T(8,128)(2,1)} %collective-permute-done.5.other_w), custom_call_target="tpu_custom_call" | custom-call | flops 3774873600 | bytes 7372800 | tf_op jit(solution)/shard_map/integrate/pallas_call | solution.py:353
  80.6 3.5 %all-to-all-start.2 = ((bf16[4,480,128]{2,1,0:T(8,128)(2,1)}), bf16[4,480,128]{2,1,0:T(8,128)(2,1)S(1)}, u32[]{:S(2)}, u32[]{:S(2)}) async-start(bf16[4,480,128]{2,1,0:T(8,128)(2,1)} %bitcast.9), calls=%async_computation.2 | async-start | bytes 983040 | tf_op jit(solution)/shard_map/all_to_all | solution.py:460
  84.1 0.0 copy-done.4
  84.1 0.1 collective-permute-start.4
  84.2 0.0 copy-done.5
  84.2 0.5 collective-permute-start.3
  84.8 0.9 collective-permute-done.4.got_dep
  85.7 0.0 copy-start.7
  85.7 0.4 collective-permute-done.3.got_free
  86.1 0.0 copy-start.8
  86.1 11.7 %all-to-all-done.2.raised = bf16[4,480,128]{2,1,0:T(8,128)(2,1)S(1)} async-done(((bf16[4,480,128]{2,1,0:T(8,128)(2,1)}), bf16[4,480,128]{2,1,0:T(8,128)(2,1)S(1)}, u32[]{:S(2)}, u32[]{:S(2)}) %all-to-all-start.2) | async-done | bytes 491552 | tf_op jit(solution)/shard_map/all_to_all | solution.py:460
  97.8 0.0 copy-done.7
  97.8 0.0 copy-done.8
  97.8 0.0 copy-start.3
  97.8 0.8 copy-done.3
  98.6 2.5 %finish.1 = f32[480,512]{1,0:T(8,128)} custom-call(s32[4]{0:T(128)} %add_add_fusion.refs_0_.place, f32[2,128,512]{2,1,0:T(8,128)} %get-tuple-element.21.mine_free, f32[2,128,512]{2,1,0:T(8,128)} %get-tuple-element.22.mine_dep, f32[1,128,512]{2,1,0:T(8,128)} %copy-done.8, f32[1,128,512]{2,1,0:T(8,128)} %copy-done.7, bf16[4,480,128]{2,1,0:T(8,128)(2,1)} %copy-done.3, ...), custom_call_target="tpu_custom_call" | custom-call | tf_op jit(solution)/shard_map/finish/pallas_call | solution.py:396
  (9 shorter events, 0.2 us)
Async XLA Ops:
  0.0 63.1 %collective-permute-start.5 = (bf16[960,1920]{1,0:T(8,128)(2,1)}, bf16[960,1920]{1,0:T(8,128)(2,1)}, u32[]{:S(2)}, u32[]{:S(2)}) collective-permute-start(bf16[960,1920]{1,0:T(8,128)(2,1)} %own_w.1), channel_id=1, source_target_pairs={{0,1},{1,0},{2,3},{3,2},{4,5},{5,4},{6,7},{7,6},{8,9},{9,8},{10,11... | collective-permute-start | bytes 11059208 | tf_op jit(solution)/shard_map/ppermute | solution.py:408
  1.2 12.2 %copy-start.9 = (f32[512]{0:T(512)}, f32[512]{0:T(512)S(1)}, u32[]{:S(2)}) copy-start(f32[512]{0:T(512)S(1)} %convert_element_type.19) | copy-start | bytes 6148
  2.2 11.2 %copy-start.6 = (f32[8,512]{1,0:T(8,128)}, f32[8,512]{1,0:T(8,128)S(1)}, u32[]{:S(2)}) copy-start(f32[8,512]{1,0:T(8,128)S(1)} %get-tuple-element.28.refs_5_) | copy-start | bytes 49156
  3.3 12.0 %collective-permute-start = (f32[264,512]{1,0:T(8,128)S(1)}, f32[264,512]{1,0:T(8,128)S(1)}, u32[]{:S(2)}, u32[]{:S(2)}) collective-permute-start(f32[264,512]{1,0:T(8,128)S(1)} %pad_maximum_fusion), channel_id=1, source_target_pairs={{0,1},{1,0},{2,3},{3,2},{4,5},{5,4},{6,7},{7,6},{8,9},{9,8},{10,11... | collective-permute-start | bytes 1622024 | tf_op jit(solution)/shard_map/ppermute | solution.py:408
  4.9 7.7 %collective-permute-start.1 = (f16[144,512]{1,0:T(8,128)(2,1)S(1)}, f16[144,512]{1,0:T(8,128)(2,1)S(1)}, u32[]{:S(2)}, u32[]{:S(2)}) collective-permute-start(f16[144,512]{1,0:T(8,128)(2,1)S(1)} %get-tuple-element.30), channel_id=1, source_target_pairs={{0,2},{1,3},{2,0},{3,1},{4,6},{5,7},{6,4},{7,5},{8,10},{9,11},{10,... | collective-permute-start | bytes 442376 | tf_op jit(solution)/shard_map/ppermute | solution.py:408
  8.0 6.5 %collective-permute-start.2 = (f16[144,512]{1,0:T(8,128)(2,1)S(1)}, f16[144,512]{1,0:T(8,128)(2,1)S(1)}, u32[]{:S(2)}, u32[]{:S(2)}) collective-permute-start(f16[144,512]{1,0:T(8,128)(2,1)S(1)} %get-tuple-element.29), channel_id=1, source_target_pairs={{0,3},{1,2},{2,1},{3,0},{4,7},{5,6},{6,5},{7,4},{8,11},{9,10},{10,... | collective-permute-start | bytes 442376 | tf_op jit(solution)/shard_map/ppermute | solution.py:408
  15.3 0.8 copy-start.2
  31.5 16.8 %all-to-all-start.1 = ((bf16[8,128,128]{2,1,0:T(8,128)(2,1)}), bf16[8,128,128]{2,1,0:T(8,128)(2,1)S(1)}, u32[]{:S(2)}, u32[]{:S(2)}) async-start(bf16[8,128,128]{2,1,0:T(8,128)(2,1)} %get-tuple-element.24), calls=%async_computation.1 | async-start | bytes 524288 | tf_op jit(solution)/shard_map/all_to_all | solution.py:455
  63.1 0.6 copy-start
  63.7 2.0 %copy-start.1 = (bf16[960,1920]{1,0:T(8,128)(2,1)S(1)}, bf16[960,1920]{1,0:T(8,128)(2,1)}, u32[]{:S(2)}) copy-start(bf16[960,1920]{1,0:T(8,128)(2,1)} %own_w.1) | copy-start | bytes 11059204
  65.8 18.3 %copy-start.4 = (f32[2,128,512]{2,1,0:T(8,128)S(1)}, f32[2,128,512]{2,1,0:T(8,128)}, u32[]{:S(2)}) copy-start(f32[2,128,512]{2,1,0:T(8,128)} %get-tuple-element.22.mine_dep) | copy-start | bytes 1572868
  65.8 18.4 %copy-start.5 = (f32[2,128,512]{2,1,0:T(8,128)S(1)}, f32[2,128,512]{2,1,0:T(8,128)}, u32[]{:S(2)}) copy-start(f32[2,128,512]{2,1,0:T(8,128)} %get-tuple-element.21.mine_free) | copy-start | bytes 1572868
  80.6 17.2 %all-to-all-start.2 = ((bf16[4,480,128]{2,1,0:T(8,128)(2,1)}), bf16[4,480,128]{2,1,0:T(8,128)(2,1)S(1)}, u32[]{:S(2)}, u32[]{:S(2)}) async-start(bf16[4,480,128]{2,1,0:T(8,128)(2,1)} %bitcast.9), calls=%async_computation.2 | async-start | bytes 983040 | tf_op jit(solution)/shard_map/all_to_all | solution.py:460
  84.1 1.6 %collective-permute-start.4 = (f32[1,128,512]{2,1,0:T(8,128)S(1)}, f32[1,128,512]{2,1,0:T(8,128)S(1)}, u32[]{:S(2)}, u32[]{:S(2)}) collective-permute-start(f32[1,128,512]{2,1,0:T(8,128)S(1)} %slice.45), channel_id=1, source_target_pairs={{0,1},{1,0},{2,3},{3,2},{4,5},{5,4},{6,7},{7,6},{8,9},{9,8},{10,11... | collective-permute-start | bytes 786440 | tf_op jit(solution)/shard_map/ppermute | solution.py:408
  84.2 1.9 %collective-permute-start.3 = (f32[1,128,512]{2,1,0:T(8,128)S(1)}, f32[1,128,512]{2,1,0:T(8,128)S(1)}, u32[]{:S(2)}, u32[]{:S(2)}) collective-permute-start(f32[1,128,512]{2,1,0:T(8,128)S(1)} %slice.44), channel_id=1, source_target_pairs={{0,1},{1,0},{2,3},{3,2},{4,5},{5,4},{6,7},{7,6},{8,9},{9,8},{10,11... | collective-permute-start | bytes 786440 | tf_op jit(solution)/shard_map/ppermute | solution.py:408
  85.7 12.1 %copy-start.7 = (f32[1,128,512]{2,1,0:T(8,128)}, f32[1,128,512]{2,1,0:T(8,128)S(1)}, u32[]{:S(2)}) copy-start(f32[1,128,512]{2,1,0:T(8,128)S(1)} %collective-permute-done.4.got_dep) | copy-start | bytes 786436
  86.1 11.7 %copy-start.8 = (f32[1,128,512]{2,1,0:T(8,128)}, f32[1,128,512]{2,1,0:T(8,128)S(1)}, u32[]{:S(2)}) copy-start(f32[1,128,512]{2,1,0:T(8,128)S(1)} %collective-permute-done.3.got_free) | copy-start | bytes 786436
  97.8 0.8 copy-start.3

commit v2 on v1

--- a/solution.py
+++ b/solution.py
@@ -16,8 +16,6 @@
 
 
 STEP_SIZE = 0.1
-
-HALO_TYPE = jnp.float16
 
 
 def extended(cells, sides, width):
@@ -150,42 +148,132 @@
 
 
 LANES = 128
+TILE = 8
 QUAD = 16
 SECTOR = 32
+CODE_SCALE = 32767.5
 
 
 def lane_pick(values, index):
     return jnp.take_along_axis(values, index, axis=1, mode="promise_in_bounds")
 
 
-def make_tables(tab_ref, u, codes_of, north):
-    lane = lax.broadcasted_iota(jnp.int32, (QUAD, LANES), 1)
-    for half in range(2):
-        code = lambda i: jnp.broadcast_to(codes_of(i, half), (QUAD, LANES))
-        column = lane + LANES * half
-        west = (column + NLON - code(0).astype(jnp.int32)) % NLON
-        east = (column + code(1).astype(jnp.int32)) % NLON
-        move = jnp.where(north, code(3), code(2)).astype(jnp.int32)
-        lat_from = (column + NLON + move) % NLON
-        for slot, source in enumerate((west, east, lat_from)):
-            tab_ref[u, half, 2 * slot] = source % LANES
-            tab_ref[u, half, 2 * slot + 1] = (source // LANES == half).astype(jnp.int32)
-        tab_ref[u, half, 6] = code(4).astype(jnp.int32)
+def split_columns(first, second):
+    lane = lax.broadcasted_iota(jnp.int32, first.shape, 1)
+    even, low = 2 * lane % LANES, lane < LANES // 2
+    return (
+        jnp.where(low, lane_pick(first, even), lane_pick(second, even)),
+        jnp.where(low, lane_pick(first, even + 1), lane_pick(second, even + 1)),
+    )
+
+
+def join_columns(even, odd):
+    lane = lax.broadcasted_iota(jnp.int32, even.shape, 1)
+    index, is_even = lane // 2, lane % 2 == 0
+    upper = index + LANES // 2
+    return (
+        jnp.where(is_even, lane_pick(even, index), lane_pick(odd, index)),
+        jnp.where(is_even, lane_pick(even, upper), lane_pick(odd, upper)),
+    )
+
+
+def encode(values):
+    return ((values * CODE_SCALE + 0.5).astype(jnp.int32) - 32768).astype(jnp.int16)
+
+
+def decode(values):
+    return (values.astype(jnp.int32) + 32768).astype(jnp.float32) * (1.0 / CODE_SCALE)
+
+
+def pack_kernel(sizes, place, spectrum, neighbours, sea_mask, mine, to_pair, to_near, to_far):
+    bins_local, half_bins, rows_local = sizes
+    sub, parity = place[1], place[2]
+    sectors = half_bins // (2 * SECTOR)
+    for row in range(rows_local):
+        halves = [slice(row * NLON + h * LANES, row * NLON + (h + 1) * LANES) for h in range(2)]
+        sea = [sea_mask[0:1, at].astype(jnp.float32) for at in halves]
+        moves = []
+        for h, at in enumerate(halves):
+            lane = lax.broadcasted_iota(jnp.int32, (4, LANES), 1) + h * LANES
+            move = (neighbours[:, at] - lane + NLON // 2) % NLON - NLON // 2
+            moves.append(jnp.concatenate([move.astype(jnp.float32), sea[h], jnp.zeros((3, LANES))], axis=0))
+        codes = split_columns(*moves)
+        for h, at in enumerate(halves):
+            mine[half_bins : half_bins + TILE, at] = codes[h]
+            to_pair[half_bins : half_bins + TILE, at] = codes[h]
+            coded = codes[h].astype(jnp.int32).astype(jnp.int16)
+            to_near[half_bins // 2 : half_bins // 2 + TILE, at] = coded
+            to_far[half_bins // 2 : half_bins // 2 + TILE, at] = coded
+    sea_rows = [
+        jnp.broadcast_to(sea_mask[0:1, j * LANES : (j + 1) * LANES].astype(jnp.float32), (SECTOR, LANES))
+        for j in range(2 * rows_local)
+    ]
+
+    def sector_of(index, carry):
+        core, group = index // (2 * sectors), index % (2 * sectors)
+        source = jnp.minimum(core * half_bins + group * SECTOR, bins_local - SECTOR)
+        source = pl.ds(pl.multiple_of(source, SECTOR), SECTOR)
+        target = pl.ds(pl.multiple_of(group * SECTOR, SECTOR), SECTOR)
+        sent = pl.ds(pl.multiple_of(group // 2 * SECTOR, SECTOR), SECTOR)
+        blocks = []
+        for row in range(rows_local):
+            pair = [
+                spectrum[source, (2 * row + h) * LANES : (2 * row + h + 1) * LANES] * sea_rows[2 * row + h]
+                for h in range(2)
+            ]
+            blocks += split_columns(*pair)
+
+        @pl.when(core == sub)
+        def _():
+            for j, block in enumerate(blocks):
+                mine[target, j * LANES : (j + 1) * LANES] = block
+
+        @pl.when(core != sub)
+        def _():
+            for j, block in enumerate(blocks):
+                to_pair[target, j * LANES : (j + 1) * LANES] = block
+
+        @pl.when((group % 2 == parity) & (core == sub))
+        def _():
+            for j, block in enumerate(blocks):
+                to_near[sent, j * LANES : (j + 1) * LANES] = encode(block)
+
+        @pl.when((group % 2 == parity) & (core != sub))
+        def _():
+            for j, block in enumerate(blocks):
+                to_far[sent, j * LANES : (j + 1) * LANES] = encode(block)
+
+        return carry
+
+    lax.fori_loop(0, 4 * sectors, sector_of, 0)
+
+
+def pack(sizes, place, spectrum, neighbours, sea_mask):
+    bins_local, half_bins, rows_local = sizes
+    points = rows_local * NLON
+    smem = pl.BlockSpec(memory_space=pltpu.SMEM)
+    vmem = pl.BlockSpec(memory_space=pltpu.VMEM)
+    return pl.pallas_call(
+        functools.partial(pack_kernel, sizes),
+        name="pack",
+        in_specs=[smem, vmem, vmem, vmem],
+        out_specs=[vmem] * 4,
+        out_shape=[jax.ShapeDtypeStruct((half_bins + TILE, points), jnp.float32)] * 2
+        + [jax.ShapeDtypeStruct((half_bins // 2 + TILE, points), jnp.int16)] * 2,
+    )(place, spectrum, neighbours, sea_mask)
 
 
 def stencil_kernel(sizes, *refs):
-    bins_local, half_bins, rows_local, dependent = sizes
+    half_bins, rows_local, dependent = sizes
     if dependent:
-        place, steps_ref, courant_ref, trig, own, own_codes, pair, near, far, start_out, field_out, tab = refs
+        place, steps_ref, courant_ref, trig, mine, pair, near, far, start_out, field_out, tab = refs
     else:
-        place, steps_ref, courant_ref, trig, own, own_codes, pair, start_out, field_out, tab = refs
+        place, steps_ref, courant_ref, trig, mine, pair, start_out, field_out, tab = refs
     lat, sub, parity, first_group = place[0], place[1], place[2], place[3]
     chip_rows = 2 * rows_local
     halo = chip_rows if dependent else 0
     north = lat == (0 if dependent else 1)
     flip = north.astype(jnp.int32)
-    pair_codes = half_bins
-    near_codes = half_bins // 2
 
     def where_is(v):
         core = (v // rows_local + flip) % 2
@@ -193,86 +281,100 @@
         local = local + flip * (rows_local - 1 - 2 * local)
         return core, local, core == sub
 
+    def lanes_of(local, half):
+        return pl.ds(pl.multiple_of(local * NLON + half * LANES, LANES), LANES)
+
     for u in range(halo + chip_rows):
-        core, local, mine = where_is(u % chip_rows)
-
-        def codes_of(i, half):
-            at = pl.ds(pl.multiple_of(local * NLON + half * LANES, LANES), LANES)
+        core, local, here = where_is(u % chip_rows)
+        for half in range(2):
+            at = lanes_of(local, half)
             if u < halo:
-                return jnp.where(
-                    mine,
-                    near[pl.ds(near_codes + i, 1), at],
-                    far[pl.ds(near_codes + i, 1), at],
-                )
-            return jnp.where(mine, own_codes[i : i + 1, at], pair[pl.ds(pair_codes + i, 1), at])
-
-        make_tables(tab, u, codes_of, north)
-
-    def block(index, carry):
-        sector, side = index // 2, index % 2
-        east = (side + flip) % 2
+                rows = slice(half_bins // 2, half_bins // 2 + TILE)
+                codes = jnp.where(here, near[rows, at].astype(jnp.int32), far[rows, at].astype(jnp.int32))
+                codes = codes.astype(jnp.float32)
+            else:
+                rows = slice(half_bins, half_bins + TILE)
+                codes = jnp.where(here, mine[rows, at], pair[rows, at])
+            wide = lambda i: jnp.broadcast_to(codes[i : i + 1], (TILE, LANES))
+            tab[u, half, 0] = wide(0)
+            tab[u, half, 1] = wide(1)
+            tab[u, half, 2] = jnp.where(north, wide(3), wide(2))
+            tab[u, half, 3] = wide(4)
+
+    def tiles(value):
+        return value.reshape(QUAD // TILE, TILE, LANES)
+
+    def turn(value, amount):
+        return pltpu.roll(value.reshape(QUAD, LANES), amount % LANES, 1).reshape(QUAD // TILE, TILE, LANES)
+
+    def block(sector, east):
         group = 2 * sector + parity
         band = jnp.minimum((first_group + group) // 2, courant_ref.shape[0] - 1)
         speed, count = courant_ref[band], steps_ref[band]
+        side = (flip + east) % 2
         trig_row = pl.ds(pl.multiple_of(SECTOR * flip + QUAD * side, QUAD), QUAD)
-        part_row = pl.multiple_of(group * SECTOR + side * QUAD, QUAD)
-        own_row = jnp.minimum(sub * half_bins + part_row, bins_local - QUAD)
-        own_row = pl.multiple_of(own_row, QUAD)
-        sent_row = pl.multiple_of(sector * SECTOR + side * QUAD, QUAD)
+        part_row = pl.ds(pl.multiple_of(group * SECTOR + side * QUAD, QUAD), QUAD)
+        sent_row = pl.ds(pl.multiple_of(sector * SECTOR + side * QUAD, QUAD), QUAD)
+        trig_x, trig_y = tiles(trig[0, trig_row, :]), tiles(trig[1, trig_row, :])
         field = []
         for u in range(halo + chip_rows):
-            core, local, mine = where_is(u % chip_rows)
+            core, local, here = where_is(u % chip_rows)
             both = []
             for half in range(2):
-                at = pl.ds(pl.multiple_of(local * NLON + half * LANES, LANES), LANES)
+                at = lanes_of(local, half)
                 if u < halo:
                     value = jnp.where(
-                        mine,
-                        near[pl.ds(sent_row, QUAD), at],
-                        far[pl.ds(sent_row, QUAD), at],
+                        here, near[sent_row, at].astype(jnp.int32), far[sent_row, at].astype(jnp.int32)
                     )
+                    value = (value + 32768).astype(jnp.float32) * (1.0 / CODE_SCALE)
                 else:
-                    value = jnp.where(
-                        mine,
-                        own[pl.ds(own_row, QUAD), at] * tab[u, half, 6].astype(jnp.float32),
-                        pair[pl.ds(part_row, QUAD), at],
-                    )
-                both.append(value)
+                    value = jnp.where(here, mine[part_row, at], pair[part_row, at])
+                both.append(tiles(value))
             field.append(both)
         for t in range(MAXSTEPS):
             now = jnp.where(t < count, speed, 0.0)
-            weight_x = now * trig[0, trig_row, :]
-            weight_y = now * trig[1, trig_row, :]
+            weight_x, weight_y = now * trig_x, now * trig_y
+            keep = 1.0 - weight_x - weight_y
             lowest = max(0, halo - (MAXSTEPS - 1 - t))
             for u in reversed(range(lowest, halo + chip_rows)):
-                centre, behind = field[u], field[max(u - 1, 0)]
+                (even, odd), (even_b, odd_b) = field[u], field[max(u - 1, 0)]
                 moved = []
                 for half in range(2):
-                    index_x = tab[u, half, 2 * east]
-                    same_x = tab[u, half, 2 * east + 1] == 1
-                    index_y = tab[u, half, 4]
-                    same_y = tab[u, half, 5] == 1
-                    sea = tab[u, half, 6].astype(jnp.float32)
-                    upwind_x = jnp.where(same_x, lane_pick(centre[half], index_x), lane_pick(centre[1 - half], index_x))
-                    upwind_y = jnp.where(same_y, lane_pick(behind[half], index_y), lane_pick(behind[1 - half], index_y))
-                    here = centre[half]
-                    moved.append(sea * (here - weight_x * (here - upwind_x) - weight_y * (here - upwind_y)))
+                    move_x, move_y = tab[u, half, east], tab[u, half, 2]
+                    near_x = (move_x == (1.0 if east else -1.0))[None]
+                    back, ahead = (move_y == -1.0)[None], (move_y == 1.0)[None]
+                    if half == 0:
+                        one = odd if east else turn(odd, 1)
+                        two = turn(even, -1 if east else 1)
+                        centre, same = even, even_b
+                        minus, plus = turn(odd_b, 1), odd_b
+                    else:
+                        one = turn(even, -1) if east else even
+                        two = turn(odd, -1 if east else 1)
+                        centre, same = odd, odd_b
+                        minus, plus = even_b, turn(even_b, -1)
+                    upwind_x = jnp.where(near_x, one, two)
+                    upwind_y = jnp.where(back, minus, jnp.where(ahead, plus, same))
+                    value = keep * centre + weight_x * upwind_x + weight_y * upwind_y
+                    moved.append(tab[u, half, 3][None] * value)
                 field[u] = moved
         for v in range(chip_rows):
-            core, local, mine = where_is(v)
+            core, local, here = where_is(v)
             for half in range(2):
-                value = field[halo + v][half]
-                quarter = local * 2 + half
-                start_out[quarter * 2 + core, pl.ds(sent_row, QUAD), :] = value.astype(jnp.bfloat16)
-                at = pl.ds(pl.multiple_of(local * NLON + half * LANES, LANES), LANES)
-                field_out[1 - mine.astype(jnp.int32), pl.ds(sent_row, QUAD), at] = value
+                value = field[halo + v][half].reshape(QUAD, LANES)
+                start_out[(local * 2 + half) * 2 + core, sent_row, :] = value.astype(jnp.bfloat16)
+                field_out[1 - here.astype(jnp.int32), sent_row, lanes_of(local, half)] = value
+
+    def both_sides(sector, carry):
+        block(sector, 0)
+        block(sector, 1)
         return carry
 
-    lax.fori_loop(0, half_bins // (2 * QUAD), block, 0)
-
-
-def stencil(sizes, place, substeps, courant, trig, own, own_codes, pair, halos=()):
-    bins_local, half_bins, rows_local, dependent = sizes
+    lax.fori_loop(0, half_bins // (2 * SECTOR), both_sides, 0)
+
+
+def stencil(sizes, place, substeps, courant, trig, *fields):
+    half_bins, rows_local, dependent = sizes
     blocks = 4 * rows_local
     rows = (4 if dependent else 2) * rows_local
     smem = pl.BlockSpec(memory_space=pltpu.SMEM)
@@ -281,15 +383,15 @@
     return pl.pallas_call(
         functools.partial(stencil_kernel, sizes),
         name="stencil_dependent" if dependent else "stencil_free",
-        in_specs=[smem] * 3 + [vmem] * (4 + len(halos)),
+        in_specs=[smem] * 3 + [vmem] * (1 + len(fields)),
         out_specs=[vmem, vmem],
         out_shape=[
             jax.ShapeDtypeStruct((blocks, half_bins // 2, LANES), jnp.bfloat16),
             jax.ShapeDtypeStruct((2, half_bins // 2, rows_local * NLON), jnp.float32),
         ],
-        scratch_shapes=[pltpu.VMEM((rows, 2, 7, QUAD, LANES), jnp.int32)],
+        scratch_shapes=[pltpu.VMEM((rows, 2, 4, TILE, LANES), jnp.float32)],
         cost_estimate=pl.CostEstimate(flops=cells * MAXSTEPS * 100, bytes_accessed=cells * 16, transcendentals=0),
-    )(place, substeps, courant, trig, own, own_codes, pair, *halos)
+    )(place, substeps, courant, trig, *fields)
 
 
 def integrate_kernel(sizes, place, free, dependent, own_w, other_w, out, w_ref, state, driver, sem):
@@ -320,19 +422,18 @@
                     state[row, :] = block.astype(jnp.float32)
     total = comps * bins_local
     for step in range(SRC_STEPS):
-        read, write = step % 2, (step + 1) % 2
-        base = (0 if step == 0 else 2)
         for which in range(2):
             half_at = (sub + which) % 2 * w_rows
-            for p in range(pieces):
+            stretch = piece if step == 0 else w_rows
+            for p in range(w_rows // stretch):
                 if step == 0:
                     copies[which * pieces + p].wait()
                 drive = jnp.dot(
-                    w_ref[which, p * piece : (p + 1) * piece, :],
+                    w_ref[which, p * stretch : (p + 1) * stretch, :],
                     driver[0 if step == 0 else 1 + step % 2, :total, :],
                     preferred_element_type=jnp.float32,
                 )
-                row = pl.ds(pl.multiple_of(half_at + p * piece, 64), piece)
+                row = pl.ds(pl.multiple_of(half_at + p * stretch, 64), stretch)
                 value = state[row, :]
                 value = value + STEP_SIZE * value * drive
                 if step + 1 < SRC_STEPS:
@@ -362,16 +463,21 @@
             pltpu.VMEM((3, spare, LANES), jnp.bfloat16),
             pltpu.SemaphoreType.DMA((2, 3)),
         ],
-        compiler_params=pltpu.CompilerParams(vmem_limit_bytes=40 << 20),
+        compiler_params=pltpu.CompilerParams(vmem_limit_bytes=60 << 20),
         cost_estimate=pl.CostEstimate(
             flops=2 * SRC_STEPS * total * total * LANES, bytes_accessed=2 * total * total, transcendentals=0
         ),
     )(place, free, dependent, own_w, other_w)
 
 
-def finish_kernel(sizes, place, mine_free, mine_dep, got_free, got_dep, raised, sea, out):
+def finish_kernel(sizes, place, mine_free, mine_dep, got_free, got_dep, raised, sea_mask, out):
     bins_local, half_bins = sizes
     sub, parity = place[1], place[2]
+    tiles = out.shape[1] // LANES
+    sea = [
+        jnp.broadcast_to(sea_mask[0:1, j * LANES : (j + 1) * LANES].astype(jnp.float32), (SECTOR, LANES))
+        for j in range(tiles)
+    ]
     for other, pair in enumerate(((mine_free, mine_dep), (got_free, got_dep))):
         for k in range(half_bins // (2 * SECTOR)):
             for dep, source in enumerate(pair):
@@ -380,16 +486,19 @@
                 @pl.when(row < bins_local)
                 def _():
                     rows = pl.ds(pl.multiple_of(row, SECTOR), SECTOR)
-                    for j in range(out.shape[1] // LANES):
-                        at = slice(j * LANES, (j + 1) * LANES)
-                        value = source[0, k * SECTOR : (k + 1) * SECTOR, at]
-                        value = value + raised[j, rows, :].astype(jnp.float32)
-                        out[rows, at] = sea[0:1, at] * value
-
-
-def finish(sizes, place, mine_free, mine_dep, got_free, got_dep, raised, sea):
+                    for j in range(0, tiles, 2):
+                        halves = [
+                            source[0, k * SECTOR : (k + 1) * SECTOR, i * LANES : (i + 1) * LANES]
+                            + raised[i, rows, :].astype(jnp.float32)
+                            for i in (j, j + 1)
+                        ]
+                        for i, value in enumerate(join_columns(*halves)):
+                            out[rows, (j + i) * LANES : (j + i + 1) * LANES] = sea[j + i] * value
+
+
+def finish(sizes, place, mine_free, mine_dep, got_free, got_dep, raised, sea_mask):
     bins_local, half_bins = sizes
-    points = sea.shape[1]
+    points = sea_mask.shape[1]
     smem = pl.BlockSpec(memory_space=pltpu.SMEM)
     vmem = pl.BlockSpec(memory_space=pltpu.VMEM)
     first = pl.BlockSpec((1, half_bins // 2, points), lambda i: (0, 0, 0))
@@ -400,7 +509,7 @@
         in_specs=[smem, first, first, first, first, vmem, vmem],
         out_specs=vmem,
         out_shape=jax.ShapeDtypeStruct((bins_local, points), jnp.float32),
-    )(place, mine_free, mine_dep, got_free, got_dep, raised, sea)
+    )(place, mine_free, mine_dep, got_free, got_dep, raised, sea_mask)
 
 
 def swap(values, bits):
@@ -415,50 +524,37 @@
     rows_local = points_local // NLON
     groups = bins_local // SECTOR
     half_bins = (groups + 3) // 4 * 2 * SECTOR
-    sea = sea_mask.astype(jnp.float32)
-    codes = offset_codes(neighbours, sea, points_local).reshape(5, points_local)
-    codes = codes.at[2:4].set(jnp.where(codes[2:4] == 2.0, 0.0, codes[2:4]))
-    codes = jnp.pad(codes, ((0, 3), (0, 0)))
+    sea_mask = sea_mask[None, :]
     first_group = comp * groups
     parity = (first_group + lat) % 2
-    place_free = jnp.stack([lat, sub, parity, first_group + sub * (half_bins // SECTOR)])
-    place_dep = jnp.stack([lat, sub, 1 - parity, first_group + sub * (half_bins // SECTOR)])
+    half_first = first_group + sub * (half_bins // SECTOR)
+    place = jnp.stack([lat, sub, parity, half_first])
+    place_dep = jnp.stack([lat, sub, 1 - parity, half_first])
     angles = (jnp.arange(ND, dtype=jnp.float32) + 0.5) * (2.0 * math.pi / ND)
     trig = jnp.abs(jnp.stack([jnp.cos(angles), jnp.sin(angles)]))
     trig = jnp.broadcast_to(trig[:, :, None], (2, ND, LANES))
 
-    padded = jnp.pad(spectrum, ((0, 2 * half_bins - bins_local), (0, 0)))
-    to_pair = lax.dynamic_slice_in_dim(padded, (1 - sub) * half_bins, half_bins, 0) * sea[None, :]
-    to_pair = jnp.concatenate([to_pair, codes], axis=0)
-    sectors = padded.reshape(2, half_bins // (2 * SECTOR), 2, SECTOR, points_local)
-
-    def to_chip(core):
-        part = lax.dynamic_slice(
-            sectors,
-            (core, 0, parity, 0, 0),
-            (1, half_bins // (2 * SECTOR), 1, SECTOR, points_local),
-        ).reshape(half_bins // 2, points_local)
-        part = part * sea[None, :]
-        return jnp.concatenate([part, codes, codes], axis=0).astype(HALO_TYPE)
-
+    mine, to_pair, to_near, to_far = pack((bins_local, half_bins, rows_local), place, spectrum, neighbours, sea_mask)
     pair = swap(to_pair, 1)
-    near = swap(to_chip(sub), 2).astype(jnp.float32)
-    far = swap(to_chip(1 - sub), 3).astype(jnp.float32)
+    near = swap(to_near, 2)
+    far = swap(to_far, 3)
     other_w = swap(source_operator, 1)
 
-    sizes = (bins_local, half_bins, rows_local)
-    free_start, free_field = stencil(sizes + (False,), place_free, substeps, courant, trig, spectrum, codes, pair)
+    free_start, free_field = stencil(
+        (half_bins, rows_local, False), place, substeps, courant, trig, mine, pair
+    )
     free_state = lax.all_to_all(free_start, ("comp", "sub"), split_axis=0, concat_axis=0, tiled=True)
+    near, far, _ = lax.optimization_barrier((near, far, free_start))
     dep_start, dep_field = stencil(
-        sizes + (True,), place_dep, substeps, courant, trig, spectrum, codes, pair, (near, far)
+        (half_bins, rows_local, True), place_dep, substeps, courant, trig, mine, pair, near, far
     )
     dep_state = lax.all_to_all(dep_start, ("comp", "sub"), split_axis=0, concat_axis=0, tiled=True)
     got_free = swap(free_field[1:], 1)
     got_dep = swap(dep_field[1:], 1)
-    raised = integrate((bins_local, half_bins, comps), place_free, free_state, dep_state, source_operator, other_w)
+    raised = integrate((bins_local, half_bins, comps), place, free_state, dep_state, source_operator, other_w)
     raised = raised.reshape(comps, bins_local, LANES)
     home = lax.all_to_all(raised, "comp", split_axis=0, concat_axis=0, tiled=True)
-    return finish((bins_local, half_bins), place_free, free_field, dep_field, got_free, got_dep, home, sea[None, :])
+    return finish((bins_local, half_bins), place, free_field, dep_field, got_free, got_dep, home, sea_mask)
 
 
 def device_step(*arrays):

time: 102 us -> 88.4 us (0.87)
  blocking collectives: 14.8 us -> 28.7 us
  Pallas kernels: 43.7 us -> 34.3 us
  starting transfers between devices: 12.9 us -> 7.58 us
  waiting for transfers between devices: 18.2 us -> 13.6 us
  other arithmetic: 5.62 us -> 1.37 us
  local copies, waits for them, and re-layouts: 5.66 us -> 2.29 us
    pallas_call x2, Pallas kernels: 26.4 us -> 9.98 us  [stencil(): pl.pallas_call(functools.partial(stencil_kernel, sizes), name='stencil_de...]
    all_to_all x0 -> x1, blocking collectives: none -> 15 us  [two_chip_device(): lax.all_to_all(dep_start, ('comp', 'sub'), split_axis=0, concat_axis=0, t...]
    all_to_all x1 -> x0, starting transfers between devices: 5.21 us -> none  [two_chip_device(): lax.all_to_all(dep_start, ('comp', 'sub'), split_axis=0, concat_axis=0, t...]
    ppermute x6, waiting for transfers between devices: 6.47 us -> 1.84 us  [swap(): lax.ppermute(values, ('lat', 'sub'), [(i, i ^ bits) for i in range(count)])]
    pallas_call x0 -> x1, Pallas kernels: none -> 4.62 us  [pack(): pl.pallas_call(functools.partial(pack_kernel, sizes), name='pack', in_spe...]
    convert_element_type x4 -> x0, other arithmetic: 2.19 us -> none  [the longest x1 0.75 us: two_chip_device(): far = swap(to_chip(1 - sub), 3).astype(jnp.float32)]
    unnamed x20 -> x16, local copies, waits for them, and re-layouts: 3.46 us -> 1.45 us
    pallas_call x1, Pallas kernels: 2.51 us -> 4.1 us  [finish(): pl.pallas_call(functools.partial(finish_kernel, sizes), name='finish', gr...]
  transfers between devices with their start and end apart: 8 -> 7, of which waited for: 5 -> 4; matrix products, arithmetic and copies ran while one was open for 8% -> 3% of each run, Pallas kernels for 26% -> 17%
where the time goes in v2:
time: 88.4 us; the launch traced here: 87.9 us
  Pallas kernels  34.3 us (39%)
  blocking collectives  28.7 us (32%)
  waiting for transfers between devices  13.6 us (15%)
  starting transfers between devices  7.58 us (9%)
  local copies, waits for them, and re-layouts  2.29 us (3%)
  other arithmetic  1.37 us (2%)
    pallas_call x1, Pallas kernels, integrate(): pl.pallas_call(functools.partial(integrate_kernel, sizes), name='integrat...  15.6 us
    all_to_all x1, blocking collectives, two_chip_device(): lax.all_to_all(dep_start, ('comp', 'sub'), split_axis=0, concat_axis=0, t...  15 us
    all_to_all x1, blocking collectives, two_chip_device(): lax.all_to_all(free_start, ('comp', 'sub'), split_axis=0, concat_axis=0,...  13.7 us
    all_to_all x1, waiting for transfers between devices, two_chip_device(): lax.all_to_all(raised, 'comp', split_axis=0, concat_axis=0, tiled=True)  11.7 us
    pallas_call x2, Pallas kernels, stencil(): pl.pallas_call(functools.partial(stencil_kernel, sizes), name='stencil_de...  9.98 us
    pallas_call x1, Pallas kernels, pack(): pl.pallas_call(functools.partial(pack_kernel, sizes), name='pack', in_spe...  4.62 us
    ppermute x6, starting transfers between devices, swap(): lax.ppermute(values, ('lat', 'sub'), [(i, i ^ bits) for i in range(count)])  4.1 us
    pallas_call x1, Pallas kernels, finish(): pl.pallas_call(functools.partial(finish_kernel, sizes), name='finish', gr...  4.1 us
  transfers between devices with their start and end apart: 7, of which 4 were waited for; matrix products, arithmetic and copies ran while one was open for 3% of the time, Pallas kernels for 17%

profile of v2, /device:TPU:0, one launch (start us, length us, event | category | flops | bytes accessed | tf_op | source)
XLA Modules:
  0.0 87.9 jit_solution(18258947742830376585)
XLA Ops:
  0.0 0.5 collective-permute-start.5
  0.5 0.7 add_add_fusion.place.refs_0_
  1.1 4.6 %pack.1 = (f32[264,512]{1,0:T(8,128)}, f32[264,512]{1,0:T(8,128)}, s16[136,512]{1,0:T(8,128)(2,1)}, s16[136,512]{1,0:T(8,128)(2,1)}) custom-call(s32[4]{0:T(128)} %add_add_fusion.place.refs_0_, f32[480,512]{1,0:T(8,128)} %spectrum.1, s32[4,512]{1,0:T(4,128)} %neighbours.1, s32[1,512]{1,0:T(1,128)} %bitcast.8), custom_call_target="tpu_custom_call" | custom-call | tf_op jit(solution)/shard_map/pack/pallas_call | solution.py:256
  5.8 0.0 collective-permute-start
  5.8 3.0 %collective-permute-start.1 = (s16[136,512]{1,0:T(8,128)(2,1)}, s16[136,512]{1,0:T(8,128)(2,1)S(1)}, u32[]{:S(2)}, u32[]{:S(2)}) collective-permute-start(s16[136,512]{1,0:T(8,128)(2,1)} %get-tuple-element.18), channel_id=1, source_target_pairs={{0,2},{1,3},{2,0},{3,1},{4,6},{5,7},{6,4},{7,5},{8,10},{9,11},{10,... | collective-permute-start | bytes 417800 | tf_op jit(solution)/shard_map/ppermute | solution.py:517
  8.8 0.0 collective-permute-start.2
  8.8 0.7 add_add_fusion.1.refs_0_
  9.5 0.0 collective-permute-done.refs_5_
  9.5 0.0 copy-start
  9.5 0.8 broadcast_in_dim.4.refs_3_
  10.3 0.0 copy-done
  10.3 4.3 %stencil_free.1 = (bf16[8,128,128]{2,1,0:T(8,128)(2,1)}, f32[2,128,512]{2,1,0:T(8,128)}) custom-call(s32[4]{0:T(128)} %add_add_fusion.place.refs_0_, s32[30]{0:T(128)} %refs_1_.3, f32[30]{0:T(128)} %refs_2_.3, f32[2,64,128]{2,1,0:T(8,128)} %broadcast_in_dim.4.refs_3_, f32[264,512]{1,0:T(8,128)} %get-tuple-element.15.refs_4_, f32[264,512]{1,0:T(8,128)} %copy-done), custom_call_target="tpu_custom_call" | custom-call | flops 78643200 | bytes 2097152 | tf_op jit(solution)/shard_map/stencil_free/pallas_call | solution.py:383
  14.6 0.0 collective-permute-done.1.refs_6_
  14.6 0.0 copy-start.6
  14.6 0.5 collective-permute-done.2.refs_7_
  15.2 0.0 copy-start.7
  15.2 0.1 copy-done.6
  15.3 0.5 copy-done.7
  15.8 5.7 %stencil_dependent.1 = (bf16[8,128,128]{2,1,0:T(8,128)(2,1)}, f32[2,128,512]{2,1,0:T(8,128)}) custom-call(s32[4]{0:T(128)} %add_add_fusion.1.refs_0_, s32[30]{0:T(128)} %refs_1_.3, f32[30]{0:T(128)} %refs_2_.3, f32[2,64,128]{2,1,0:T(8,128)} %broadcast_in_dim.4.refs_3_, f32[264,512]{1,0:T(8,128)} %get-tuple-element.15.refs_4_, f32[264,512]{1,0:T(8,128)} %copy-done, ...), custom_call_target="tpu_custom_call" | custom-call | flops 78643200 | bytes 2097152 | tf_op jit(solution)/shard_map/stencil_dependent/pallas_call | solution.py:383
  21.5 15.0 %all_to_all.15.dependent = bf16[8,128,128]{2,1,0:T(8,128)(2,1)} all-to-all(bf16[8,128,128]{2,1,0:T(8,128)(2,1)} %get-tuple-element.24), channel_id=1, replica_groups=mesh['members'=2,'comp'=4,'lat'=2,'sub'=2] {'comp','sub'}, dimensions={0} | all-to-all | bytes 524288 | tf_op jit(solution)/shard_map/all_to_all | solution.py:551
  36.5 13.7 %all_to_all.16.free = bf16[8,128,128]{2,1,0:T(8,128)(2,1)} all-to-all(bf16[8,128,128]{2,1,0:T(8,128)(2,1)} %get-tuple-element.20), channel_id=1, replica_groups=mesh['members'=2,'comp'=4,'lat'=2,'sub'=2] {'comp','sub'}, dimensions={0} | all-to-all | bytes 524288 | tf_op jit(solution)/shard_map/all_to_all | solution.py:546
  50.2 0.0 copy-start.3
  50.2 0.0 copy-start.2
  50.2 0.0 collective-permute-done.5.other_w
  50.2 15.6 %integrate.1 = bf16[1920,128]{1,0:T(8,128)(2,1)} custom-call(s32[4]{0:T(128)} %add_add_fusion.place.refs_0_, bf16[8,128,128]{2,1,0:T(8,128)(2,1)} %all_to_all.16.free, bf16[8,128,128]{2,1,0:T(8,128)(2,1)} %all_to_all.15.dependent, bf16[960,1920]{1,0:T(8,128)(2,1)} %own_w.1, bf16[960,1920]{1,0:T(8,128)(2,1)} %collective-permute-done.5.other_w), custom_call_target="tpu_custom_call" | custom-call | flops 3774873600 | bytes 7372800 | tf_op jit(solution)/shard_map/integrate/pallas_call | solution.py:454
  65.8 3.5 %all-to-all-start.2 = ((bf16[4,480,128]{2,1,0:T(8,128)(2,1)}), bf16[4,480,128]{2,1,0:T(8,128)(2,1)S(1)}, u32[]{:S(2)}, u32[]{:S(2)}) async-start(bf16[4,480,128]{2,1,0:T(8,128)(2,1)} %bitcast.7), calls=%async_computation.2 | async-start | bytes 983040 | tf_op jit(solution)/shard_map/all_to_all | solution.py:556
  69.3 0.0 copy-done.3
  69.3 0.1 collective-permute-start.4
  69.4 0.0 copy-done.2
  69.5 0.5 collective-permute-start.3
  70.0 0.9 %collective-permute-done.4.got_dep = f32[1,128,512]{2,1,0:T(8,128)S(1)} collective-permute-done((f32[1,128,512]{2,1,0:T(8,128)S(1)}, f32[1,128,512]{2,1,0:T(8,128)S(1)}, u32[]{:S(2)}, u32[]{:S(2)}) %collective-permute-start.4) | collective-permute-done | bytes 262176 | tf_op jit(solution)/shard_map/ppermute | solution.py:517
  71.0 0.0 copy-start.4
  71.0 0.4 collective-permute-done.3.got_free
  71.3 0.0 copy-start.5
  71.3 11.7 %all-to-all-done.2.raised = bf16[4,480,128]{2,1,0:T(8,128)(2,1)S(1)} async-done(((bf16[4,480,128]{2,1,0:T(8,128)(2,1)}), bf16[4,480,128]{2,1,0:T(8,128)(2,1)S(1)}, u32[]{:S(2)}, u32[]{:S(2)}) %all-to-all-start.2) | async-done | bytes 491552 | tf_op jit(solution)/shard_map/all_to_all | solution.py:556
  83.1 0.0 copy-done.4
  83.1 0.0 copy-done.5
  83.1 0.0 copy-start.1
  83.1 0.8 copy-done.1
  83.9 4.1 %finish.1 = f32[480,512]{1,0:T(8,128)} custom-call(s32[4]{0:T(128)} %add_add_fusion.place.refs_0_, f32[2,128,512]{2,1,0:T(8,128)} %get-tuple-element.17.mine_free, f32[2,128,512]{2,1,0:T(8,128)} %get-tuple-element.23.mine_dep, f32[1,128,512]{2,1,0:T(8,128)} %copy-done.5, f32[1,128,512]{2,1,0:T(8,128)} %copy-done.4, bf16[4,480,128]{2,1,0:T(8,128)(2,1)} %copy-done.1, ...), custom_call_target="tpu_custom_call" | custom-call | tf_op jit(solution)/shard_map/finish/pallas_call | solution.py:505
  (4 shorter events, 0.1 us)
Async XLA Ops:
  0.0 50.2 %collective-permute-start.5 = (bf16[960,1920]{1,0:T(8,128)(2,1)}, bf16[960,1920]{1,0:T(8,128)(2,1)}, u32[]{:S(2)}, u32[]{:S(2)}) collective-permute-start(bf16[960,1920]{1,0:T(8,128)(2,1)} %own_w.1), channel_id=1, source_target_pairs={{0,1},{1,0},{2,3},{3,2},{4,5},{5,4},{6,7},{7,6},{8,9},{9,8},{10,11... | collective-permute-start | bytes 11059208 | tf_op jit(solution)/shard_map/ppermute | solution.py:517
  5.8 3.7 %collective-permute-start = (f32[264,512]{1,0:T(8,128)}, f32[264,512]{1,0:T(8,128)S(1)}, u32[]{:S(2)}, u32[]{:S(2)}) collective-permute-start(f32[264,512]{1,0:T(8,128)} %get-tuple-element.16), channel_id=1, source_target_pairs={{0,1},{1,0},{2,3},{3,2},{4,5},{5,4},{6,7},{7,6},{8,9},{9,8},{10,11... | collective-permute-start | bytes 1622024 | tf_op jit(solution)/shard_map/ppermute | solution.py:517
  5.8 8.8 %collective-permute-start.1 = (s16[136,512]{1,0:T(8,128)(2,1)}, s16[136,512]{1,0:T(8,128)(2,1)S(1)}, u32[]{:S(2)}, u32[]{:S(2)}) collective-permute-start(s16[136,512]{1,0:T(8,128)(2,1)} %get-tuple-element.18), channel_id=1, source_target_pairs={{0,2},{1,3},{2,0},{3,1},{4,6},{5,7},{6,4},{7,5},{8,10},{9,11},{10,... | collective-permute-start | bytes 417800 | tf_op jit(solution)/shard_map/ppermute | solution.py:517
  8.8 6.4 %collective-permute-start.2 = (s16[136,512]{1,0:T(8,128)(2,1)}, s16[136,512]{1,0:T(8,128)(2,1)S(1)}, u32[]{:S(2)}, u32[]{:S(2)}) collective-permute-start(s16[136,512]{1,0:T(8,128)(2,1)} %get-tuple-element.19), channel_id=1, source_target_pairs={{0,3},{1,2},{2,1},{3,0},{4,7},{5,6},{6,5},{7,4},{8,11},{9,10},{10,... | collective-permute-start | bytes 417800 | tf_op jit(solution)/shard_map/ppermute | solution.py:517
  9.5 0.8 copy-start
  14.6 0.7 copy-start.6
  15.2 0.6 copy-start.7
  50.2 19.1 %copy-start.3 = (f32[2,128,512]{2,1,0:T(8,128)S(1)}, f32[2,128,512]{2,1,0:T(8,128)}, u32[]{:S(2)}) copy-start(f32[2,128,512]{2,1,0:T(8,128)} %get-tuple-element.23.mine_dep) | copy-start | bytes 1572868
  50.2 19.2 %copy-start.2 = (f32[2,128,512]{2,1,0:T(8,128)S(1)}, f32[2,128,512]{2,1,0:T(8,128)}, u32[]{:S(2)}) copy-start(f32[2,128,512]{2,1,0:T(8,128)} %get-tuple-element.17.mine_free) | copy-start | bytes 1572868
  65.8 17.2 %all-to-all-start.2 = ((bf16[4,480,128]{2,1,0:T(8,128)(2,1)}), bf16[4,480,128]{2,1,0:T(8,128)(2,1)S(1)}, u32[]{:S(2)}, u32[]{:S(2)}) async-start(bf16[4,480,128]{2,1,0:T(8,128)(2,1)} %bitcast.7), calls=%async_computation.2 | async-start | bytes 983040 | tf_op jit(solution)/shard_map/all_to_all | solution.py:556
  69.3 1.6 %collective-permute-start.4 = (f32[1,128,512]{2,1,0:T(8,128)S(1)}, f32[1,128,512]{2,1,0:T(8,128)S(1)}, u32[]{:S(2)}, u32[]{:S(2)}) collective-permute-start(f32[1,128,512]{2,1,0:T(8,128)S(1)} %slice.7), channel_id=1, source_target_pairs={{0,1},{1,0},{2,3},{3,2},{4,5},{5,4},{6,7},{7,6},{8,9},{9,8},{10,11... | collective-permute-start | bytes 786440 | tf_op jit(solution)/shard_map/ppermute | solution.py:517
  69.5 1.9 %collective-permute-start.3 = (f32[1,128,512]{2,1,0:T(8,128)S(1)}, f32[1,128,512]{2,1,0:T(8,128)S(1)}, u32[]{:S(2)}, u32[]{:S(2)}) collective-permute-start(f32[1,128,512]{2,1,0:T(8,128)S(1)} %slice.6), channel_id=1, source_target_pairs={{0,1},{1,0},{2,3},{3,2},{4,5},{5,4},{6,7},{7,6},{8,9},{9,8},{10,11... | collective-permute-start | bytes 786440 | tf_op jit(solution)/shard_map/ppermute | solution.py:517
  71.0 12.1 %copy-start.4 = (f32[1,128,512]{2,1,0:T(8,128)}, f32[1,128,512]{2,1,0:T(8,128)S(1)}, u32[]{:S(2)}) copy-start(f32[1,128,512]{2,1,0:T(8,128)S(1)} %collective-permute-done.4.got_dep) | copy-start | bytes 786436
  71.3 11.7 %copy-start.5 = (f32[1,128,512]{2,1,0:T(8,128)}, f32[1,128,512]{2,1,0:T(8,128)S(1)}, u32[]{:S(2)}) copy-start(f32[1,128,512]{2,1,0:T(8,128)S(1)} %collective-permute-done.3.got_free) | copy-start | bytes 786436
  83.1 0.8 copy-start.1

commit v3 on v2

--- a/solution.py
+++ b/solution.py
@@ -3,6 +3,7 @@
 
 import jax
 import jax.numpy as jnp
+import numpy as np
 from jax import lax
 from jax.experimental import pallas as pl
 from jax.experimental.pallas import tpu as pltpu
@@ -185,9 +186,15 @@
     return (values.astype(jnp.int32) + 32768).astype(jnp.float32) * (1.0 / CODE_SCALE)
 
 
-def pack_kernel(sizes, place, spectrum, neighbours, sea_mask, mine, to_pair, to_near, to_far):
+def device_place(bins_local):
+    lat, sub = lax.axis_index("lat"), lax.axis_index("sub")
+    first_group = lax.axis_index("comp") * (bins_local // SECTOR)
+    return lat, sub, (first_group + lat) % 2, first_group
+
+
+def pack_kernel(sizes, spectrum, neighbours, sea_mask, mine, to_pair, to_near, to_far):
     bins_local, half_bins, rows_local = sizes
-    sub, parity = place[1], place[2]
+    _, sub, parity, _ = device_place(bins_local)
     sectors = half_bins // (2 * SECTOR)
     for row in range(rows_local):
         halves = [slice(row * NLON + h * LANES, row * NLON + (h + 1) * LANES) for h in range(2)]
@@ -209,67 +216,49 @@
         for j in range(2 * rows_local)
     ]
 
-    def sector_of(index, carry):
-        core, group = index // (2 * sectors), index % (2 * sectors)
-        source = jnp.minimum(core * half_bins + group * SECTOR, bins_local - SECTOR)
-        source = pl.ds(pl.multiple_of(source, SECTOR), SECTOR)
-        target = pl.ds(pl.multiple_of(group * SECTOR, SECTOR), SECTOR)
-        sent = pl.ds(pl.multiple_of(group // 2 * SECTOR, SECTOR), SECTOR)
-        blocks = []
-        for row in range(rows_local):
-            pair = [
-                spectrum[source, (2 * row + h) * LANES : (2 * row + h + 1) * LANES] * sea_rows[2 * row + h]
-                for h in range(2)
-            ]
-            blocks += split_columns(*pair)
-
-        @pl.when(core == sub)
-        def _():
-            for j, block in enumerate(blocks):
-                mine[target, j * LANES : (j + 1) * LANES] = block
-
-        @pl.when(core != sub)
-        def _():
-            for j, block in enumerate(blocks):
-                to_pair[target, j * LANES : (j + 1) * LANES] = block
-
-        @pl.when((group % 2 == parity) & (core == sub))
-        def _():
-            for j, block in enumerate(blocks):
-                to_near[sent, j * LANES : (j + 1) * LANES] = encode(block)
-
-        @pl.when((group % 2 == parity) & (core != sub))
-        def _():
-            for j, block in enumerate(blocks):
-                to_far[sent, j * LANES : (j + 1) * LANES] = encode(block)
-
-        return carry
-
-    lax.fori_loop(0, 4 * sectors, sector_of, 0)
-
-
-def pack(sizes, place, spectrum, neighbours, sea_mask):
+    for other in range(2):
+        base = (sub + other) % 2 * half_bins
+        whole, sent = (to_pair, to_far) if other else (mine, to_near)
+        for k in range(sectors):
+            for rest in range(2):
+                group = (2 * k + (parity + rest) % 2) * SECTOR
+                source = pl.ds(pl.multiple_of(jnp.minimum(base + group, bins_local - SECTOR), SECTOR), SECTOR)
+                target = pl.ds(pl.multiple_of(group, SECTOR), SECTOR)
+                for row in range(rows_local):
+                    pair = [
+                        spectrum[source, (2 * row + h) * LANES : (2 * row + h + 1) * LANES] * sea_rows[2 * row + h]
+                        for h in range(2)
+                    ]
+                    for h, block in enumerate(split_columns(*pair)):
+                        at = slice((2 * row + h) * LANES, (2 * row + h + 1) * LANES)
+                        whole[target, at] = block
+                        if not rest:
+                            sent[k * SECTOR : (k + 1) * SECTOR, at] = encode(block)
+
+
+def pack(sizes, spectrum, neighbours, sea_mask):
     bins_local, half_bins, rows_local = sizes
     points = rows_local * NLON
-    smem = pl.BlockSpec(memory_space=pltpu.SMEM)
     vmem = pl.BlockSpec(memory_space=pltpu.VMEM)
     return pl.pallas_call(
         functools.partial(pack_kernel, sizes),
         name="pack",
-        in_specs=[smem, vmem, vmem, vmem],
+        in_specs=[vmem, vmem, vmem],
         out_specs=[vmem] * 4,
         out_shape=[jax.ShapeDtypeStruct((half_bins + TILE, points), jnp.float32)] * 2
         + [jax.ShapeDtypeStruct((half_bins // 2 + TILE, points), jnp.int16)] * 2,
-    )(place, spectrum, neighbours, sea_mask)
+    )(spectrum, neighbours, sea_mask)
 
 
 def stencil_kernel(sizes, *refs):
-    half_bins, rows_local, dependent = sizes
+    bins_local, half_bins, rows_local, dependent = sizes
     if dependent:
-        place, steps_ref, courant_ref, trig, mine, pair, near, far, start_out, field_out, tab = refs
+        steps_ref, courant_ref, trig, mine, pair, near, far, start_out, field_out, tab = refs
     else:
-        place, steps_ref, courant_ref, trig, mine, pair, start_out, field_out, tab = refs
-    lat, sub, parity, first_group = place[0], place[1], place[2], place[3]
+        steps_ref, courant_ref, trig, mine, pair, start_out, field_out, tab = refs
+    lat, sub, parity, first_group = device_place(bins_local)
+    parity = (parity + int(dependent)) % 2
+    first_group = first_group + sub * (half_bins // SECTOR)
     chip_rows = 2 * rows_local
     halo = chip_rows if dependent else 0
     north = lat == (0 if dependent else 1)
@@ -373,8 +362,8 @@
     lax.fori_loop(0, half_bins // (2 * SECTOR), both_sides, 0)
 
 
-def stencil(sizes, place, substeps, courant, trig, *fields):
-    half_bins, rows_local, dependent = sizes
+def stencil(sizes, substeps, courant, trig, *fields):
+    bins_local, half_bins, rows_local, dependent = sizes
     blocks = 4 * rows_local
     rows = (4 if dependent else 2) * rows_local
     smem = pl.BlockSpec(memory_space=pltpu.SMEM)
@@ -383,7 +372,7 @@
     return pl.pallas_call(
         functools.partial(stencil_kernel, sizes),
         name="stencil_dependent" if dependent else "stencil_free",
-        in_specs=[smem] * 3 + [vmem] * (1 + len(fields)),
+        in_specs=[smem] * 2 + [vmem] * (1 + len(fields)),
         out_specs=[vmem, vmem],
         out_shape=[
             jax.ShapeDtypeStruct((blocks, half_bins // 2, LANES), jnp.bfloat16),
@@ -391,89 +380,85 @@
         ],
         scratch_shapes=[pltpu.VMEM((rows, 2, 4, TILE, LANES), jnp.float32)],
         cost_estimate=pl.CostEstimate(flops=cells * MAXSTEPS * 100, bytes_accessed=cells * 16, transcendentals=0),
-    )(place, substeps, courant, trig, *fields)
-
-
-def integrate_kernel(sizes, place, free, dependent, own_w, other_w, out, w_ref, state, driver, sem):
+    )(substeps, courant, trig, *fields)
+
+
+def integrate_kernel(sizes, arrived, own_w, other_w, out, w_ref, joined, state, driver, sem):
     bins_local, half_bins, comps = sizes
-    lat, sub = place[0], place[1]
+    lat, sub, _, _ = device_place(bins_local)
     w_rows = own_w.shape[0]
-    pieces = 3
-    piece = w_rows // pieces
+    total = comps * bins_local
     copies = []
-    for which, source in enumerate((own_w, other_w)):
-        for p in range(pieces):
-            at = pl.ds(p * piece, piece)
-            copy = pltpu.make_async_copy(source.at[at], w_ref.at[which, at], sem.at[which, p])
-            copy.start()
-            copies.append(copy)
+    for other, source in enumerate((own_w, other_w)):
+        at = pl.ds(pl.multiple_of((sub + other) % 2 * w_rows, 64), w_rows)
+        copy = pltpu.make_async_copy(source, w_ref.at[at], sem.at[other])
+        copy.start()
+        copies.append(copy)
     sectors = half_bins // (2 * SECTOR)
     groups = bins_local // SECTOR
     for c in range(comps):
         first = (c * groups) % 2
         for s in range(2):
             for k in range(sectors):
-                for dep, source in enumerate((free, dependent)):
+                for dep in range(2):
                     parity = (first + lat + dep) % 2
                     row = c * bins_local + s * half_bins + (2 * k + parity) * SECTOR
                     row = pl.ds(pl.multiple_of(row, SECTOR), SECTOR)
-                    block = source[2 * c + s, k * SECTOR : (k + 1) * SECTOR, :]
-                    driver[0, row, :] = block
-                    state[row, :] = block.astype(jnp.float32)
-    total = comps * bins_local
+                    joined[row, :] = arrived[2 * c + s, (sectors * dep + k) * SECTOR : (sectors * dep + k + 1) * SECTOR, :]
+    for b in range(total // LANES):
+        at = slice(b * LANES, (b + 1) * LANES)
+        block = joined[at, :].astype(jnp.float32).T
+        state[:, at] = block
+        driver[0, :, at] = block.astype(jnp.bfloat16)
+    for copy in copies:
+        copy.wait()
+    width = 2 * LANES
     for step in range(SRC_STEPS):
-        for which in range(2):
-            half_at = (sub + which) % 2 * w_rows
-            stretch = piece if step == 0 else w_rows
-            for p in range(w_rows // stretch):
-                if step == 0:
-                    copies[which * pieces + p].wait()
-                drive = jnp.dot(
-                    w_ref[which, p * stretch : (p + 1) * stretch, :],
-                    driver[0 if step == 0 else 1 + step % 2, :total, :],
-                    preferred_element_type=jnp.float32,
-                )
-                row = pl.ds(pl.multiple_of(half_at + p * stretch, 64), stretch)
-                value = state[row, :]
-                value = value + STEP_SIZE * value * drive
-                if step + 1 < SRC_STEPS:
-                    state[row, :] = value
-                    driver[1 + (step + 1) % 2, row, :] = value.astype(jnp.bfloat16)
-                else:
-                    begun = driver[0, row, :].astype(jnp.float32)
-                    out[row, :] = (value - begun).astype(jnp.bfloat16)
-
-
-def integrate(sizes, place, free, dependent, own_w, other_w):
+        read = 0 if step == 0 else 1 + step % 2
+        for first in range(0, total, width):
+            at = slice(first, min(first + width, total))
+            drive = lax.dot_general(
+                driver[read], w_ref[at, :], (((1,), (1,)), ((), ())), preferred_element_type=jnp.float32
+            )
+            value = state[:, at]
+            value = value + STEP_SIZE * value * drive
+            if step + 1 < SRC_STEPS:
+                state[:, at] = value
+                driver[1 + (step + 1) % 2, :, at] = value.astype(jnp.bfloat16)
+            else:
+                raised = value - driver[0, :, at].astype(jnp.float32)
+                out[at, :] = raised.T.astype(jnp.bfloat16)
+
+
+def integrate(sizes, arrived, own_w, other_w):
     bins_local, half_bins, comps = sizes
     total = comps * bins_local
-    spare = total + SECTOR
-    smem = pl.BlockSpec(memory_space=pltpu.SMEM)
     vmem = pl.BlockSpec(memory_space=pltpu.VMEM)
     hbm = pl.BlockSpec(memory_space=pl.ANY)
     return pl.pallas_call(
         functools.partial(integrate_kernel, sizes),
         name="integrate",
-        in_specs=[smem, vmem, vmem, hbm, hbm],
+        in_specs=[vmem, hbm, hbm],
         out_specs=vmem,
         out_shape=jax.ShapeDtypeStruct((total, LANES), jnp.bfloat16),
         scratch_shapes=[
-            pltpu.VMEM((2,) + own_w.shape, jnp.bfloat16),
-            pltpu.VMEM((spare, LANES), jnp.float32),
-            pltpu.VMEM((3, spare, LANES), jnp.bfloat16),
-            pltpu.SemaphoreType.DMA((2, 3)),
+            pltpu.VMEM((total, total), jnp.bfloat16),
+            pltpu.VMEM((total + SECTOR, LANES), jnp.bfloat16),
+            pltpu.VMEM((LANES, total), jnp.float32),
+            pltpu.VMEM((3, LANES, total), jnp.bfloat16),
+            pltpu.SemaphoreType.DMA((2,)),
         ],
         compiler_params=pltpu.CompilerParams(vmem_limit_bytes=60 << 20),
         cost_estimate=pl.CostEstimate(
             flops=2 * SRC_STEPS * total * total * LANES, bytes_accessed=2 * total * total, transcendentals=0
         ),
-    )(place, free, dependent, own_w, other_w)
-
-
-def finish_kernel(sizes, place, mine_free, mine_dep, got_free, got_dep, raised, sea_mask, out):
+    )(arrived, own_w, other_w)
+
+
+def finish_kernel(sizes, mine_free, mine_dep, got_free, got_dep, raised, sea_mask, out, whole, sem):
     bins_local, half_bins = sizes
-    sub, parity = place[1], place[2]
-    tiles = out.shape[1] // LANES
+    _, sub, parity, _ = device_place(bins_local)
+    tiles = whole.shape[1] // LANES
     sea = [
         jnp.broadcast_to(sea_mask[0:1, j * LANES : (j + 1) * LANES].astype(jnp.float32), (SECTOR, LANES))
         for j in range(tiles)
@@ -482,34 +467,35 @@
         for k in range(half_bins // (2 * SECTOR)):
             for dep, source in enumerate(pair):
                 row = (sub + other) % 2 * half_bins + (2 * k + (parity + dep) % 2) * SECTOR
-
-                @pl.when(row < bins_local)
-                def _():
-                    rows = pl.ds(pl.multiple_of(row, SECTOR), SECTOR)
-                    for j in range(0, tiles, 2):
-                        halves = [
-                            source[0, k * SECTOR : (k + 1) * SECTOR, i * LANES : (i + 1) * LANES]
-                            + raised[i, rows, :].astype(jnp.float32)
-                            for i in (j, j + 1)
-                        ]
-                        for i, value in enumerate(join_columns(*halves)):
-                            out[rows, (j + i) * LANES : (j + i + 1) * LANES] = sea[j + i] * value
-
-
-def finish(sizes, place, mine_free, mine_dep, got_free, got_dep, raised, sea_mask):
+                rows = pl.ds(pl.multiple_of(row, SECTOR), SECTOR)
+                added = pl.ds(pl.multiple_of(jnp.minimum(row, bins_local - SECTOR), SECTOR), SECTOR)
+                for j in range(0, tiles, 2):
+                    halves = [
+                        source[0, k * SECTOR : (k + 1) * SECTOR, i * LANES : (i + 1) * LANES]
+                        + raised[i, added, :].astype(jnp.float32)
+                        for i in (j, j + 1)
+                    ]
+                    for i, value in enumerate(join_columns(*halves)):
+                        whole[rows, (j + i) * LANES : (j + i + 1) * LANES] = sea[j + i] * value
+    copy = pltpu.make_async_copy(whole.at[pl.ds(0, bins_local)], out, sem)
+    copy.start()
+    copy.wait()
+
+
+def finish(sizes, mine_free, mine_dep, got_free, got_dep, raised, sea_mask):
     bins_local, half_bins = sizes
     points = sea_mask.shape[1]
-    smem = pl.BlockSpec(memory_space=pltpu.SMEM)
     vmem = pl.BlockSpec(memory_space=pltpu.VMEM)
     first = pl.BlockSpec((1, half_bins // 2, points), lambda i: (0, 0, 0))
     return pl.pallas_call(
         functools.partial(finish_kernel, sizes),
         name="finish",
         grid=(1,),
-        in_specs=[smem, first, first, first, first, vmem, vmem],
-        out_specs=vmem,
+        in_specs=[first, first, first, first, vmem, vmem],
+        out_specs=pl.BlockSpec(memory_space=pl.ANY),
         out_shape=jax.ShapeDtypeStruct((bins_local, points), jnp.float32),
-    )(place, mine_free, mine_dep, got_free, got_dep, raised, sea_mask)
+        scratch_shapes=[pltpu.VMEM((2 * half_bins, points), jnp.float32), pltpu.SemaphoreType.DMA],
+    )(mine_free, mine_dep, got_free, got_dep, raised, sea_mask)
 
 
 def swap(values, bits):
@@ -518,43 +504,34 @@
 
 
 def two_chip_device(spectrum, sea_mask, neighbours, substeps, courant, source_operator):
-    comp, lat, sub = (lax.axis_index(name) for name in ("comp", "lat", "sub"))
     comps = lax.axis_size("comp")
     bins_local, points_local = spectrum.shape
     rows_local = points_local // NLON
-    groups = bins_local // SECTOR
-    half_bins = (groups + 3) // 4 * 2 * SECTOR
+    half_bins = (bins_local // SECTOR + 3) // 4 * 2 * SECTOR
     sea_mask = sea_mask[None, :]
-    first_group = comp * groups
-    parity = (first_group + lat) % 2
-    half_first = first_group + sub * (half_bins // SECTOR)
-    place = jnp.stack([lat, sub, parity, half_first])
-    place_dep = jnp.stack([lat, sub, 1 - parity, half_first])
-    angles = (jnp.arange(ND, dtype=jnp.float32) + 0.5) * (2.0 * math.pi / ND)
-    trig = jnp.abs(jnp.stack([jnp.cos(angles), jnp.sin(angles)]))
-    trig = jnp.broadcast_to(trig[:, :, None], (2, ND, LANES))
-
-    mine, to_pair, to_near, to_far = pack((bins_local, half_bins, rows_local), place, spectrum, neighbours, sea_mask)
+    angles = (np.arange(ND, dtype=np.float32) + np.float32(0.5)) * np.float32(2.0 * math.pi / ND)
+    trig = np.abs(np.stack([np.cos(angles), np.sin(angles)])).astype(np.float32)
+    trig = jnp.asarray(np.repeat(trig[:, :, None], LANES, axis=2))
+
+    mine, to_pair, to_near, to_far = pack((bins_local, half_bins, rows_local), spectrum, neighbours, sea_mask)
     pair = swap(to_pair, 1)
     near = swap(to_near, 2)
     far = swap(to_far, 3)
     other_w = swap(source_operator, 1)
 
-    free_start, free_field = stencil(
-        (half_bins, rows_local, False), place, substeps, courant, trig, mine, pair
-    )
-    free_state = lax.all_to_all(free_start, ("comp", "sub"), split_axis=0, concat_axis=0, tiled=True)
+    free_start, free_field = stencil((bins_local, half_bins, rows_local, False), substeps, courant, trig, mine, pair)
     near, far, _ = lax.optimization_barrier((near, far, free_start))
     dep_start, dep_field = stencil(
-        (half_bins, rows_local, True), place_dep, substeps, courant, trig, mine, pair, near, far
-    )
-    dep_state = lax.all_to_all(dep_start, ("comp", "sub"), split_axis=0, concat_axis=0, tiled=True)
+        (bins_local, half_bins, rows_local, True), substeps, courant, trig, mine, pair, near, far
+    )
+    start = jnp.concatenate([free_start, dep_start], axis=1)
+    arrived = lax.all_to_all(start, ("comp", "sub"), split_axis=0, concat_axis=0, tiled=True)
     got_free = swap(free_field[1:], 1)
     got_dep = swap(dep_field[1:], 1)
-    raised = integrate((bins_local, half_bins, comps), place, free_state, dep_state, source_operator, other_w)
+    raised = integrate((bins_local, half_bins, comps), arrived, source_operator, other_w)
     raised = raised.reshape(comps, bins_local, LANES)
     home = lax.all_to_all(raised, "comp", split_axis=0, concat_axis=0, tiled=True)
-    return finish((bins_local, half_bins), place, free_field, dep_field, got_free, got_dep, home, sea_mask)
+    return finish((bins_local, half_bins), free_field, dep_field, got_free, got_dep, home, sea_mask)
 
 
 def device_step(*arrays):
@@ -565,6 +542,7 @@
         and bins_local % SECTOR == 0
         and points_local % NLON == 0
         and points_local == lax.axis_size("comp") * LANES
+        and lax.axis_size("comp") * bins_local % LANES == 0
     )
     return (two_chip_device if two_chips else per_device)(*arrays)
 

time: 88.4 us -> 77.3 us (0.87)
  blocking collectives: 28.7 us -> 21.4 us
  Pallas kernels: 34.3 us -> 30.3 us
    all_to_all x2 -> x1, blocking collectives: 28.7 us -> 21.4 us  [two_chip_device(): lax.all_to_all(start, ('comp', 'sub'), split_axis=0, concat_axis=0, tiled...]
    pallas_call x1, Pallas kernels: 4.62 us -> 2.92 us  [pack(): pl.pallas_call(functools.partial(pack_kernel, sizes), name='pack', in_spe...]
    pallas_call x1, Pallas kernels: 15.6 us -> 14.2 us  [integrate(): pl.pallas_call(functools.partial(integrate_kernel, sizes), name='integrat...]
    another operation x2 -> x0, other arithmetic: 1.32 us -> none  [the longest x1 0.66 us: two_chip_device(): place_dep = jnp.stack([lat, sub, 1 - parity, half_first])]
    concatenate x0 -> x1, other arithmetic: none -> 1.06 us  [two_chip_device(): start = jnp.concatenate([free_start, dep_start], axis=1)]
    pallas_call x1, Pallas kernels: 4.1 us -> 3.12 us  [finish(): pl.pallas_call(functools.partial(finish_kernel, sizes), name='finish', gr...]
  transfers between devices with their start and end apart: 7 -> 7, of which waited for: 4 -> 5; matrix products, arithmetic and copies ran while one was open for 3% -> 1% of each run, Pallas kernels for 17% -> 17%
where the time goes in v3:
time: 77.3 us; the launch traced here: 76.9 us
  Pallas kernels  30.3 us (39%)
  blocking collectives  21.4 us (28%)
  waiting for transfers between devices  14.2 us (18%)
  starting transfers between devices  7.58 us (10%)
  local copies, waits for them, and re-layouts  2.28 us (3%)
  other arithmetic  1.06 us (1%)
    all_to_all x1, blocking collectives, two_chip_device(): lax.all_to_all(start, ('comp', 'sub'), split_axis=0, concat_axis=0, tiled...  21.4 us
    pallas_call x1, Pallas kernels, integrate(): pl.pallas_call(functools.partial(integrate_kernel, sizes), name='integrat...  14.2 us
    all_to_all x1, waiting for transfers between devices, two_chip_device(): lax.all_to_all(raised, 'comp', split_axis=0, concat_axis=0, tiled=True)  11.7 us
    pallas_call x2, Pallas kernels, stencil(): pl.pallas_call(functools.partial(stencil_kernel, sizes), name='stencil_de...  10 us
    ppermute x6, starting transfers between devices, swap(): lax.ppermute(values, ('lat', 'sub'), [(i, i ^ bits) for i in range(count)])  4.1 us
    all_to_all x1, starting transfers between devices, two_chip_device(): lax.all_to_all(raised, 'comp', split_axis=0, concat_axis=0, tiled=True)  3.48 us
    pallas_call x1, Pallas kernels, finish(): pl.pallas_call(functools.partial(finish_kernel, sizes), name='finish', gr...  3.12 us
    pallas_call x1, Pallas kernels, pack(): pl.pallas_call(functools.partial(pack_kernel, sizes), name='pack', in_spe...  2.92 us
  transfers between devices with their start and end apart: 7, of which 5 were waited for; matrix products, arithmetic and copies ran while one was open for 1% of the time, Pallas kernels for 17%

profile of v3, /device:TPU:0, one launch (start us, length us, event | category | flops | bytes accessed | tf_op | source)
XLA Modules:
  0.0 76.9 jit_solution(1685059172432949632)
XLA Ops:
  0.0 0.5 collective-permute-start.5
  0.5 2.9 %pack.1 = (f32[264,512]{1,0:T(8,128)}, f32[264,512]{1,0:T(8,128)}, s16[136,512]{1,0:T(8,128)(2,1)}, s16[136,512]{1,0:T(8,128)(2,1)}) custom-call(f32[480,512]{1,0:T(8,128)} %spectrum.1, s32[4,512]{1,0:T(4,128)} %neighbours.1, s32[1,512]{1,0:T(1,128)} %bitcast.3), custom_call_target="tpu_custom_call" | custom-call | tf_op jit(solution)/shard_map/pack/pallas_call | solution.py:243
  3.4 0.0 collective-permute-start
  3.4 3.0 %collective-permute-start.1 = (s16[136,512]{1,0:T(8,128)(2,1)}, s16[136,512]{1,0:T(8,128)(2,1)S(1)}, u32[]{:S(2)}, u32[]{:S(2)}) collective-permute-start(s16[136,512]{1,0:T(8,128)(2,1)} %get-tuple-element.18), channel_id=1, source_target_pairs={{0,2},{1,3},{2,0},{3,1},{4,6},{5,7},{6,4},{7,5},{8,10},{9,11},{10,... | collective-permute-start | bytes 417800 | tf_op jit(solution)/shard_map/ppermute | solution.py:503
  6.4 0.0 collective-permute-start.2
  6.4 1.1 %collective-permute-done.refs_4_ = f32[264,512]{1,0:T(8,128)S(1)} collective-permute-done((f32[264,512]{1,0:T(8,128)}, f32[264,512]{1,0:T(8,128)S(1)}, u32[]{:S(2)}, u32[]{:S(2)}) %collective-permute-start) | collective-permute-done | bytes 540704 | tf_op jit(solution)/shard_map/ppermute | solution.py:503
  7.5 0.0 copy-start
  7.5 0.8 %copy-done = f32[264,512]{1,0:T(8,128)} copy-done((f32[264,512]{1,0:T(8,128)}, f32[264,512]{1,0:T(8,128)S(1)}, u32[]{:S(2)}) %copy-start) | copy-done | bytes 540696
  8.3 4.3 %stencil_free.1 = (bf16[8,128,128]{2,1,0:T(8,128)(2,1)}, f32[2,128,512]{2,1,0:T(8,128)}) custom-call(s32[30]{0:T(128)} %refs_0_.3, f32[30]{0:T(128)} %refs_1_.3, f32[2,64,128]{2,1,0:T(8,128)} %constant.2.clone.refs_2_, f32[264,512]{1,0:T(8,128)} %get-tuple-element.15.refs_3_, f32[264,512]{1,0:T(8,128)} %copy-done), custom_call_target="tpu_custom_call" | custom-call | flops 78643200 | bytes 2097152 | tf_op jit(solution)/shard_map/stencil_free/pallas_call | solution.py:372
  12.7 0.0 collective-permute-done.1.refs_5_
  12.7 0.0 copy-start.6
  12.7 0.1 collective-permute-done.2.refs_6_
  12.8 0.0 copy-start.7
  12.8 0.5 copy-done.6
  13.3 0.1 copy-done.7
  13.4 5.7 %stencil_dependent.1 = (bf16[8,128,128]{2,1,0:T(8,128)(2,1)}, f32[2,128,512]{2,1,0:T(8,128)}) custom-call(s32[30]{0:T(128)} %refs_0_.3, f32[30]{0:T(128)} %refs_1_.3, f32[2,64,128]{2,1,0:T(8,128)} %constant.2.clone.refs_2_, f32[264,512]{1,0:T(8,128)} %get-tuple-element.15.refs_3_, f32[264,512]{1,0:T(8,128)} %copy-done, s16[136,512]{1,0:T(8,128)(2,1)} %copy-done.6, ...), custom_call_target="tpu_custom_call" | custom-call | flops 78643200 | bytes 2097152 | tf_op jit(solution)/shard_map/stencil_dependent/pallas_call | solution.py:372
  19.1 1.1 %pad_maximum_fusion = bf16[8,256,128]{2,1,0:T(8,128)(2,1)S(1)} fusion(bf16[8,128,128]{2,1,0:T(8,128)(2,1)} %get-tuple-element.24, bf16[8,128,128]{2,1,0:T(8,128)(2,1)} %get-tuple-element.20), kind=kLoop, calls=%fused_computation | loop fusion | flops 1048576 | bytes 1048576 | tf_op jit(solution)/shard_map/concatenate | solution.py:527
  20.2 21.4 %all_to_all.10.arrived = bf16[8,256,128]{2,1,0:T(8,128)(2,1)} all-to-all(bf16[8,256,128]{2,1,0:T(8,128)(2,1)S(1)} %pad_maximum_fusion), channel_id=1, replica_groups=mesh['members'=2,'comp'=4,'lat'=2,'sub'=2] {'comp','sub'}, dimensions={0} | all-to-all | bytes 1048576 | tf_op jit(solution)/shard_map/all_to_all | solution.py:528
  41.6 0.0 copy-start.3
  41.6 0.0 copy-start.2
  41.6 0.0 collective-permute-done.5.other_w
  41.6 14.2 %integrate.1 = bf16[1920,128]{1,0:T(8,128)(2,1)} custom-call(bf16[8,256,128]{2,1,0:T(8,128)(2,1)} %all_to_all.10.arrived, bf16[960,1920]{1,0:T(8,128)(2,1)} %own_w.1, bf16[960,1920]{1,0:T(8,128)(2,1)} %collective-permute-done.5.other_w), custom_call_target="tpu_custom_call" | custom-call | flops 3774873600 | bytes 7372800 | tf_op jit(solution)/shard_map/integrate/pallas_call | solution.py:438
  55.9 3.5 %all-to-all-start.1 = ((bf16[4,480,128]{2,1,0:T(8,128)(2,1)}), bf16[4,480,128]{2,1,0:T(8,128)(2,1)S(1)}, u32[]{:S(2)}, u32[]{:S(2)}) async-start(bf16[4,480,128]{2,1,0:T(8,128)(2,1)} %bitcast.2), calls=%async_computation.1 | async-start | bytes 983040 | tf_op jit(solution)/shard_map/all_to_all | solution.py:533
  59.3 0.0 copy-done.3
  59.4 0.1 collective-permute-start.4
  59.5 0.0 copy-done.2
  59.5 0.5 collective-permute-start.3
  60.0 0.9 %collective-permute-done.4.got_dep = f32[1,128,512]{2,1,0:T(8,128)S(1)} collective-permute-done((f32[1,128,512]{2,1,0:T(8,128)S(1)}, f32[1,128,512]{2,1,0:T(8,128)S(1)}, u32[]{:S(2)}, u32[]{:S(2)}) %collective-permute-start.4) | collective-permute-done | bytes 262176 | tf_op jit(solution)/shard_map/ppermute | solution.py:503
  61.0 0.0 copy-start.4
  61.0 0.4 collective-permute-done.3.got_free
  61.4 0.0 copy-start.5
  61.4 11.7 %all-to-all-done.1.raised = bf16[4,480,128]{2,1,0:T(8,128)(2,1)S(1)} async-done(((bf16[4,480,128]{2,1,0:T(8,128)(2,1)}), bf16[4,480,128]{2,1,0:T(8,128)(2,1)S(1)}, u32[]{:S(2)}, u32[]{:S(2)}) %all-to-all-start.1) | async-done | bytes 491552 | tf_op jit(solution)/shard_map/all_to_all | solution.py:533
  73.0 0.0 copy-done.4
  73.0 0.0 copy-done.5
  73.0 0.0 copy-start.1
  73.0 0.8 %copy-done.1 = bf16[4,480,128]{2,1,0:T(8,128)(2,1)} copy-done((bf16[4,480,128]{2,1,0:T(8,128)(2,1)}, bf16[4,480,128]{2,1,0:T(8,128)(2,1)S(1)}, u32[]{:S(2)}) %copy-start.1) | copy-done | bytes 491544
  73.8 3.1 %finish.1 = f32[480,512]{1,0:T(8,128)} custom-call(f32[2,128,512]{2,1,0:T(8,128)} %get-tuple-element.17.mine_free, f32[2,128,512]{2,1,0:T(8,128)} %get-tuple-element.23.mine_dep, f32[1,128,512]{2,1,0:T(8,128)} %copy-done.5, f32[1,128,512]{2,1,0:T(8,128)} %copy-done.4, bf16[4,480,128]{2,1,0:T(8,128)(2,1)} %copy-done.1, s32[1,512]{1,0:T(1,128)} %bitcast.4), custom_call_target="tpu_custom_call" | custom-call | tf_op jit(solution)/shard_map/finish/pallas_call | solution.py:490
  (2 shorter events, 0.0 us)
Async XLA Ops:
  0.0 41.6 %collective-permute-start.5 = (bf16[960,1920]{1,0:T(8,128)(2,1)}, bf16[960,1920]{1,0:T(8,128)(2,1)}, u32[]{:S(2)}, u32[]{:S(2)}) collective-permute-start(bf16[960,1920]{1,0:T(8,128)(2,1)} %own_w.1), channel_id=1, source_target_pairs={{0,1},{1,0},{2,3},{3,2},{4,5},{5,4},{6,7},{7,6},{8,9},{9,8},{10,11... | collective-permute-start | bytes 11059208 | tf_op jit(solution)/shard_map/ppermute | solution.py:503
  3.4 4.1 %collective-permute-start = (f32[264,512]{1,0:T(8,128)}, f32[264,512]{1,0:T(8,128)S(1)}, u32[]{:S(2)}, u32[]{:S(2)}) collective-permute-start(f32[264,512]{1,0:T(8,128)} %get-tuple-element.16), channel_id=1, source_target_pairs={{0,1},{1,0},{2,3},{3,2},{4,5},{5,4},{6,7},{7,6},{8,9},{9,8},{10,11... | collective-permute-start | bytes 1622024 | tf_op jit(solution)/shard_map/ppermute | solution.py:503
  3.4 9.2 %collective-permute-start.1 = (s16[136,512]{1,0:T(8,128)(2,1)}, s16[136,512]{1,0:T(8,128)(2,1)S(1)}, u32[]{:S(2)}, u32[]{:S(2)}) collective-permute-start(s16[136,512]{1,0:T(8,128)(2,1)} %get-tuple-element.18), channel_id=1, source_target_pairs={{0,2},{1,3},{2,0},{3,1},{4,6},{5,7},{6,4},{7,5},{8,10},{9,11},{10,... | collective-permute-start | bytes 417800 | tf_op jit(solution)/shard_map/ppermute | solution.py:503
  6.4 6.4 %collective-permute-start.2 = (s16[136,512]{1,0:T(8,128)(2,1)}, s16[136,512]{1,0:T(8,128)(2,1)S(1)}, u32[]{:S(2)}, u32[]{:S(2)}) collective-permute-start(s16[136,512]{1,0:T(8,128)(2,1)} %get-tuple-element.19), channel_id=1, source_target_pairs={{0,3},{1,2},{2,1},{3,0},{4,7},{5,6},{6,5},{7,4},{8,11},{9,10},{10,... | collective-permute-start | bytes 417800 | tf_op jit(solution)/shard_map/ppermute | solution.py:503
  7.5 0.8 %copy-start = (f32[264,512]{1,0:T(8,128)}, f32[264,512]{1,0:T(8,128)S(1)}, u32[]{:S(2)}) copy-start(f32[264,512]{1,0:T(8,128)S(1)} %collective-permute-done.refs_4_) | copy-start | bytes 1622020
  12.7 0.7 copy-start.6
  12.8 0.6 copy-start.7
  41.6 17.7 %copy-start.3 = (f32[2,128,512]{2,1,0:T(8,128)S(1)}, f32[2,128,512]{2,1,0:T(8,128)}, u32[]{:S(2)}) copy-start(f32[2,128,512]{2,1,0:T(8,128)} %get-tuple-element.23.mine_dep) | copy-start | bytes 1572868
  41.6 17.8 %copy-start.2 = (f32[2,128,512]{2,1,0:T(8,128)S(1)}, f32[2,128,512]{2,1,0:T(8,128)}, u32[]{:S(2)}) copy-start(f32[2,128,512]{2,1,0:T(8,128)} %get-tuple-element.17.mine_free) | copy-start | bytes 1572868
  55.9 17.2 %all-to-all-start.1 = ((bf16[4,480,128]{2,1,0:T(8,128)(2,1)}), bf16[4,480,128]{2,1,0:T(8,128)(2,1)S(1)}, u32[]{:S(2)}, u32[]{:S(2)}) async-start(bf16[4,480,128]{2,1,0:T(8,128)(2,1)} %bitcast.2), calls=%async_computation.1 | async-start | bytes 983040 | tf_op jit(solution)/shard_map/all_to_all | solution.py:533
  59.4 1.6 %collective-permute-start.4 = (f32[1,128,512]{2,1,0:T(8,128)S(1)}, f32[1,128,512]{2,1,0:T(8,128)S(1)}, u32[]{:S(2)}, u32[]{:S(2)}) collective-permute-start(f32[1,128,512]{2,1,0:T(8,128)S(1)} %slice.7), channel_id=1, source_target_pairs={{0,1},{1,0},{2,3},{3,2},{4,5},{5,4},{6,7},{7,6},{8,9},{9,8},{10,11... | collective-permute-start | bytes 786440 | tf_op jit(solution)/shard_map/ppermute | solution.py:503
  59.5 1.9 %collective-permute-start.3 = (f32[1,128,512]{2,1,0:T(8,128)S(1)}, f32[1,128,512]{2,1,0:T(8,128)S(1)}, u32[]{:S(2)}, u32[]{:S(2)}) collective-permute-start(f32[1,128,512]{2,1,0:T(8,128)S(1)} %slice.6), channel_id=1, source_target_pairs={{0,1},{1,0},{2,3},{3,2},{4,5},{5,4},{6,7},{7,6},{8,9},{9,8},{10,11... | collective-permute-start | bytes 786440 | tf_op jit(solution)/shard_map/ppermute | solution.py:503
  61.0 12.0 %copy-start.4 = (f32[1,128,512]{2,1,0:T(8,128)}, f32[1,128,512]{2,1,0:T(8,128)S(1)}, u32[]{:S(2)}) copy-start(f32[1,128,512]{2,1,0:T(8,128)S(1)} %collective-permute-done.4.got_dep) | copy-start | bytes 786436
  61.4 11.7 %copy-start.5 = (f32[1,128,512]{2,1,0:T(8,128)}, f32[1,128,512]{2,1,0:T(8,128)S(1)}, u32[]{:S(2)}) copy-start(f32[1,128,512]{2,1,0:T(8,128)S(1)} %collective-permute-done.3.got_free) | copy-start | bytes 786436
  73.0 0.8 %copy-start.1 = (bf16[4,480,128]{2,1,0:T(8,128)(2,1)}, bf16[4,480,128]{2,1,0:T(8,128)(2,1)S(1)}, u32[]{:S(2)}) copy-start(bf16[4,480,128]{2,1,0:T(8,128)(2,1)S(1)} %all-to-all-done.1.raised) | copy-start | bytes 1474564

commit v4 on v3

--- a/solution.py
+++ b/solution.py
@@ -153,6 +153,7 @@
 QUAD = 16
 SECTOR = 32
 CODE_SCALE = 32767.5
+GRANT = pltpu.CompilerParams(vmem_limit_bytes=12 << 20)
 
 
 def lane_pick(values, index):
@@ -243,17 +244,19 @@
     return pl.pallas_call(
         functools.partial(pack_kernel, sizes),
         name="pack",
+        compiler_params=GRANT,
         in_specs=[vmem, vmem, vmem],
         out_specs=[vmem] * 4,
-        out_shape=[jax.ShapeDtypeStruct((half_bins + TILE, points), jnp.float32)] * 2
-        + [jax.ShapeDtypeStruct((half_bins // 2 + TILE, points), jnp.int16)] * 2,
+        out_shape=[pltpu.VMEM((half_bins + TILE, points), jnp.float32)] * 2
+        + [pltpu.VMEM((half_bins // 2 + TILE, points), jnp.int16)] * 2,
     )(spectrum, neighbours, sea_mask)
 
 
 def stencil_kernel(sizes, *refs):
     bins_local, half_bins, rows_local, dependent = sizes
     if dependent:
-        steps_ref, courant_ref, trig, mine, pair, near, far, start_out, field_out, tab = refs
+        (steps_ref, courant_ref, trig, mine, pair, near, far, free_start, own_w, other_w) = refs[:10]
+        start_out, field_out, whole_w, tab, sem = refs[10:]
     else:
         steps_ref, courant_ref, trig, mine, pair, start_out, field_out, tab = refs
     lat, sub, parity, first_group = device_place(bins_local)
@@ -261,6 +264,18 @@
     first_group = first_group + sub * (half_bins // SECTOR)
     chip_rows = 2 * rows_local
     halo = chip_rows if dependent else 0
+    sent_first = 0
+    copies = []
+    if dependent:
+        w_rows = own_w.shape[0]
+        for other, source in enumerate((own_w, other_w)):
+            at = pl.ds(pl.multiple_of((sub + other) % 2 * w_rows, 64), w_rows)
+            copy = pltpu.make_async_copy(source, whole_w.at[at], sem.at[other])
+            copy.start()
+            copies.append(copy)
+        sent_first = half_bins // 2
+        for block in range(start_out.shape[0]):
+            start_out[block, :sent_first, :] = free_start[block]
     north = lat == (0 if dependent else 1)
     flip = north.astype(jnp.int32)
 
@@ -304,6 +319,7 @@
         trig_row = pl.ds(pl.multiple_of(SECTOR * flip + QUAD * side, QUAD), QUAD)
         part_row = pl.ds(pl.multiple_of(group * SECTOR + side * QUAD, QUAD), QUAD)
         sent_row = pl.ds(pl.multiple_of(sector * SECTOR + side * QUAD, QUAD), QUAD)
+        start_row = pl.ds(pl.multiple_of(sent_first + sector * SECTOR + side * QUAD, QUAD), QUAD)
         trig_x, trig_y = tiles(trig[0, trig_row, :]), tiles(trig[1, trig_row, :])
         field = []
         for u in range(halo + chip_rows):
@@ -351,7 +367,7 @@
             core, local, here = where_is(v)
             for half in range(2):
                 value = field[halo + v][half].reshape(QUAD, LANES)
-                start_out[(local * 2 + half) * 2 + core, sent_row, :] = value.astype(jnp.bfloat16)
+                start_out[(local * 2 + half) * 2 + core, start_row, :] = value.astype(jnp.bfloat16)
                 field_out[1 - here.astype(jnp.int32), sent_row, lanes_of(local, half)] = value
 
     def both_sides(sector, carry):
@@ -360,40 +376,44 @@
         return carry
 
     lax.fori_loop(0, half_bins // (2 * SECTOR), both_sides, 0)
-
-
-def stencil(sizes, substeps, courant, trig, *fields):
+    for copy in copies:
+        copy.wait()
+
+
+def stencil(sizes, substeps, courant, trig, *fields, operator=()):
     bins_local, half_bins, rows_local, dependent = sizes
     blocks = 4 * rows_local
     rows = (4 if dependent else 2) * rows_local
     smem = pl.BlockSpec(memory_space=pltpu.SMEM)
     vmem = pl.BlockSpec(memory_space=pltpu.VMEM)
+    hbm = pl.BlockSpec(memory_space=pl.ANY)
     cells = half_bins // 2 * rows_local * 2 * NLON
+    start_bins = half_bins if dependent else half_bins // 2
+    out_shape = [
+        pltpu.VMEM((blocks, start_bins, LANES), jnp.bfloat16),
+        pltpu.VMEM((2, half_bins // 2, rows_local * NLON), jnp.float32),
+    ]
+    scratch = [pltpu.VMEM((rows, 2, 4, TILE, LANES), jnp.float32)]
+    if dependent:
+        total = operator[0].shape[1]
+        out_shape.append(pltpu.VMEM((total, total), jnp.bfloat16))
+        scratch.append(pltpu.SemaphoreType.DMA((2,)))
     return pl.pallas_call(
         functools.partial(stencil_kernel, sizes),
         name="stencil_dependent" if dependent else "stencil_free",
-        in_specs=[smem] * 2 + [vmem] * (1 + len(fields)),
-        out_specs=[vmem, vmem],
-        out_shape=[
-            jax.ShapeDtypeStruct((blocks, half_bins // 2, LANES), jnp.bfloat16),
-            jax.ShapeDtypeStruct((2, half_bins // 2, rows_local * NLON), jnp.float32),
-        ],
-        scratch_shapes=[pltpu.VMEM((rows, 2, 4, TILE, LANES), jnp.float32)],
+        compiler_params=GRANT,
+        in_specs=[smem] * 2 + [vmem] * (1 + len(fields)) + [hbm] * len(operator),
+        out_specs=[vmem] * len(out_shape),
+        out_shape=out_shape,
+        scratch_shapes=scratch,
         cost_estimate=pl.CostEstimate(flops=cells * MAXSTEPS * 100, bytes_accessed=cells * 16, transcendentals=0),
-    )(substeps, courant, trig, *fields)
-
-
-def integrate_kernel(sizes, arrived, own_w, other_w, out, w_ref, joined, state, driver, sem):
+    )(*map(off_chip, (substeps, courant, trig)), *map(on_chip, fields), *map(off_chip, operator))
+
+
+def integrate_kernel(sizes, arrived, whole_w, out, state, driver):
     bins_local, half_bins, comps = sizes
-    lat, sub, _, _ = device_place(bins_local)
-    w_rows = own_w.shape[0]
+    lat = lax.axis_index("lat")
     total = comps * bins_local
-    copies = []
-    for other, source in enumerate((own_w, other_w)):
-        at = pl.ds(pl.multiple_of((sub + other) % 2 * w_rows, 64), w_rows)
-        copy = pltpu.make_async_copy(source, w_ref.at[at], sem.at[other])
-        copy.start()
-        copies.append(copy)
     sectors = half_bins // (2 * SECTOR)
     groups = bins_local // SECTOR
     for c in range(comps):
@@ -404,55 +424,43 @@
                     parity = (first + lat + dep) % 2
                     row = c * bins_local + s * half_bins + (2 * k + parity) * SECTOR
                     row = pl.ds(pl.multiple_of(row, SECTOR), SECTOR)
-                    joined[row, :] = arrived[2 * c + s, (sectors * dep + k) * SECTOR : (sectors * dep + k + 1) * SECTOR, :]
-    for b in range(total // LANES):
-        at = slice(b * LANES, (b + 1) * LANES)
-        block = joined[at, :].astype(jnp.float32).T
-        state[:, at] = block
-        driver[0, :, at] = block.astype(jnp.bfloat16)
-    for copy in copies:
-        copy.wait()
-    width = 2 * LANES
+                    block = arrived[2 * c + s, (sectors * dep + k) * SECTOR : (sectors * dep + k + 1) * SECTOR, :]
+                    driver[0, row, :] = block
+                    state[row, :] = block.astype(jnp.float32)
+    stretch = total // 2
     for step in range(SRC_STEPS):
         read = 0 if step == 0 else 1 + step % 2
-        for first in range(0, total, width):
-            at = slice(first, min(first + width, total))
-            drive = lax.dot_general(
-                driver[read], w_ref[at, :], (((1,), (1,)), ((), ())), preferred_element_type=jnp.float32
-            )
-            value = state[:, at]
+        for first in range(0, total, stretch):
+            at = slice(first, first + stretch)
+            drive = jnp.dot(whole_w[at, :], driver[read, :total, :], preferred_element_type=jnp.float32)
+            value = state[at, :]
             value = value + STEP_SIZE * value * drive
             if step + 1 < SRC_STEPS:
-                state[:, at] = value
-                driver[1 + (step + 1) % 2, :, at] = value.astype(jnp.bfloat16)
+                state[at, :] = value
+                driver[1 + (step + 1) % 2, at, :] = value.astype(jnp.bfloat16)
             else:
-                raised = value - driver[0, :, at].astype(jnp.float32)
-                out[at, :] = raised.T.astype(jnp.bfloat16)
-
-
-def integrate(sizes, arrived, own_w, other_w):
+                out[at, :] = (value - driver[0, at, :].astype(jnp.float32)).astype(jnp.bfloat16)
+
+
+def integrate(sizes, arrived, whole_w):
     bins_local, half_bins, comps = sizes
     total = comps * bins_local
     vmem = pl.BlockSpec(memory_space=pltpu.VMEM)
-    hbm = pl.BlockSpec(memory_space=pl.ANY)
     return pl.pallas_call(
         functools.partial(integrate_kernel, sizes),
         name="integrate",
-        in_specs=[vmem, hbm, hbm],
+        compiler_params=GRANT,
+        in_specs=[vmem, vmem],
         out_specs=vmem,
-        out_shape=jax.ShapeDtypeStruct((total, LANES), jnp.bfloat16),
+        out_shape=pltpu.VMEM((total, LANES), jnp.bfloat16),
         scratch_shapes=[
-            pltpu.VMEM((total, total), jnp.bfloat16),
-            pltpu.VMEM((total + SECTOR, LANES), jnp.bfloat16),
-            pltpu.VMEM((LANES, total), jnp.float32),
-            pltpu.VMEM((3, LANES, total), jnp.bfloat16),
-            pltpu.SemaphoreType.DMA((2,)),
+            pltpu.VMEM((total + SECTOR, LANES), jnp.float32),
+            pltpu.VMEM((3, total + SECTOR, LANES), jnp.bfloat16),
         ],
-        compiler_params=pltpu.CompilerParams(vmem_limit_bytes=60 << 20),
         cost_estimate=pl.CostEstimate(
             flops=2 * SRC_STEPS * total * total * LANES, bytes_accessed=2 * total * total, transcendentals=0
         ),
-    )(arrived, own_w, other_w)
+    )(on_chip(arrived), on_chip(whole_w))
 
 
 def finish_kernel(sizes, mine_free, mine_dep, got_free, got_dep, raised, sea_mask, out, whole, sem):
@@ -463,10 +471,17 @@
         jnp.broadcast_to(sea_mask[0:1, j * LANES : (j + 1) * LANES].astype(jnp.float32), (SECTOR, LANES))
         for j in range(tiles)
     ]
+    sectors = half_bins // (2 * SECTOR)
+
+    def rows_out(group, semaphore):
+        at = pl.ds(pl.multiple_of(group, SECTOR), SECTOR)
+        return pltpu.make_async_copy(whole.at[at], out.at[at], semaphore)
+
     for other, pair in enumerate(((mine_free, mine_dep), (got_free, got_dep))):
-        for k in range(half_bins // (2 * SECTOR)):
+        base = (sub + other) % 2 * half_bins
+        for k in range(sectors):
             for dep, source in enumerate(pair):
-                row = (sub + other) % 2 * half_bins + (2 * k + (parity + dep) % 2) * SECTOR
+                row = base + (2 * k + (parity + dep) % 2) * SECTOR
                 rows = pl.ds(pl.multiple_of(row, SECTOR), SECTOR)
                 added = pl.ds(pl.multiple_of(jnp.minimum(row, bins_local - SECTOR), SECTOR), SECTOR)
                 for j in range(0, tiles, 2):
@@ -477,25 +492,48 @@
                     ]
                     for i, value in enumerate(join_columns(*halves)):
                         whole[rows, (j + i) * LANES : (j + i + 1) * LANES] = sea[j + i] * value
-    copy = pltpu.make_async_copy(whole.at[pl.ds(0, bins_local)], out, sem)
-    copy.start()
-    copy.wait()
+            for rest in range(2):
+                group = base + (2 * k + rest) * SECTOR
+
+                @pl.when(group < bins_local)
+                def _():
+                    rows_out(group, sem.at[other, k, rest]).start()
+
+    for other in range(2):
+        for k in range(sectors):
+            for rest in range(2):
+                group = (sub + other) % 2 * half_bins + (2 * k + rest) * SECTOR
+
+                @pl.when(group < bins_local)
+                def _():
+                    rows_out(group, sem.at[other, k, rest]).wait()
 
 
 def finish(sizes, mine_free, mine_dep, got_free, got_dep, raised, sea_mask):
     bins_local, half_bins = sizes
     points = sea_mask.shape[1]
     vmem = pl.BlockSpec(memory_space=pltpu.VMEM)
-    first = pl.BlockSpec((1, half_bins // 2, points), lambda i: (0, 0, 0))
+    fields = [on_chip(field) for field in (mine_free, mine_dep, got_free, got_dep, raised)]
     return pl.pallas_call(
         functools.partial(finish_kernel, sizes),
         name="finish",
-        grid=(1,),
-        in_specs=[first, first, first, first, vmem, vmem],
+        compiler_params=GRANT,
+        in_specs=[vmem] * 6,
         out_specs=pl.BlockSpec(memory_space=pl.ANY),
         out_shape=jax.ShapeDtypeStruct((bins_local, points), jnp.float32),
-        scratch_shapes=[pltpu.VMEM((2 * half_bins, points), jnp.float32), pltpu.SemaphoreType.DMA],
-    )(mine_free, mine_dep, got_free, got_dep, raised, sea_mask)
+        scratch_shapes=[
+            pltpu.VMEM((2 * half_bins, points), jnp.float32),
+            pltpu.SemaphoreType.DMA((2, half_bins // (2 * SECTOR), 2)),
+        ],
+    )(*fields, sea_mask)
+
+
+def on_chip(values):
+    return pltpu.with_memory_space_constraint(values, pltpu.VMEM)
+
+
+def off_chip(values):
+    return pltpu.with_memory_space_constraint(values, pltpu.HBM)
 
 
 def swap(values, bits):
@@ -521,14 +559,22 @@
 
     free_start, free_field = stencil((bins_local, half_bins, rows_local, False), substeps, courant, trig, mine, pair)
     near, far, _ = lax.optimization_barrier((near, far, free_start))
-    dep_start, dep_field = stencil(
-        (bins_local, half_bins, rows_local, True), substeps, courant, trig, mine, pair, near, far
-    )
-    start = jnp.concatenate([free_start, dep_start], axis=1)
+    start, dep_field, whole_w = stencil(
+        (bins_local, half_bins, rows_local, True),
+        substeps,
+        courant,
+        trig,
+        mine,
+        pair,
+        near,
+        far,
+        free_start,
+        operator=(source_operator, other_w),
+    )
     arrived = lax.all_to_all(start, ("comp", "sub"), split_axis=0, concat_axis=0, tiled=True)
     got_free = swap(free_field[1:], 1)
     got_dep = swap(dep_field[1:], 1)
-    raised = integrate((bins_local, half_bins, comps), arrived, source_operator, other_w)
+    raised = integrate((bins_local, half_bins, comps), arrived, whole_w)
     raised = raised.reshape(comps, bins_local, LANES)
     home = lax.all_to_all(raised, "comp", split_axis=0, concat_axis=0, tiled=True)
     return finish((bins_local, half_bins), free_field, dep_field, got_free, got_dep, home, sea_mask)

time: 77.3 us -> 68.1 us (0.88)
  Pallas kernels: 30.3 us -> 19.1 us
  local copies, waits for them, and re-layouts: 2.28 us -> 4.42 us
  waiting for transfers between devices: 14.2 us -> 16.2 us
  blocking collectives: 21.4 us -> 20.3 us
  other arithmetic: 1.06 us -> 0 us
    pallas_call x1, Pallas kernels: 14.2 us -> 9.26 us  [integrate(): pl.pallas_call(functools.partial(integrate_kernel, sizes), name='integrat...]
    pallas_call x2, Pallas kernels: 6.04 us -> 2.43 us  [the longest x1 1.61 us: finish(): pl.pallas_call(functools.partial(finish_kernel, sizes), name='finish', co...]
    pallas_call x2, Pallas kernels: 10 us -> 7.41 us  [stencil(): pl.pallas_call(functools.partial(stencil_kernel, sizes), name='stencil_de...]
    unnamed x16 -> x10, local copies, waits for them, and re-layouts: 2.25 us -> 4.38 us
    ppermute x6, waiting for transfers between devices: 2.57 us -> 4.54 us  [swap(): lax.ppermute(values, ('lat', 'sub'), [(i, i ^ bits) for i in range(count)])]
    all_to_all x1, blocking collectives: 21.4 us -> 20.3 us  [two_chip_device(): lax.all_to_all(start, ('comp', 'sub'), split_axis=0, concat_axis=0, tiled...]
    concatenate x1 -> x0, other arithmetic: 1.06 us -> none  [two_chip_device(): start = jnp.concatenate([free_start, dep_start], axis=1)]
  transfers between devices with their start and end apart: 7 -> 7, of which waited for: 5 -> 6; matrix products, arithmetic and copies ran while one was open for 1% -> 0% of each run, Pallas kernels for 17% -> 6%
where the time goes in v4:
time: 68.1 us; the launch traced here: 67.7 us
  blocking collectives  20.3 us (30%)
  Pallas kernels  19.1 us (28%)
  waiting for transfers between devices  16.2 us (24%)
  starting transfers between devices  7.64 us (11%)
  local copies, waits for them, and re-layouts  4.42 us (6%)
    all_to_all x1, blocking collectives, two_chip_device(): lax.all_to_all(start, ('comp', 'sub'), split_axis=0, concat_axis=0, tiled...  20.3 us
    all_to_all x1, waiting for transfers between devices, two_chip_device(): lax.all_to_all(raised, 'comp', split_axis=0, concat_axis=0, tiled=True)  11.7 us
    pallas_call x1, Pallas kernels, integrate(): pl.pallas_call(functools.partial(integrate_kernel, sizes), name='integrat...  9.26 us
    pallas_call x2, Pallas kernels, stencil(): pl.pallas_call(functools.partial(stencil_kernel, sizes), name='stencil_de...  7.41 us
    ppermute x6, waiting for transfers between devices, swap(): lax.ppermute(values, ('lat', 'sub'), [(i, i ^ bits) for i in range(count)])  4.54 us
    unnamed x10, local copies, waits for them, and re-layouts  4.38 us
    ppermute x6, starting transfers between devices, swap(): lax.ppermute(values, ('lat', 'sub'), [(i, i ^ bits) for i in range(count)])  4.17 us
    all_to_all x1, starting transfers between devices, two_chip_device(): lax.all_to_all(raised, 'comp', split_axis=0, concat_axis=0, tiled=True)  3.47 us
  transfers between devices with their start and end apart: 7, of which 6 were waited for; matrix products, arithmetic and copies ran while one was open for 0% of the time, Pallas kernels for 6%

profile of v4, /device:TPU:0, one launch (start us, length us, event | category | flops | bytes accessed | tf_op | source)
XLA Modules:
  0.0 67.7 jit_solution(2055436029884737113)
XLA Ops:
  0.0 0.5 collective-permute-start.3
  0.5 0.0 copy-start
  0.5 1.2 %copy-done = f32[480,512]{1,0:T(8,128)S(1)} copy-done((f32[480,512]{1,0:T(8,128)S(1)}, f32[480,512]{1,0:T(8,128)}, u32[]{:S(2)}) %copy-start) | copy-done | bytes 983064
  1.7 0.0 copy-start.1
  1.7 0.7 %copy-done.1 = s32[4,512]{1,0:T(4,128)S(1)} copy-done((s32[4,512]{1,0:T(4,128)S(1)}, s32[4,512]{1,0:T(4,128)}, u32[]{:S(2)}) %copy-start.1) | copy-done | bytes 8216
  2.4 0.0 copy-start.2
  2.4 0.7 %copy-done.2 = s32[512]{0:T(512)S(1)} copy-done((s32[512]{0:T(512)S(1)}, s32[512]{0:T(512)}, u32[]{:S(2)}) %copy-start.2) | copy-done | bytes 2072
  3.1 0.8 %pack.1 = (f32[264,512]{1,0:T(8,128)S(1)}, f32[264,512]{1,0:T(8,128)S(1)}, s16[136,512]{1,0:T(8,128)(2,1)S(1)}, s16[136,512]{1,0:T(8,128)(2,1)S(1)}) custom-call(f32[480,512]{1,0:T(8,128)S(1)} %copy-done, s32[4,512]{1,0:T(4,128)S(1)} %copy-done.1, s32[1,512]{1,0:T(1,128)S(1)} %bitcast.2), custom_call_target="tpu_custom_call" | custom-call | tf_op jit(solution)/shard_map/pack/pallas_call | solution.py:244
  3.9 0.1 collective-permute-start
  4.0 3.0 %collective-permute-start.1 = (s16[136,512]{1,0:T(8,128)(2,1)S(1)}, s16[136,512]{1,0:T(8,128)(2,1)S(1)}, u32[]{:S(2)}, u32[]{:S(2)}) collective-permute-start(s16[136,512]{1,0:T(8,128)(2,1)S(1)} %get-tuple-element.19), channel_id=1, source_target_pairs={{0,2},{1,3},{2,0},{3,1},{4,6},{5,7},{6,4},{7,5},{8,10},{9,11},{10,... | collective-permute-start | bytes 417800 | tf_op jit(solution)/shard_map/ppermute | solution.py:541
  7.0 0.0 collective-permute-start.2
  7.0 0.6 collective-permute-done.refs_4_
  7.5 3.1 %stencil_free.1 = (bf16[8,128,128]{2,1,0:T(8,128)(2,1)S(1)}, f32[2,128,512]{2,1,0:T(8,128)S(1)}) custom-call(s32[30]{0:T(128)} %refs_0_.3, f32[30]{0:T(128)} %refs_1_.3, f32[2,64,128]{2,1,0:T(8,128)} %constant.2.clone.refs_2_, f32[264,512]{1,0:T(8,128)S(1)} %get-tuple-element.16.refs_3_, f32[264,512]{1,0:T(8,128)S(1)} %collective-permute-done.refs_4_), custom_call_target="tpu_custom_call" | custom-call | flops 78643200 | bytes 2097152 | tf_op jit(solution)/shard_map/stencil_free/pallas_call | solution.py:401
  10.6 0.9 %collective-permute-done.1.refs_5_ = s16[136,512]{1,0:T(8,128)(2,1)S(1)} collective-permute-done((s16[136,512]{1,0:T(8,128)(2,1)S(1)}, s16[136,512]{1,0:T(8,128)(2,1)S(1)}, u32[]{:S(2)}, u32[]{:S(2)}) %collective-permute-start.1) | collective-permute-done | bytes 139296 | tf_op jit(solution)/shard_map/ppermute | solution.py:541
  11.5 1.8 %collective-permute-done.2.refs_6_ = s16[136,512]{1,0:T(8,128)(2,1)S(1)} collective-permute-done((s16[136,512]{1,0:T(8,128)(2,1)S(1)}, s16[136,512]{1,0:T(8,128)(2,1)S(1)}, u32[]{:S(2)}, u32[]{:S(2)}) %collective-permute-start.2) | collective-permute-done | bytes 139296 | tf_op jit(solution)/shard_map/ppermute | solution.py:541
  13.2 0.0 collective-permute-done.3.refs_9_
  13.3 0.0 copy-start.4
  13.3 1.8 %copy-done.4 = bf16[960,1920]{1,0:T(8,128)(2,1)} copy-done((bf16[960,1920]{1,0:T(8,128)(2,1)}, bf16[960,1920]{1,0:T(8,128)(2,1)S(1)}, u32[]{:S(2)}) %copy-start.4) | copy-done | bytes 3686424
  15.1 4.4 %stencil_dependent.1 = (bf16[8,256,128]{2,1,0:T(8,128)(2,1)S(1)}, f32[2,128,512]{2,1,0:T(8,128)S(1)}, bf16[1920,1920]{1,0:T(8,128)(2,1)S(1)}) custom-call(s32[30]{0:T(128)} %refs_0_.3, f32[30]{0:T(128)} %refs_1_.3, f32[2,64,128]{2,1,0:T(8,128)} %constant.2.clone.refs_2_, f32[264,512]{1,0:T(8,128)S(1)} %get-tuple-element.16.refs_3_, ...), custom_call_target="tpu_custom_call" | custom-call | flops 78643200 | bytes 2097152 | tf_op jit(solution)/shard_map/stencil_dependent/pallas_call | solution.py:401
  19.4 20.3 %all_to_all.10.arrived = bf16[8,256,128]{2,1,0:T(8,128)(2,1)S(1)} all-to-all(bf16[8,256,128]{2,1,0:T(8,128)(2,1)S(1)} %get-tuple-element.25), channel_id=1, replica_groups=mesh['members'=2,'comp'=4,'lat'=2,'sub'=2] {'comp','sub'}, dimensions={0} | all-to-all | bytes 1048576 | tf_op jit(solution)/shard_map/all_to_all | solution.py:574
  39.7 0.0 copy-start.3
  39.7 9.3 %integrate.1 = bf16[1920,128]{1,0:T(8,128)(2,1)} custom-call(bf16[8,256,128]{2,1,0:T(8,128)(2,1)S(1)} %all_to_all.10.arrived, bf16[1920,1920]{1,0:T(8,128)(2,1)S(1)} %get-tuple-element.26.whole_w), custom_call_target="tpu_custom_call" | custom-call | flops 3774873600 | bytes 7372800 | tf_op jit(solution)/shard_map/integrate/pallas_call | solution.py:449
  49.0 3.5 %all-to-all-start.1 = ((bf16[4,480,128]{2,1,0:T(8,128)(2,1)}), bf16[4,480,128]{2,1,0:T(8,128)(2,1)S(1)}, u32[]{:S(2)}, u32[]{:S(2)}) async-start(bf16[4,480,128]{2,1,0:T(8,128)(2,1)} %bitcast.1), calls=%async_computation.1 | async-start | bytes 983040 | tf_op jit(solution)/shard_map/all_to_all | solution.py:579
  52.5 0.1 collective-permute-start.4
  52.6 0.6 collective-permute-start.5
  53.1 0.9 %collective-permute-done.4.got_free = f32[1,128,512]{2,1,0:T(8,128)S(1)} collective-permute-done((f32[1,128,512]{2,1,0:T(8,128)S(1)}, f32[1,128,512]{2,1,0:T(8,128)S(1)}, u32[]{:S(2)}, u32[]{:S(2)}) %collective-permute-start.4) | collective-permute-done | bytes 262176 | tf_op jit(solution)/shard_map/ppermute | solution.py:541
  54.1 0.4 collective-permute-done.5.got_dep
  54.4 11.7 %all-to-all-done.1.raised = bf16[4,480,128]{2,1,0:T(8,128)(2,1)S(1)} async-done(((bf16[4,480,128]{2,1,0:T(8,128)(2,1)}), bf16[4,480,128]{2,1,0:T(8,128)(2,1)S(1)}, u32[]{:S(2)}, u32[]{:S(2)}) %all-to-all-start.1) | async-done | bytes 491552 | tf_op jit(solution)/shard_map/all_to_all | solution.py:579
  66.1 0.0 copy-done.3
  66.1 1.6 %finish.1 = f32[480,512]{1,0:T(8,128)} custom-call(f32[2,128,512]{2,1,0:T(8,128)S(1)} %get-tuple-element.18.mine_free, f32[2,128,512]{2,1,0:T(8,128)S(1)} %get-tuple-element.24.mine_dep, f32[1,128,512]{2,1,0:T(8,128)S(1)} %collective-permute-done.4.got_free, f32[1,128,512]{2,1,0:T(8,128)S(1)} %collective-permute-done.5.got_dep, ...), custom_call_target="tpu_custom_call" | custom-call | tf_op jit(solution)/shard_map/finish/pallas_call | solution.py:517
  (2 shorter events, 0.0 us)
Async XLA Ops:
  0.0 13.2 %collective-permute-start.3 = (bf16[960,1920]{1,0:T(8,128)(2,1)}, bf16[960,1920]{1,0:T(8,128)(2,1)S(1)}, u32[]{:S(2)}, u32[]{:S(2)}) collective-permute-start(bf16[960,1920]{1,0:T(8,128)(2,1)} %refs_8_.1), channel_id=1, source_target_pairs={{0,1},{1,0},{2,3},{3,2},{4,5},{5,4},{6,7},{7,6},{8,9},{9,8},{10,11... | collective-permute-start | bytes 11059208 | tf_op jit(solution)/shard_map/ppermute | solution.py:541
  0.5 1.2 %copy-start = (f32[480,512]{1,0:T(8,128)S(1)}, f32[480,512]{1,0:T(8,128)}, u32[]{:S(2)}) copy-start(f32[480,512]{1,0:T(8,128)} %spectrum.1) | copy-start | bytes 2949124
  1.7 0.7 %copy-start.1 = (s32[4,512]{1,0:T(4,128)S(1)}, s32[4,512]{1,0:T(4,128)}, u32[]{:S(2)}) copy-start(s32[4,512]{1,0:T(4,128)} %neighbours.1) | copy-start | bytes 24580
  2.4 0.7 %copy-start.2 = (s32[512]{0:T(512)S(1)}, s32[512]{0:T(512)}, u32[]{:S(2)}) copy-start(s32[512]{0:T(512)} %param.8) | copy-start | bytes 6148
  3.9 3.6 %collective-permute-start = (f32[264,512]{1,0:T(8,128)S(1)}, f32[264,512]{1,0:T(8,128)S(1)}, u32[]{:S(2)}, u32[]{:S(2)}) collective-permute-start(f32[264,512]{1,0:T(8,128)S(1)} %get-tuple-element.17), channel_id=1, source_target_pairs={{0,1},{1,0},{2,3},{3,2},{4,5},{5,4},{6,7},{7,6},{8,9},{9,8},{10,11... | collective-permute-start | bytes 1622024 | tf_op jit(solution)/shard_map/ppermute | solution.py:541
  4.0 7.5 %collective-permute-start.1 = (s16[136,512]{1,0:T(8,128)(2,1)S(1)}, s16[136,512]{1,0:T(8,128)(2,1)S(1)}, u32[]{:S(2)}, u32[]{:S(2)}) collective-permute-start(s16[136,512]{1,0:T(8,128)(2,1)S(1)} %get-tuple-element.19), channel_id=1, source_target_pairs={{0,2},{1,3},{2,0},{3,1},{4,6},{5,7},{6,4},{7,5},{8,10},{9,11},{10,... | collective-permute-start | bytes 417800 | tf_op jit(solution)/shard_map/ppermute | solution.py:541
  7.0 6.3 %collective-permute-start.2 = (s16[136,512]{1,0:T(8,128)(2,1)S(1)}, s16[136,512]{1,0:T(8,128)(2,1)S(1)}, u32[]{:S(2)}, u32[]{:S(2)}) collective-permute-start(s16[136,512]{1,0:T(8,128)(2,1)S(1)} %get-tuple-element.20), channel_id=1, source_target_pairs={{0,3},{1,2},{2,1},{3,0},{4,7},{5,6},{6,5},{7,4},{8,11},{9,10},{10,... | collective-permute-start | bytes 417800 | tf_op jit(solution)/shard_map/ppermute | solution.py:541
  13.3 1.8 %copy-start.4 = (bf16[960,1920]{1,0:T(8,128)(2,1)}, bf16[960,1920]{1,0:T(8,128)(2,1)S(1)}, u32[]{:S(2)}) copy-start(bf16[960,1920]{1,0:T(8,128)(2,1)S(1)} %collective-permute-done.3.refs_9_) | copy-start | bytes 11059204
  39.7 26.4 %copy-start.3 = (s32[512]{0:T(512)S(1)}, s32[512]{0:T(512)}, u32[]{:S(2)}) copy-start(s32[512]{0:T(512)} %param.8) | copy-start | bytes 6148
  49.0 17.1 %all-to-all-start.1 = ((bf16[4,480,128]{2,1,0:T(8,128)(2,1)}), bf16[4,480,128]{2,1,0:T(8,128)(2,1)S(1)}, u32[]{:S(2)}, u32[]{:S(2)}) async-start(bf16[4,480,128]{2,1,0:T(8,128)(2,1)} %bitcast.1), calls=%async_computation.1 | async-start | bytes 983040 | tf_op jit(solution)/shard_map/all_to_all | solution.py:579
  52.5 1.6 %collective-permute-start.4 = (f32[1,128,512]{2,1,0:T(8,128)S(1)}, f32[1,128,512]{2,1,0:T(8,128)S(1)}, u32[]{:S(2)}, u32[]{:S(2)}) collective-permute-start(f32[1,128,512]{2,1,0:T(8,128)S(1)} %slice.6), channel_id=1, source_target_pairs={{0,1},{1,0},{2,3},{3,2},{4,5},{5,4},{6,7},{7,6},{8,9},{9,8},{10,11... | collective-permute-start | bytes 786440 | tf_op jit(solution)/shard_map/ppermute | solution.py:541
  52.6 1.9 %collective-permute-start.5 = (f32[1,128,512]{2,1,0:T(8,128)S(1)}, f32[1,128,512]{2,1,0:T(8,128)S(1)}, u32[]{:S(2)}, u32[]{:S(2)}) collective-permute-start(f32[1,128,512]{2,1,0:T(8,128)S(1)} %slice.7), channel_id=1, source_target_pairs={{0,1},{1,0},{2,3},{3,2},{4,5},{5,4},{6,7},{7,6},{8,9},{9,8},{10,11... | collective-permute-start | bytes 786440 | tf_op jit(solution)/shard_map/ppermute | solution.py:541

commit v5 on v4

--- a/solution.py
+++ b/solution.py
@@ -153,7 +153,7 @@
 QUAD = 16
 SECTOR = 32
 CODE_SCALE = 32767.5
-GRANT = pltpu.CompilerParams(vmem_limit_bytes=12 << 20)
+GRANT = pltpu.CompilerParams(vmem_limit_bytes=16 << 20)
 
 
 def lane_pick(values, index):
@@ -249,14 +249,13 @@
         out_specs=[vmem] * 4,
         out_shape=[pltpu.VMEM((half_bins + TILE, points), jnp.float32)] * 2
         + [pltpu.VMEM((half_bins // 2 + TILE, points), jnp.int16)] * 2,
-    )(spectrum, neighbours, sea_mask)
+    )(*map(off_chip, (spectrum, neighbours, sea_mask)))
 
 
 def stencil_kernel(sizes, *refs):
     bins_local, half_bins, rows_local, dependent = sizes
     if dependent:
-        (steps_ref, courant_ref, trig, mine, pair, near, far, free_start, own_w, other_w) = refs[:10]
-        start_out, field_out, whole_w, tab, sem = refs[10:]
+        steps_ref, courant_ref, trig, mine, pair, near, far, free_start, start_out, field_out, tab = refs
     else:
         steps_ref, courant_ref, trig, mine, pair, start_out, field_out, tab = refs
     lat, sub, parity, first_group = device_place(bins_local)
@@ -265,14 +264,7 @@
     chip_rows = 2 * rows_local
     halo = chip_rows if dependent else 0
     sent_first = 0
-    copies = []
     if dependent:
-        w_rows = own_w.shape[0]
-        for other, source in enumerate((own_w, other_w)):
-            at = pl.ds(pl.multiple_of((sub + other) % 2 * w_rows, 64), w_rows)
-            copy = pltpu.make_async_copy(source, whole_w.at[at], sem.at[other])
-            copy.start()
-            copies.append(copy)
         sent_first = half_bins // 2
         for block in range(start_out.shape[0]):
             start_out[block, :sent_first, :] = free_start[block]
@@ -376,17 +368,14 @@
         return carry
 
     lax.fori_loop(0, half_bins // (2 * SECTOR), both_sides, 0)
-    for copy in copies:
-        copy.wait()
-
-
-def stencil(sizes, substeps, courant, trig, *fields, operator=()):
+
+
+def stencil(sizes, substeps, courant, trig, *fields):
     bins_local, half_bins, rows_local, dependent = sizes
     blocks = 4 * rows_local
     rows = (4 if dependent else 2) * rows_local
     smem = pl.BlockSpec(memory_space=pltpu.SMEM)
     vmem = pl.BlockSpec(memory_space=pltpu.VMEM)
-    hbm = pl.BlockSpec(memory_space=pl.ANY)
     cells = half_bins // 2 * rows_local * 2 * NLON
     start_bins = half_bins if dependent else half_bins // 2
     out_shape = [
@@ -394,26 +383,34 @@
         pltpu.VMEM((2, half_bins // 2, rows_local * NLON), jnp.float32),
     ]
     scratch = [pltpu.VMEM((rows, 2, 4, TILE, LANES), jnp.float32)]
-    if dependent:
-        total = operator[0].shape[1]
-        out_shape.append(pltpu.VMEM((total, total), jnp.bfloat16))
-        scratch.append(pltpu.SemaphoreType.DMA((2,)))
     return pl.pallas_call(
         functools.partial(stencil_kernel, sizes),
         name="stencil_dependent" if dependent else "stencil_free",
         compiler_params=GRANT,
-        in_specs=[smem] * 2 + [vmem] * (1 + len(fields)) + [hbm] * len(operator),
+        in_specs=[smem] * 2 + [vmem] * (1 + len(fields)),
         out_specs=[vmem] * len(out_shape),
         out_shape=out_shape,
         scratch_shapes=scratch,
         cost_estimate=pl.CostEstimate(flops=cells * MAXSTEPS * 100, bytes_accessed=cells * 16, transcendentals=0),
-    )(*map(off_chip, (substeps, courant, trig)), *map(on_chip, fields), *map(off_chip, operator))
-
-
-def integrate_kernel(sizes, arrived, whole_w, out, state, driver):
+    )(*map(off_chip, (substeps, courant, trig)), *map(on_chip, fields))
+
+
+def integrate_kernel(sizes, arrived, own_w, other_w, *refs):
     bins_local, half_bins, comps = sizes
-    lat = lax.axis_index("lat")
+    outs, (held_w, state, driver, sem) = refs[:comps], refs[comps:]
+    comp, lat, sub = (lax.axis_index(name) for name in ("comp", "lat", "sub"))
     total = comps * bins_local
+    stretch = total // 2
+    pieces = 2
+    piece = stretch // pieces
+    copies = []
+    for other, source in enumerate((own_w, other_w)):
+        for p in range(pieces):
+            copy = pltpu.make_async_copy(
+                source.at[pl.ds(p * piece, piece)], held_w.at[other, pl.ds(p * piece, piece)], sem.at[other, p]
+            )
+            copy.start()
+            copies.append(copy)
     sectors = half_bins // (2 * SECTOR)
     groups = bins_local // SECTOR
     for c in range(comps):
@@ -427,22 +424,34 @@
                     block = arrived[2 * c + s, (sectors * dep + k) * SECTOR : (sectors * dep + k + 1) * SECTOR, :]
                     driver[0, row, :] = block
                     state[row, :] = block.astype(jnp.float32)
-    stretch = total // 2
     for step in range(SRC_STEPS):
         read = 0 if step == 0 else 1 + step % 2
-        for first in range(0, total, stretch):
-            at = slice(first, first + stretch)
-            drive = jnp.dot(whole_w[at, :], driver[read, :total, :], preferred_element_type=jnp.float32)
-            value = state[at, :]
-            value = value + STEP_SIZE * value * drive
-            if step + 1 < SRC_STEPS:
-                state[at, :] = value
-                driver[1 + (step + 1) % 2, at, :] = value.astype(jnp.bfloat16)
-            else:
-                out[at, :] = (value - driver[0, at, :].astype(jnp.float32)).astype(jnp.bfloat16)
-
-
-def integrate(sizes, arrived, whole_w):
+        write = 1 + (step + 1) % 2
+        parts = pieces if step == 0 else 1
+        rows = stretch // parts
+        for other in range(2):
+            for p in range(parts):
+                if step == 0:
+                    copies[other * pieces + p].wait()
+                at = pl.ds(pl.multiple_of((sub + other) % 2 * stretch + p * rows, SECTOR), rows)
+                drive = jnp.dot(
+                    held_w[other, p * rows : (p + 1) * rows, :],
+                    driver[read, :total, :],
+                    preferred_element_type=jnp.float32,
+                )
+                value = state[at, :]
+                value = value + STEP_SIZE * value * drive
+                if step + 1 < SRC_STEPS:
+                    state[at, :] = value
+                    driver[write, at, :] = value.astype(jnp.bfloat16)
+                else:
+                    driver[write, at, :] = (value - driver[0, at, :].astype(jnp.float32)).astype(jnp.bfloat16)
+    for k in range(comps):
+        at = pl.ds(pl.multiple_of((comp + k) % comps * bins_local, SECTOR), bins_local)
+        outs[k][...] = driver[write, at, :]
+
+
+def integrate(sizes, arrived, own_w, other_w):
     bins_local, half_bins, comps = sizes
     total = comps * bins_local
     vmem = pl.BlockSpec(memory_space=pltpu.VMEM)
@@ -450,21 +459,29 @@
         functools.partial(integrate_kernel, sizes),
         name="integrate",
         compiler_params=GRANT,
-        in_specs=[vmem, vmem],
-        out_specs=vmem,
-        out_shape=pltpu.VMEM((total, LANES), jnp.bfloat16),
+        in_specs=[vmem] + [pl.BlockSpec(memory_space=pl.ANY)] * 2,
+        out_specs=[vmem] * comps,
+        out_shape=[pltpu.VMEM((bins_local, LANES), jnp.bfloat16)] * comps,
         scratch_shapes=[
+            pltpu.VMEM((2,) + own_w.shape, jnp.bfloat16),
             pltpu.VMEM((total + SECTOR, LANES), jnp.float32),
             pltpu.VMEM((3, total + SECTOR, LANES), jnp.bfloat16),
+            pltpu.SemaphoreType.DMA((2, 2)),
         ],
         cost_estimate=pl.CostEstimate(
             flops=2 * SRC_STEPS * total * total * LANES, bytes_accessed=2 * total * total, transcendentals=0
         ),
-    )(on_chip(arrived), on_chip(whole_w))
-
-
-def finish_kernel(sizes, mine_free, mine_dep, got_free, got_dep, raised, sea_mask, out, whole, sem):
+    )(on_chip(arrived), off_chip(own_w), off_chip(other_w))
+
+
+def finish_kernel(sizes, *refs):
     bins_local, half_bins = sizes
+    mine_free, mine_dep, got_free, got_dep, sea_mask = refs[:5]
+    out, whole, raised, sem = refs[-4:]
+    steps_up = refs[5:-4]
+    comp = lax.axis_index("comp")
+    for k, increments in enumerate(steps_up):
+        raised[(comp + len(steps_up) - k) % len(steps_up)] = increments[...]
     _, sub, parity, _ = device_place(bins_local)
     tiles = whole.shape[1] // LANES
     sea = [
@@ -509,23 +526,24 @@
                     rows_out(group, sem.at[other, k, rest]).wait()
 
 
-def finish(sizes, mine_free, mine_dep, got_free, got_dep, raised, sea_mask):
+def finish(sizes, fields, sea_mask, steps_up):
     bins_local, half_bins = sizes
     points = sea_mask.shape[1]
     vmem = pl.BlockSpec(memory_space=pltpu.VMEM)
-    fields = [on_chip(field) for field in (mine_free, mine_dep, got_free, got_dep, raised)]
+    comps = len(steps_up)
     return pl.pallas_call(
         functools.partial(finish_kernel, sizes),
         name="finish",
         compiler_params=GRANT,
-        in_specs=[vmem] * 6,
+        in_specs=[vmem] * (5 + comps),
         out_specs=pl.BlockSpec(memory_space=pl.ANY),
         out_shape=jax.ShapeDtypeStruct((bins_local, points), jnp.float32),
         scratch_shapes=[
             pltpu.VMEM((2 * half_bins, points), jnp.float32),
+            pltpu.VMEM((comps, bins_local, LANES), jnp.bfloat16),
             pltpu.SemaphoreType.DMA((2, half_bins // (2 * SECTOR), 2)),
         ],
-    )(*fields, sea_mask)
+    )(*map(on_chip, fields), sea_mask, *map(on_chip, steps_up))
 
 
 def on_chip(values):
@@ -555,11 +573,10 @@
     pair = swap(to_pair, 1)
     near = swap(to_near, 2)
     far = swap(to_far, 3)
+    free_start, free_field = stencil((bins_local, half_bins, rows_local, False), substeps, courant, trig, mine, pair)
+    near, far, source_operator, _ = lax.optimization_barrier((near, far, source_operator, free_start))
     other_w = swap(source_operator, 1)
-
-    free_start, free_field = stencil((bins_local, half_bins, rows_local, False), substeps, courant, trig, mine, pair)
-    near, far, _ = lax.optimization_barrier((near, far, free_start))
-    start, dep_field, whole_w = stencil(
+    start, dep_field = stencil(
         (bins_local, half_bins, rows_local, True),
         substeps,
         courant,
@@ -569,15 +586,15 @@
         near,
         far,
         free_start,
-        operator=(source_operator, other_w),
     )
     arrived = lax.all_to_all(start, ("comp", "sub"), split_axis=0, concat_axis=0, tiled=True)
     got_free = swap(free_field[1:], 1)
     got_dep = swap(dep_field[1:], 1)
-    raised = integrate((bins_local, half_bins, comps), arrived, whole_w)
-    raised = raised.reshape(comps, bins_local, LANES)
-    home = lax.all_to_all(raised, "comp", split_axis=0, concat_axis=0, tiled=True)
-    return finish((bins_local, half_bins), free_field, dep_field, got_free, got_dep, home, sea_mask)
+    raised = integrate((bins_local, half_bins, comps), arrived, source_operator, other_w)
+    home = [raised[0]] + [
+        lax.ppermute(raised[k], "comp", [(i, (i + k) % comps) for i in range(comps)]) for k in range(1, comps)
+    ]
+    return finish((bins_local, half_bins), (free_field, dep_field, got_free, got_dep), sea_mask, home)
 
 
 def device_step(*arrays):

time: 68.1 us -> 67 us (0.984)
  blocking collectives: 20.3 us -> 0 us
  waiting for transfers between devices: 16.2 us -> 26.7 us
  Pallas kernels: 19.1 us -> 27.1 us
  starting transfers between devices: 7.64 us -> 12.9 us
  local copies, waits for them, and re-layouts: 4.42 us -> 0.04 us
    all_to_all x1 -> x0, blocking collectives: 20.3 us -> none  [two_chip_device(): lax.all_to_all(start, ('comp', 'sub'), split_axis=0, concat_axis=0, tiled...]
    ppermute x0 -> x3, waiting for transfers between devices: none -> 8.17 us  [two_chip_device(): lax.ppermute(raised[k], 'comp', [(i, (i + k) % comps) for i in range(comp...]
    pallas_call x1, Pallas kernels: 9.26 us -> 15.2 us  [integrate(): pl.pallas_call(functools.partial(integrate_kernel, sizes), name='integrat...]
    unnamed x10 -> x2, local copies, waits for them, and re-layouts: 4.38 us -> 0.01 us
    ppermute x0 -> x3, starting transfers between devices: none -> 3.87 us  [two_chip_device(): lax.ppermute(raised[k], 'comp', [(i, (i + k) % comps) for i in range(comp...]
    all_to_all x1, waiting for transfers between devices: 11.7 us -> 14.6 us  [two_chip_device(): lax.all_to_all(start, ('comp', 'sub'), split_axis=0, concat_axis=0, tiled...]
    all_to_all x1, starting transfers between devices: 3.47 us -> 5.1 us  [two_chip_device(): lax.all_to_all(start, ('comp', 'sub'), split_axis=0, concat_axis=0, tiled...]
    pallas_call x1, Pallas kernels: 0.83 us -> 2.05 us  [pack(): pl.pallas_call(functools.partial(pack_kernel, sizes), name='pack', compil...]
  transfers between devices with their start and end apart: 7 -> 10, of which waited for: 6 -> 5; matrix products, arithmetic and copies ran while one was open for 0% -> 0% of each run, Pallas kernels for 6% -> 35%
where the time goes in v5:
time: 67 us; the launch traced here: 66.7 us
  Pallas kernels  27.1 us (40%)
  waiting for transfers between devices  26.7 us (40%)
  starting transfers between devices  12.9 us (19%)
    pallas_call x1, Pallas kernels, integrate(): pl.pallas_call(functools.partial(integrate_kernel, sizes), name='integrat...  15.2 us
    all_to_all x1, waiting for transfers between devices, two_chip_device(): lax.all_to_all(start, ('comp', 'sub'), split_axis=0, concat_axis=0, tiled...  14.6 us
    pallas_call x2, Pallas kernels, stencil(): pl.pallas_call(functools.partial(stencil_kernel, sizes), name='stencil_de...  8.17 us
    ppermute x3, waiting for transfers between devices, two_chip_device(): lax.ppermute(raised[k], 'comp', [(i, (i + k) % comps) for i in range(comp...  8.17 us
    all_to_all x1, starting transfers between devices, two_chip_device(): lax.all_to_all(start, ('comp', 'sub'), split_axis=0, concat_axis=0, tiled...  5.1 us
    ppermute x6, starting transfers between devices, swap(): lax.ppermute(values, ('lat', 'sub'), [(i, i ^ bits) for i in range(count)])  3.92 us
    ppermute x6, waiting for transfers between devices, swap(): lax.ppermute(values, ('lat', 'sub'), [(i, i ^ bits) for i in range(count)])  3.89 us
    ppermute x3, starting transfers between devices, two_chip_device(): lax.ppermute(raised[k], 'comp', [(i, (i + k) % comps) for i in range(comp...  3.87 us
  transfers between devices with their start and end apart: 10, of which 5 were waited for; matrix products, arithmetic and copies ran while one was open for 0% of the time, Pallas kernels for 35%

profile of v5, /device:TPU:0, one launch (start us, length us, event | category | flops | bytes accessed | tf_op | source)
XLA Modules:
  0.0 66.7 jit_solution(12909489991310767379)
XLA Ops:
  0.0 2.0 %pack.1 = (f32[264,512]{1,0:T(8,128)S(1)}, f32[264,512]{1,0:T(8,128)S(1)}, s16[136,512]{1,0:T(8,128)(2,1)S(1)}, s16[136,512]{1,0:T(8,128)(2,1)S(1)}) custom-call(f32[480,512]{1,0:T(8,128)} %spectrum.1, s32[4,512]{1,0:T(4,128)} %neighbours.1, s32[1,512]{1,0:T(1,128)} %bitcast.1), custom_call_target="tpu_custom_call" | custom-call | tf_op jit(solution)/shard_map/pack/pallas_call | solution.py:244
  2.1 0.6 collective-permute-start
  2.6 2.6 %collective-permute-start.1 = (s16[136,512]{1,0:T(8,128)(2,1)S(1)}, s16[136,512]{1,0:T(8,128)(2,1)S(1)}, u32[]{:S(2)}, u32[]{:S(2)}) collective-permute-start(s16[136,512]{1,0:T(8,128)(2,1)S(1)} %get-tuple-element.23), channel_id=1, source_target_pairs={{0,2},{1,3},{2,0},{3,1},{4,6},{5,7},{6,4},{7,5},{8,10},{9,11},{10,... | collective-permute-start | bytes 417800 | tf_op jit(solution)/shard_map/ppermute | solution.py:559
  5.2 0.0 collective-permute-start.2
  5.2 0.0 collective-permute-done.refs_4_
  5.2 3.1 %stencil_free.1 = (bf16[8,128,128]{2,1,0:T(8,128)(2,1)S(1)}, f32[2,128,512]{2,1,0:T(8,128)S(1)}) custom-call(s32[30]{0:T(128)} %refs_0_.3, f32[30]{0:T(128)} %refs_1_.3, f32[2,64,128]{2,1,0:T(8,128)} %constant.2.clone.refs_2_, f32[264,512]{1,0:T(8,128)S(1)} %get-tuple-element.20.refs_3_, f32[264,512]{1,0:T(8,128)S(1)} %collective-permute-done.refs_4_), custom_call_target="tpu_custom_call" | custom-call | flops 78643200 | bytes 2097152 | tf_op jit(solution)/shard_map/stencil_free/pallas_call | solution.py:386
  8.3 1.4 %collective-permute-done.1.refs_5_ = s16[136,512]{1,0:T(8,128)(2,1)S(1)} collective-permute-done((s16[136,512]{1,0:T(8,128)(2,1)S(1)}, s16[136,512]{1,0:T(8,128)(2,1)S(1)}, u32[]{:S(2)}, u32[]{:S(2)}) %collective-permute-start.1) | collective-permute-done | bytes 139296 | tf_op jit(solution)/shard_map/ppermute | solution.py:559
  9.7 2.5 %collective-permute-done.2.refs_6_ = s16[136,512]{1,0:T(8,128)(2,1)S(1)} collective-permute-done((s16[136,512]{1,0:T(8,128)(2,1)S(1)}, s16[136,512]{1,0:T(8,128)(2,1)S(1)}, u32[]{:S(2)}, u32[]{:S(2)}) %collective-permute-start.2) | collective-permute-done | bytes 139296 | tf_op jit(solution)/shard_map/ppermute | solution.py:559
  12.2 0.1 collective-permute-start.5
  12.3 5.1 %stencil_dependent.1 = (bf16[8,256,128]{2,1,0:T(8,128)(2,1)}, f32[2,128,512]{2,1,0:T(8,128)S(1)}) custom-call(s32[30]{0:T(128)} %refs_0_.3, f32[30]{0:T(128)} %refs_1_.3, f32[2,64,128]{2,1,0:T(8,128)} %constant.2.clone.refs_2_, f32[264,512]{1,0:T(8,128)S(1)} %get-tuple-element.20.refs_3_, f32[264,512]{1,0:T(8,128)S(1)} %collective-permute-done.refs_4_, ...), custom_call_target="tpu_custom_call" | custom-call | flops 78643200 | bytes 2097152 | tf_op jit(solution)/shard_map/stencil_dependent/pallas_call | solution.py:386
  17.4 5.1 %all-to-all-start = ((bf16[8,256,128]{2,1,0:T(8,128)(2,1)}), bf16[8,256,128]{2,1,0:T(8,128)(2,1)S(1)}, u32[]{:S(2)}, u32[]{:S(2)}) async-start(bf16[8,256,128]{2,1,0:T(8,128)(2,1)} %get-tuple-element.29), calls=%async_computation | async-start | bytes 1048576 | tf_op jit(solution)/shard_map/all_to_all | solution.py:590
  22.5 0.6 collective-permute-start.4
  23.1 0.0 copy-start
  23.1 0.1 collective-permute-start.3
  23.2 14.6 %all-to-all-done.arrived = bf16[8,256,128]{2,1,0:T(8,128)(2,1)S(1)} async-done(((bf16[8,256,128]{2,1,0:T(8,128)(2,1)}), bf16[8,256,128]{2,1,0:T(8,128)(2,1)S(1)}, u32[]{:S(2)}, u32[]{:S(2)}) %all-to-all-start) | async-done | bytes 524320 | tf_op jit(solution)/shard_map/all_to_all | solution.py:590
  37.8 0.0 collective-permute-done.5.other_w
  37.8 15.2 %integrate.1 = (bf16[480,128]{1,0:T(8,128)(2,1)S(1)}, bf16[480,128]{1,0:T(8,128)(2,1)S(1)}, bf16[480,128]{1,0:T(8,128)(2,1)S(1)}, bf16[480,128]{1,0:T(8,128)(2,1)S(1)}) custom-call(bf16[8,256,128]{2,1,0:T(8,128)(2,1)S(1)} %all-to-all-done.arrived, bf16[960,1920]{1,0:T(8,128)(2,1)} %own_w, bf16[960,1920]{1,0:T(8,128)(2,1)} %collective-permute-done.5.other_w), custom_call_target="tpu_custom_call" | custom-call | flops 3774873600 | bytes 7372800 | tf_op jit(solution)/shard_map/integrate/pallas_call | solution.py:458
  53.0 0.1 collective-permute-start.6
  53.1 1.8 %collective-permute-start.7 = (bf16[480,128]{1,0:T(8,128)(2,1)S(1)}, bf16[480,128]{1,0:T(8,128)(2,1)S(1)}, u32[]{:S(2)}, u32[]{:S(2)}) collective-permute-start(bf16[480,128]{1,0:T(8,128)(2,1)S(1)} %get-tuple-element.33), channel_id=1, source_target_pairs={{0,8},{4,12},{8,0},{12,4},{1,9},{5,13},{9,1},{13,5},{2,10},{6,14},... | collective-permute-start | bytes 368648 | tf_op jit(solution)/shard_map/ppermute | solution.py:595
  54.9 2.0 %collective-permute-start.8 = (bf16[480,128]{1,0:T(8,128)(2,1)S(1)}, bf16[480,128]{1,0:T(8,128)(2,1)S(1)}, u32[]{:S(2)}, u32[]{:S(2)}) collective-permute-start(bf16[480,128]{1,0:T(8,128)(2,1)S(1)} %get-tuple-element.34), channel_id=1, source_target_pairs={{0,12},{4,0},{8,4},{12,8},{1,13},{5,1},{9,5},{13,9},{2,14},{6,2},{... | collective-permute-start | bytes 368648 | tf_op jit(solution)/shard_map/ppermute | solution.py:595
  56.9 0.0 collective-permute-done.4.refs_3_
  56.9 0.0 collective-permute-done.3.refs_2_
  56.9 4.2 %collective-permute-done.6.refs_6_ = bf16[480,128]{1,0:T(8,128)(2,1)S(1)} collective-permute-done((bf16[480,128]{1,0:T(8,128)(2,1)S(1)}, bf16[480,128]{1,0:T(8,128)(2,1)S(1)}, u32[]{:S(2)}, u32[]{:S(2)}) %collective-permute-start.6) | collective-permute-done | bytes 122912 | tf_op jit(solution)/shard_map/ppermute | solution.py:595
  61.1 4.0 %collective-permute-done.7.refs_7_ = bf16[480,128]{1,0:T(8,128)(2,1)S(1)} collective-permute-done((bf16[480,128]{1,0:T(8,128)(2,1)S(1)}, bf16[480,128]{1,0:T(8,128)(2,1)S(1)}, u32[]{:S(2)}, u32[]{:S(2)}) %collective-permute-start.7) | collective-permute-done | bytes 122912 | tf_op jit(solution)/shard_map/ppermute | solution.py:595
  65.1 0.0 collective-permute-done.8.refs_8_
  65.1 0.0 copy-done
  65.1 1.6 %finish.1 = f32[480,512]{1,0:T(8,128)} custom-call(f32[2,128,512]{2,1,0:T(8,128)S(1)} %get-tuple-element.22.refs_0_, f32[2,128,512]{2,1,0:T(8,128)S(1)} %get-tuple-element.28.refs_1_, f32[1,128,512]{2,1,0:T(8,128)S(1)} %collective-permute-done.3.refs_2_, f32[1,128,512]{2,1,0:T(8,128)S(1)} %collective-permute-done.4.refs_3_, s32[1,512]{1,0:T(1,128)S(1)} %bitcast.2, ...), custom_call_target="tpu_custom_call" | custom-call | tf_op jit(solution)/shard_map/finish/pallas_call | solution.py:534
  (2 shorter events, 0.0 us)
Async XLA Ops:
  2.1 3.2 %collective-permute-start = (f32[264,512]{1,0:T(8,128)S(1)}, f32[264,512]{1,0:T(8,128)S(1)}, u32[]{:S(2)}, u32[]{:S(2)}) collective-permute-start(f32[264,512]{1,0:T(8,128)S(1)} %get-tuple-element.21), channel_id=1, source_target_pairs={{0,1},{1,0},{2,3},{3,2},{4,5},{5,4},{6,7},{7,6},{8,9},{9,8},{10,11... | collective-permute-start | bytes 1622024 | tf_op jit(solution)/shard_map/ppermute | solution.py:559
  2.6 7.1 %collective-permute-start.1 = (s16[136,512]{1,0:T(8,128)(2,1)S(1)}, s16[136,512]{1,0:T(8,128)(2,1)S(1)}, u32[]{:S(2)}, u32[]{:S(2)}) collective-permute-start(s16[136,512]{1,0:T(8,128)(2,1)S(1)} %get-tuple-element.23), channel_id=1, source_target_pairs={{0,2},{1,3},{2,0},{3,1},{4,6},{5,7},{6,4},{7,5},{8,10},{9,11},{10,... | collective-permute-start | bytes 417800 | tf_op jit(solution)/shard_map/ppermute | solution.py:559
  5.2 7.0 %collective-permute-start.2 = (s16[136,512]{1,0:T(8,128)(2,1)S(1)}, s16[136,512]{1,0:T(8,128)(2,1)S(1)}, u32[]{:S(2)}, u32[]{:S(2)}) collective-permute-start(s16[136,512]{1,0:T(8,128)(2,1)S(1)} %get-tuple-element.24), channel_id=1, source_target_pairs={{0,3},{1,2},{2,1},{3,0},{4,7},{5,6},{6,5},{7,4},{8,11},{9,10},{10,... | collective-permute-start | bytes 417800 | tf_op jit(solution)/shard_map/ppermute | solution.py:559
  12.2 25.7 %collective-permute-start.5 = (bf16[960,1920]{1,0:T(8,128)(2,1)}, bf16[960,1920]{1,0:T(8,128)(2,1)}, u32[]{:S(2)}, u32[]{:S(2)}) collective-permute-start(bf16[960,1920]{1,0:T(8,128)(2,1)} %own_w), channel_id=1, source_target_pairs={{0,1},{1,0},{2,3},{3,2},{4,5},{5,4},{6,7},{7,6},{8,9},{9,8},{10,11... | collective-permute-start | bytes 11059208 | tf_op jit(solution)/shard_map/ppermute | solution.py:559
  17.4 20.4 %all-to-all-start = ((bf16[8,256,128]{2,1,0:T(8,128)(2,1)}), bf16[8,256,128]{2,1,0:T(8,128)(2,1)S(1)}, u32[]{:S(2)}, u32[]{:S(2)}) async-start(bf16[8,256,128]{2,1,0:T(8,128)(2,1)} %get-tuple-element.29), calls=%async_computation | async-start | bytes 1048576 | tf_op jit(solution)/shard_map/all_to_all | solution.py:590
  22.5 34.4 %collective-permute-start.4 = (f32[1,128,512]{2,1,0:T(8,128)S(1)}, f32[1,128,512]{2,1,0:T(8,128)S(1)}, u32[]{:S(2)}, u32[]{:S(2)}) collective-permute-start(f32[1,128,512]{2,1,0:T(8,128)S(1)} %slice.7), channel_id=1, source_target_pairs={{0,1},{1,0},{2,3},{3,2},{4,5},{5,4},{6,7},{7,6},{8,9},{9,8},{10,11... | collective-permute-start | bytes 786440 | tf_op jit(solution)/shard_map/ppermute | solution.py:559
  23.1 42.0 %copy-start = (s32[512]{0:T(512)S(1)}, s32[512]{0:T(512)}, u32[]{:S(2)}) copy-start(s32[512]{0:T(512)} %param.8) | copy-start | bytes 6148
  23.1 33.8 %collective-permute-start.3 = (f32[1,128,512]{2,1,0:T(8,128)S(1)}, f32[1,128,512]{2,1,0:T(8,128)S(1)}, u32[]{:S(2)}, u32[]{:S(2)}) collective-permute-start(f32[1,128,512]{2,1,0:T(8,128)S(1)} %slice.6), channel_id=1, source_target_pairs={{0,1},{1,0},{2,3},{3,2},{4,5},{5,4},{6,7},{7,6},{8,9},{9,8},{10,11... | collective-permute-start | bytes 786440 | tf_op jit(solution)/shard_map/ppermute | solution.py:559
  53.0 8.1 %collective-permute-start.6 = (bf16[480,128]{1,0:T(8,128)(2,1)S(1)}, bf16[480,128]{1,0:T(8,128)(2,1)S(1)}, u32[]{:S(2)}, u32[]{:S(2)}) collective-permute-start(bf16[480,128]{1,0:T(8,128)(2,1)S(1)} %get-tuple-element.32), channel_id=1, source_target_pairs={{0,4},{4,8},{8,12},{12,0},{1,5},{5,9},{9,13},{13,1},{2,6},{6,10},{... | collective-permute-start | bytes 368648 | tf_op jit(solution)/shard_map/ppermute | solution.py:595
  53.1 12.0 %collective-permute-start.7 = (bf16[480,128]{1,0:T(8,128)(2,1)S(1)}, bf16[480,128]{1,0:T(8,128)(2,1)S(1)}, u32[]{:S(2)}, u32[]{:S(2)}) collective-permute-start(bf16[480,128]{1,0:T(8,128)(2,1)S(1)} %get-tuple-element.33), channel_id=1, source_target_pairs={{0,8},{4,12},{8,0},{12,4},{1,9},{5,13},{9,1},{13,5},{2,10},{6,14},... | collective-permute-start | bytes 368648 | tf_op jit(solution)/shard_map/ppermute | solution.py:595
  54.9 10.2 %collective-permute-start.8 = (bf16[480,128]{1,0:T(8,128)(2,1)S(1)}, bf16[480,128]{1,0:T(8,128)(2,1)S(1)}, u32[]{:S(2)}, u32[]{:S(2)}) collective-permute-start(bf16[480,128]{1,0:T(8,128)(2,1)S(1)} %get-tuple-element.34), channel_id=1, source_target_pairs={{0,12},{4,0},{8,4},{12,8},{1,13},{5,1},{9,5},{13,9},{2,14},{6,2},{... | collective-permute-start | bytes 368648 | tf_op jit(solution)/shard_map/ppermute | solution.py:595

commit v6 on v4

--- a/solution.py
+++ b/solution.py
@@ -8,6 +8,7 @@
 from jax.experimental import pallas as pl
 from jax.experimental.pallas import tpu as pltpu
 from jax.sharding import PartitionSpec as P
+
 
 NF = 30
 ND = 64
@@ -153,7 +154,7 @@
 QUAD = 16
 SECTOR = 32
 CODE_SCALE = 32767.5
-GRANT = pltpu.CompilerParams(vmem_limit_bytes=12 << 20)
+GRANT = pltpu.CompilerParams(vmem_limit_bytes=16 << 20)
 
 
 def lane_pick(values, index):
@@ -181,10 +182,6 @@
 
 def encode(values):
     return ((values * CODE_SCALE + 0.5).astype(jnp.int32) - 32768).astype(jnp.int16)
-
-
-def decode(values):
-    return (values.astype(jnp.int32) + 32768).astype(jnp.float32) * (1.0 / CODE_SCALE)
 
 
 def device_place(bins_local):
@@ -238,7 +235,7 @@
 
 
 def pack(sizes, spectrum, neighbours, sea_mask):
-    bins_local, half_bins, rows_local = sizes
+    _, half_bins, rows_local = sizes
     points = rows_local * NLON
     vmem = pl.BlockSpec(memory_space=pltpu.VMEM)
     return pl.pallas_call(
@@ -249,13 +246,13 @@
         out_specs=[vmem] * 4,
         out_shape=[pltpu.VMEM((half_bins + TILE, points), jnp.float32)] * 2
         + [pltpu.VMEM((half_bins // 2 + TILE, points), jnp.int16)] * 2,
-    )(spectrum, neighbours, sea_mask)
+    )(*map(off_chip, (spectrum, neighbours, sea_mask)))
 
 
 def stencil_kernel(sizes, *refs):
     bins_local, half_bins, rows_local, dependent = sizes
     if dependent:
-        (steps_ref, courant_ref, trig, mine, pair, near, far, free_start, own_w, other_w) = refs[:10]
+        steps_ref, courant_ref, trig, mine, pair, near, far, free_start, other_w, own_w = refs[:10]
         start_out, field_out, whole_w, tab, sem = refs[10:]
     else:
         steps_ref, courant_ref, trig, mine, pair, start_out, field_out, tab = refs
@@ -264,18 +261,15 @@
     first_group = first_group + sub * (half_bins // SECTOR)
     chip_rows = 2 * rows_local
     halo = chip_rows if dependent else 0
-    sent_first = 0
     copies = []
+    sent_first = half_bins // 2 if dependent else 0
     if dependent:
-        w_rows = own_w.shape[0]
+        for b in range(start_out.shape[0]):
+            start_out[b, :sent_first, :] = free_start[b]
         for other, source in enumerate((own_w, other_w)):
-            at = pl.ds(pl.multiple_of((sub + other) % 2 * w_rows, 64), w_rows)
-            copy = pltpu.make_async_copy(source, whole_w.at[at], sem.at[other])
-            copy.start()
-            copies.append(copy)
-        sent_first = half_bins // 2
-        for block in range(start_out.shape[0]):
-            start_out[block, :sent_first, :] = free_start[block]
+            at = pl.ds(pl.multiple_of((sub + other) % 2 * source.shape[0], 64), source.shape[0])
+            copies.append(pltpu.make_async_copy(source, whole_w.at[at], sem.at[other]))
+            copies[other].start()
     north = lat == (0 if dependent else 1)
     flip = north.astype(jnp.int32)
 
@@ -289,7 +283,7 @@
         return pl.ds(pl.multiple_of(local * NLON + half * LANES, LANES), LANES)
 
     for u in range(halo + chip_rows):
-        core, local, here = where_is(u % chip_rows)
+        _, local, here = where_is(u % chip_rows)
         for half in range(2):
             at = lanes_of(local, half)
             if u < halo:
@@ -380,39 +374,41 @@
         copy.wait()
 
 
-def stencil(sizes, substeps, courant, trig, *fields, operator=()):
-    bins_local, half_bins, rows_local, dependent = sizes
+def stencil(sizes, substeps, courant, trig, *fields, operator=None):
+    _, half_bins, rows_local, dependent = sizes
     blocks = 4 * rows_local
     rows = (4 if dependent else 2) * rows_local
     smem = pl.BlockSpec(memory_space=pltpu.SMEM)
     vmem = pl.BlockSpec(memory_space=pltpu.VMEM)
-    hbm = pl.BlockSpec(memory_space=pl.ANY)
     cells = half_bins // 2 * rows_local * 2 * NLON
-    start_bins = half_bins if dependent else half_bins // 2
+    in_specs = [smem] * 2 + [vmem] * (1 + len(fields))
     out_shape = [
-        pltpu.VMEM((blocks, start_bins, LANES), jnp.bfloat16),
+        pltpu.VMEM((blocks, half_bins // (1 if dependent else 2), LANES), jnp.bfloat16),
         pltpu.VMEM((2, half_bins // 2, rows_local * NLON), jnp.float32),
     ]
     scratch = [pltpu.VMEM((rows, 2, 4, TILE, LANES), jnp.float32)]
+    args = list(map(off_chip, (substeps, courant, trig))) + list(map(on_chip, fields))
     if dependent:
-        total = operator[0].shape[1]
-        out_shape.append(pltpu.VMEM((total, total), jnp.bfloat16))
+        in_specs.append(pl.BlockSpec(memory_space=pl.ANY))
+        args.append(off_chip(operator))
+        out_shape.append(pltpu.VMEM((2 * operator.shape[0], operator.shape[1]), jnp.bfloat16))
         scratch.append(pltpu.SemaphoreType.DMA((2,)))
     return pl.pallas_call(
         functools.partial(stencil_kernel, sizes),
         name="stencil_dependent" if dependent else "stencil_free",
         compiler_params=GRANT,
-        in_specs=[smem] * 2 + [vmem] * (1 + len(fields)) + [hbm] * len(operator),
+        in_specs=in_specs,
         out_specs=[vmem] * len(out_shape),
         out_shape=out_shape,
         scratch_shapes=scratch,
         cost_estimate=pl.CostEstimate(flops=cells * MAXSTEPS * 100, bytes_accessed=cells * 16, transcendentals=0),
-    )(*map(off_chip, (substeps, courant, trig)), *map(on_chip, fields), *map(off_chip, operator))
-
-
-def integrate_kernel(sizes, arrived, whole_w, out, state, driver):
+    )(*args)
+
+
+def integrate_kernel(sizes, arrived, whole_w, *refs):
     bins_local, half_bins, comps = sizes
-    lat = lax.axis_index("lat")
+    outs, (state, driver) = refs[:comps], refs[comps:]
+    comp, lat = lax.axis_index("comp"), lax.axis_index("lat")
     total = comps * bins_local
     sectors = half_bins // (2 * SECTOR)
     groups = bins_local // SECTOR
@@ -430,6 +426,7 @@
     stretch = total // 2
     for step in range(SRC_STEPS):
         read = 0 if step == 0 else 1 + step % 2
+        write = 1 + (step + 1) % 2
         for first in range(0, total, stretch):
             at = slice(first, first + stretch)
             drive = jnp.dot(whole_w[at, :], driver[read, :total, :], preferred_element_type=jnp.float32)
@@ -437,22 +434,25 @@
             value = value + STEP_SIZE * value * drive
             if step + 1 < SRC_STEPS:
                 state[at, :] = value
-                driver[1 + (step + 1) % 2, at, :] = value.astype(jnp.bfloat16)
+                driver[write, at, :] = value.astype(jnp.bfloat16)
             else:
-                out[at, :] = (value - driver[0, at, :].astype(jnp.float32)).astype(jnp.bfloat16)
+                driver[write, at, :] = (value - driver[0, at, :].astype(jnp.float32)).astype(jnp.bfloat16)
+    for k in range(comps):
+        at = pl.ds(pl.multiple_of((comp + k) % comps * bins_local, SECTOR), bins_local)
+        outs[k][...] = driver[write, at, :]
 
 
 def integrate(sizes, arrived, whole_w):
-    bins_local, half_bins, comps = sizes
+    bins_local, _, comps = sizes
     total = comps * bins_local
     vmem = pl.BlockSpec(memory_space=pltpu.VMEM)
     return pl.pallas_call(
         functools.partial(integrate_kernel, sizes),
         name="integrate",
         compiler_params=GRANT,
-        in_specs=[vmem, vmem],
-        out_specs=vmem,
-        out_shape=pltpu.VMEM((total, LANES), jnp.bfloat16),
+        in_specs=[vmem] * 2,
+        out_specs=[vmem] * comps,
+        out_shape=[pltpu.VMEM((bins_local, LANES), jnp.bfloat16)] * comps,
         scratch_shapes=[
             pltpu.VMEM((total + SECTOR, LANES), jnp.float32),
             pltpu.VMEM((3, total + SECTOR, LANES), jnp.bfloat16),
@@ -463,8 +463,14 @@
     )(on_chip(arrived), on_chip(whole_w))
 
 
-def finish_kernel(sizes, mine_free, mine_dep, got_free, got_dep, raised, sea_mask, out, whole, sem):
+def finish_kernel(sizes, *refs):
     bins_local, half_bins = sizes
+    mine_free, mine_dep, got_free, got_dep, sea_mask = refs[:5]
+    out, whole, raised, sem = refs[-4:]
+    steps_up = refs[5:-4]
+    comp = lax.axis_index("comp")
+    for k, increments in enumerate(steps_up):
+        raised[(comp + len(steps_up) - k) % len(steps_up)] = increments[...]
     _, sub, parity, _ = device_place(bins_local)
     tiles = whole.shape[1] // LANES
     sea = [
@@ -509,23 +515,24 @@
                     rows_out(group, sem.at[other, k, rest]).wait()
 
 
-def finish(sizes, mine_free, mine_dep, got_free, got_dep, raised, sea_mask):
+def finish(sizes, fields, sea_mask, steps_up):
     bins_local, half_bins = sizes
     points = sea_mask.shape[1]
     vmem = pl.BlockSpec(memory_space=pltpu.VMEM)
-    fields = [on_chip(field) for field in (mine_free, mine_dep, got_free, got_dep, raised)]
+    comps = len(steps_up)
     return pl.pallas_call(
         functools.partial(finish_kernel, sizes),
         name="finish",
         compiler_params=GRANT,
-        in_specs=[vmem] * 6,
+        in_specs=[vmem] * (5 + comps),
         out_specs=pl.BlockSpec(memory_space=pl.ANY),
         out_shape=jax.ShapeDtypeStruct((bins_local, points), jnp.float32),
         scratch_shapes=[
             pltpu.VMEM((2 * half_bins, points), jnp.float32),
+            pltpu.VMEM((comps, bins_local, LANES), jnp.bfloat16),
             pltpu.SemaphoreType.DMA((2, half_bins // (2 * SECTOR), 2)),
         ],
-    )(*fields, sea_mask)
+    )(*map(on_chip, fields), sea_mask, *map(on_chip, steps_up))
 
 
 def on_chip(values):
@@ -555,10 +562,11 @@
     pair = swap(to_pair, 1)
     near = swap(to_near, 2)
     far = swap(to_far, 3)
+    source_operator, mine = lax.optimization_barrier((source_operator, mine))
     other_w = swap(source_operator, 1)
 
     free_start, free_field = stencil((bins_local, half_bins, rows_local, False), substeps, courant, trig, mine, pair)
-    near, far, _ = lax.optimization_barrier((near, far, free_start))
+    near, far, other_w, free_start = lax.optimization_barrier((near, far, other_w, free_start))
     start, dep_field, whole_w = stencil(
         (bins_local, half_bins, rows_local, True),
         substeps,
@@ -569,15 +577,18 @@
         near,
         far,
         free_start,
-        operator=(source_operator, other_w),
+        other_w,
+        operator=source_operator,
     )
     arrived = lax.all_to_all(start, ("comp", "sub"), split_axis=0, concat_axis=0, tiled=True)
+    raised = integrate((bins_local, half_bins, comps), arrived, whole_w)
+    free_field, dep_field, raised = lax.optimization_barrier((free_field, dep_field, raised))
+    home = [raised[0]] + [
+        lax.ppermute(raised[k], "comp", [(i, (i + k) % comps) for i in range(comps)]) for k in range(1, comps)
+    ]
     got_free = swap(free_field[1:], 1)
     got_dep = swap(dep_field[1:], 1)
-    raised = integrate((bins_local, half_bins, comps), arrived, whole_w)
-    raised = raised.reshape(comps, bins_local, LANES)
-    home = lax.all_to_all(raised, "comp", split_axis=0, concat_axis=0, tiled=True)
-    return finish((bins_local, half_bins), free_field, dep_field, got_free, got_dep, home, sea_mask)
+    return finish((bins_local, half_bins), (free_field, dep_field, got_free, got_dep), sea_mask, home)
 
 
 def device_step(*arrays):

time: 68.1 us -> 62.2 us (0.913)
  local copies, waits for them, and re-layouts: 4.42 us -> 0.04 us
  waiting for transfers between devices: 16.2 us -> 12.6 us
  blocking collectives: 20.3 us -> 21.4 us
  Pallas kernels: 19.1 us -> 19.9 us
    all_to_all x1 -> x0, waiting for transfers between devices: 11.7 us -> none  [two_chip_device(): lax.all_to_all(raised, 'comp', split_axis=0, concat_axis=0, tiled=True)]
    ppermute x0 -> x3, waiting for transfers between devices: none -> 8.55 us  [two_chip_device(): lax.ppermute(raised[k], 'comp', [(i, (i + k) % comps) for i in range(comp...]
    unnamed x10 -> x2, local copies, waits for them, and re-layouts: 4.38 us -> 0.01 us
    ppermute x0 -> x3, starting transfers between devices: none -> 3.83 us  [two_chip_device(): lax.ppermute(raised[k], 'comp', [(i, (i + k) % comps) for i in range(comp...]
    all_to_all x1 -> x0, starting transfers between devices: 3.47 us -> none  [two_chip_device(): lax.all_to_all(raised, 'comp', split_axis=0, concat_axis=0, tiled=True)]
    pallas_call x1, Pallas kernels: 0.83 us -> 2.05 us  [pack(): pl.pallas_call(functools.partial(pack_kernel, sizes), name='pack', compil...]
    all_to_all x1, blocking collectives: 20.3 us -> 21.4 us  [two_chip_device(): lax.all_to_all(start, ('comp', 'sub'), split_axis=0, concat_axis=0, tiled...]
    pallas_call x1, Pallas kernels: 9.26 us -> 8.47 us  [integrate(): pl.pallas_call(functools.partial(integrate_kernel, sizes), name='integrat...]
  transfers between devices with their start and end apart: 7 -> 9, of which waited for: 6 -> 3; matrix products, arithmetic and copies ran while one was open for 0% -> 0% of each run, Pallas kernels for 6% -> 5%
where the time goes in v6:
time: 62.2 us; the launch traced here: 61.9 us
  blocking collectives  21.4 us (34%)
  Pallas kernels  19.9 us (32%)
  waiting for transfers between devices  12.6 us (20%)
  starting transfers between devices  7.94 us (13%)
    all_to_all x1, blocking collectives, two_chip_device(): lax.all_to_all(start, ('comp', 'sub'), split_axis=0, concat_axis=0, tiled...  21.4 us
    ppermute x3, waiting for transfers between devices, two_chip_device(): lax.ppermute(raised[k], 'comp', [(i, (i + k) % comps) for i in range(comp...  8.55 us
    pallas_call x1, Pallas kernels, integrate(): pl.pallas_call(functools.partial(integrate_kernel, sizes), name='integrat...  8.47 us
    pallas_call x2, Pallas kernels, stencil(): pl.pallas_call(functools.partial(stencil_kernel, sizes), name='stencil_de...  7.69 us
    ppermute x6, starting transfers between devices, swap(): lax.ppermute(values, ('lat', 'sub'), [(i, i ^ bits) for i in range(count)])  4.11 us
    ppermute x6, waiting for transfers between devices, swap(): lax.ppermute(values, ('lat', 'sub'), [(i, i ^ bits) for i in range(count)])  4.07 us
    ppermute x3, starting transfers between devices, two_chip_device(): lax.ppermute(raised[k], 'comp', [(i, (i + k) % comps) for i in range(comp...  3.83 us
    pallas_call x1, Pallas kernels, pack(): pl.pallas_call(functools.partial(pack_kernel, sizes), name='pack', compil...  2.05 us
  transfers between devices with their start and end apart: 9, of which 3 were waited for; matrix products, arithmetic and copies ran while one was open for 0% of the time, Pallas kernels for 5%

profile of v6, /device:TPU:0, one launch (start us, length us, event | category | flops | bytes accessed | tf_op | source)
XLA Modules:
  0.0 61.9 jit_solution(4019836494547984150)
XLA Ops:
  0.0 2.0 %pack.1 = (f32[264,512]{1,0:T(8,128)S(1)}, f32[264,512]{1,0:T(8,128)S(1)}, s16[136,512]{1,0:T(8,128)(2,1)S(1)}, s16[136,512]{1,0:T(8,128)(2,1)S(1)}) custom-call(f32[480,512]{1,0:T(8,128)} %spectrum.1, s32[4,512]{1,0:T(4,128)} %neighbours.1, s32[1,512]{1,0:T(1,128)} %bitcast.1), custom_call_target="tpu_custom_call" | custom-call | tf_op jit(solution)/shard_map/pack/pallas_call | solution.py:241
  2.1 0.6 collective-permute-start.3
  2.6 0.1 collective-permute-start
  2.7 2.9 %collective-permute-start.1 = (s16[136,512]{1,0:T(8,128)(2,1)S(1)}, s16[136,512]{1,0:T(8,128)(2,1)S(1)}, u32[]{:S(2)}, u32[]{:S(2)}) collective-permute-start(s16[136,512]{1,0:T(8,128)(2,1)S(1)} %get-tuple-element.34), channel_id=1, source_target_pairs={{0,2},{1,3},{2,0},{3,1},{4,6},{5,7},{6,4},{7,5},{8,10},{9,11},{10,... | collective-permute-start | bytes 417800 | tf_op jit(solution)/shard_map/ppermute | solution.py:548
  5.6 0.0 collective-permute-start.2
  5.6 4.1 %collective-permute-done.refs_4_ = f32[264,512]{1,0:T(8,128)S(1)} collective-permute-done((f32[264,512]{1,0:T(8,128)S(1)}, f32[264,512]{1,0:T(8,128)S(1)}, u32[]{:S(2)}, u32[]{:S(2)}) %collective-permute-start) | collective-permute-done | bytes 540704 | tf_op jit(solution)/shard_map/ppermute | solution.py:548
  9.7 3.1 %stencil_free.1 = (bf16[8,128,128]{2,1,0:T(8,128)(2,1)S(1)}, f32[2,128,512]{2,1,0:T(8,128)S(1)}) custom-call(s32[30]{0:T(128)} %refs_0_.3, f32[30]{0:T(128)} %refs_1_.3, f32[2,64,128]{2,1,0:T(8,128)} %constant.2.clone.refs_2_, f32[264,512]{1,0:T(8,128)S(1)} %get-tuple-element.31.refs_3_, f32[264,512]{1,0:T(8,128)S(1)} %collective-permute-done.refs_4_), custom_call_target="tpu_custom_call" | custom-call | flops 78643200 | bytes 2097152 | tf_op jit(solution)/shard_map/stencil_free/pallas_call | solution.py:396
  12.7 0.0 collective-permute-done.1.refs_5_
  12.7 0.0 collective-permute-done.2.refs_6_
  12.7 0.0 collective-permute-done.3.refs_8_
  12.8 4.6 %stencil_dependent.1 = (bf16[8,256,128]{2,1,0:T(8,128)(2,1)S(1)}, f32[2,128,512]{2,1,0:T(8,128)S(1)}, bf16[1920,1920]{1,0:T(8,128)(2,1)S(1)}) custom-call(s32[30]{0:T(128)} %refs_0_.3, f32[30]{0:T(128)} %refs_1_.3, f32[2,64,128]{2,1,0:T(8,128)} %constant.2.clone.refs_2_, f32[264,512]{1,0:T(8,128)S(1)} %get-tuple-element.31.refs_3_, ...), custom_call_target="tpu_custom_call" | custom-call | flops 78643200 | bytes 2097152 | tf_op jit(solution)/shard_map/stencil_dependent/pallas_call | solution.py:396
  17.4 21.4 %all_to_all.5.arrived = bf16[8,256,128]{2,1,0:T(8,128)(2,1)S(1)} all-to-all(bf16[8,256,128]{2,1,0:T(8,128)(2,1)S(1)} %get-tuple-element.43), channel_id=1, replica_groups=mesh['members'=2,'comp'=4,'lat'=2,'sub'=2] {'comp','sub'}, dimensions={0} | all-to-all | bytes 1048576 | tf_op jit(solution)/shard_map/all_to_all | solution.py:583
  38.8 0.0 copy-start
  38.8 8.5 %integrate.1 = (bf16[480,128]{1,0:T(8,128)(2,1)S(1)}, bf16[480,128]{1,0:T(8,128)(2,1)S(1)}, bf16[480,128]{1,0:T(8,128)(2,1)S(1)}, bf16[480,128]{1,0:T(8,128)(2,1)S(1)}) custom-call(bf16[8,256,128]{2,1,0:T(8,128)(2,1)S(1)} %all_to_all.5.arrived, bf16[1920,1920]{1,0:T(8,128)(2,1)S(1)} %get-tuple-element.44.whole_w), custom_call_target="tpu_custom_call" | custom-call | flops 3774873600 | bytes 7372800 | tf_op jit(solution)/shard_map/integrate/pallas_call | solution.py:449
  47.3 0.1 collective-permute-start.5
  47.4 0.5 collective-permute-start.4
  47.9 0.0 collective-permute-start.6
  47.9 1.9 %collective-permute-start.7 = (bf16[480,128]{1,0:T(8,128)(2,1)S(1)}, bf16[480,128]{1,0:T(8,128)(2,1)S(1)}, u32[]{:S(2)}, u32[]{:S(2)}) collective-permute-start(bf16[480,128]{1,0:T(8,128)(2,1)S(1)} %get-tuple-element.53), channel_id=1, source_target_pairs={{0,8},{4,12},{8,0},{12,4},{1,9},{5,13},{9,1},{13,5},{2,10},{6,14},... | collective-permute-start | bytes 368648 | tf_op jit(solution)/shard_map/ppermute | solution.py:587
  49.7 2.0 %collective-permute-start.8 = (bf16[480,128]{1,0:T(8,128)(2,1)S(1)}, bf16[480,128]{1,0:T(8,128)(2,1)S(1)}, u32[]{:S(2)}, u32[]{:S(2)}) collective-permute-start(bf16[480,128]{1,0:T(8,128)(2,1)S(1)} %get-tuple-element.54), channel_id=1, source_target_pairs={{0,12},{4,0},{8,4},{12,8},{1,13},{5,1},{9,5},{13,9},{2,14},{6,2},{... | collective-permute-start | bytes 368648 | tf_op jit(solution)/shard_map/ppermute | solution.py:587
  51.7 4.3 %collective-permute-done.6.refs_6_ = bf16[480,128]{1,0:T(8,128)(2,1)S(1)} collective-permute-done((bf16[480,128]{1,0:T(8,128)(2,1)S(1)}, bf16[480,128]{1,0:T(8,128)(2,1)S(1)}, u32[]{:S(2)}, u32[]{:S(2)}) %collective-permute-start.6) | collective-permute-done | bytes 122912 | tf_op jit(solution)/shard_map/ppermute | solution.py:587
  56.0 4.3 %collective-permute-done.7.refs_7_ = bf16[480,128]{1,0:T(8,128)(2,1)S(1)} collective-permute-done((bf16[480,128]{1,0:T(8,128)(2,1)S(1)}, bf16[480,128]{1,0:T(8,128)(2,1)S(1)}, u32[]{:S(2)}, u32[]{:S(2)}) %collective-permute-start.7) | collective-permute-done | bytes 122912 | tf_op jit(solution)/shard_map/ppermute | solution.py:587
  60.2 0.0 collective-permute-done.8.refs_8_
  60.2 0.0 collective-permute-done.5.refs_3_
  60.2 0.0 collective-permute-done.4.refs_2_
  60.3 0.0 copy-done
  60.3 1.6 %finish.1 = f32[480,512]{1,0:T(8,128)} custom-call(f32[2,128,512]{2,1,0:T(8,128)S(1)} %get-tuple-element.49.refs_0_, f32[2,128,512]{2,1,0:T(8,128)S(1)} %get-tuple-element.50.refs_1_, f32[1,128,512]{2,1,0:T(8,128)S(1)} %collective-permute-done.4.refs_2_, f32[1,128,512]{2,1,0:T(8,128)S(1)} %collective-permute-done.5.refs_3_, s32[1,512]{1,0:T(1,128)S(1)} %bitcast.2, ...), custom_call_target="tpu_custom_call" | custom-call | tf_op jit(solution)/shard_map/finish/pallas_call | solution.py:523
  (2 shorter events, 0.0 us)
Async XLA Ops:
  2.1 10.7 %collective-permute-start.3 = (bf16[960,1920]{1,0:T(8,128)(2,1)}, bf16[960,1920]{1,0:T(8,128)(2,1)S(1)}, u32[]{:S(2)}, u32[]{:S(2)}) collective-permute-start(bf16[960,1920]{1,0:T(8,128)(2,1)} %refs_9_), channel_id=1, source_target_pairs={{0,1},{1,0},{2,3},{3,2},{4,5},{5,4},{6,7},{7,6},{8,9},{9,8},{10,11... | collective-permute-start | bytes 11059208 | tf_op jit(solution)/shard_map/ppermute | solution.py:548
  2.6 7.0 %collective-permute-start = (f32[264,512]{1,0:T(8,128)S(1)}, f32[264,512]{1,0:T(8,128)S(1)}, u32[]{:S(2)}, u32[]{:S(2)}) collective-permute-start(f32[264,512]{1,0:T(8,128)S(1)} %get-tuple-element.32), channel_id=1, source_target_pairs={{0,1},{1,0},{2,3},{3,2},{4,5},{5,4},{6,7},{7,6},{8,9},{9,8},{10,11... | collective-permute-start | bytes 1622024 | tf_op jit(solution)/shard_map/ppermute | solution.py:548
  2.7 10.0 %collective-permute-start.1 = (s16[136,512]{1,0:T(8,128)(2,1)S(1)}, s16[136,512]{1,0:T(8,128)(2,1)S(1)}, u32[]{:S(2)}, u32[]{:S(2)}) collective-permute-start(s16[136,512]{1,0:T(8,128)(2,1)S(1)} %get-tuple-element.34), channel_id=1, source_target_pairs={{0,2},{1,3},{2,0},{3,1},{4,6},{5,7},{6,4},{7,5},{8,10},{9,11},{10,... | collective-permute-start | bytes 417800 | tf_op jit(solution)/shard_map/ppermute | solution.py:548
  5.6 7.1 %collective-permute-start.2 = (s16[136,512]{1,0:T(8,128)(2,1)S(1)}, s16[136,512]{1,0:T(8,128)(2,1)S(1)}, u32[]{:S(2)}, u32[]{:S(2)}) collective-permute-start(s16[136,512]{1,0:T(8,128)(2,1)S(1)} %get-tuple-element.35), channel_id=1, source_target_pairs={{0,3},{1,2},{2,1},{3,0},{4,7},{5,6},{6,5},{7,4},{8,11},{9,10},{10,... | collective-permute-start | bytes 417800 | tf_op jit(solution)/shard_map/ppermute | solution.py:548
  38.8 21.5 %copy-start = (s32[512]{0:T(512)S(1)}, s32[512]{0:T(512)}, u32[]{:S(2)}) copy-start(s32[512]{0:T(512)} %param.8) | copy-start | bytes 6148
  47.3 13.0 %collective-permute-start.5 = (f32[1,128,512]{2,1,0:T(8,128)S(1)}, f32[1,128,512]{2,1,0:T(8,128)S(1)}, u32[]{:S(2)}, u32[]{:S(2)}) collective-permute-start(f32[1,128,512]{2,1,0:T(8,128)S(1)} %slice.7), channel_id=1, source_target_pairs={{0,1},{1,0},{2,3},{3,2},{4,5},{5,4},{6,7},{7,6},{8,9},{9,8},{10,11... | collective-permute-start | bytes 786440 | tf_op jit(solution)/shard_map/ppermute | solution.py:548
  47.4 12.9 %collective-permute-start.4 = (f32[1,128,512]{2,1,0:T(8,128)S(1)}, f32[1,128,512]{2,1,0:T(8,128)S(1)}, u32[]{:S(2)}, u32[]{:S(2)}) collective-permute-start(f32[1,128,512]{2,1,0:T(8,128)S(1)} %slice.6), channel_id=1, source_target_pairs={{0,1},{1,0},{2,3},{3,2},{4,5},{5,4},{6,7},{7,6},{8,9},{9,8},{10,11... | collective-permute-start | bytes 786440 | tf_op jit(solution)/shard_map/ppermute | solution.py:548
  47.9 8.1 %collective-permute-start.6 = (bf16[480,128]{1,0:T(8,128)(2,1)S(1)}, bf16[480,128]{1,0:T(8,128)(2,1)S(1)}, u32[]{:S(2)}, u32[]{:S(2)}) collective-permute-start(bf16[480,128]{1,0:T(8,128)(2,1)S(1)} %get-tuple-element.52), channel_id=1, source_target_pairs={{0,4},{4,8},{8,12},{12,0},{1,5},{5,9},{9,13},{13,1},{2,6},{6,10},{... | collective-permute-start | bytes 368648 | tf_op jit(solution)/shard_map/ppermute | solution.py:587
  47.9 12.4 %collective-permute-start.7 = (bf16[480,128]{1,0:T(8,128)(2,1)S(1)}, bf16[480,128]{1,0:T(8,128)(2,1)S(1)}, u32[]{:S(2)}, u32[]{:S(2)}) collective-permute-start(bf16[480,128]{1,0:T(8,128)(2,1)S(1)} %get-tuple-element.53), channel_id=1, source_target_pairs={{0,8},{4,12},{8,0},{12,4},{1,9},{5,13},{9,1},{13,5},{2,10},{6,14},... | collective-permute-start | bytes 368648 | tf_op jit(solution)/shard_map/ppermute | solution.py:587
  49.7 10.5 %collective-permute-start.8 = (bf16[480,128]{1,0:T(8,128)(2,1)S(1)}, bf16[480,128]{1,0:T(8,128)(2,1)S(1)}, u32[]{:S(2)}, u32[]{:S(2)}) collective-permute-start(bf16[480,128]{1,0:T(8,128)(2,1)S(1)} %get-tuple-element.54), channel_id=1, source_target_pairs={{0,12},{4,0},{8,4},{12,8},{1,13},{5,1},{9,5},{13,9},{2,14},{6,2},{... | collective-permute-start | bytes 368648 | tf_op jit(solution)/shard_map/ppermute | solution.py:587

commit v7 on v6

--- a/solution.py
+++ b/solution.py
@@ -252,20 +252,18 @@
 def stencil_kernel(sizes, *refs):
     bins_local, half_bins, rows_local, dependent = sizes
     if dependent:
-        steps_ref, courant_ref, trig, mine, pair, near, far, free_start, other_w, own_w = refs[:10]
-        start_out, field_out, whole_w, tab, sem = refs[10:]
+        steps_ref, courant_ref, trig, mine, pair, near, far, kept, crossed, other_w, own_w = refs[:11]
+        passed, field_out, whole_w = refs[11:14]
+        sent, (tab, begun, sem) = refs[14:-3], refs[-3:]
     else:
-        steps_ref, courant_ref, trig, mine, pair, start_out, field_out, tab = refs
+        steps_ref, courant_ref, trig, mine, pair, kept, passed, field_out, tab, begun = refs
     lat, sub, parity, first_group = device_place(bins_local)
     parity = (parity + int(dependent)) % 2
     first_group = first_group + sub * (half_bins // SECTOR)
     chip_rows = 2 * rows_local
     halo = chip_rows if dependent else 0
     copies = []
-    sent_first = half_bins // 2 if dependent else 0
     if dependent:
-        for b in range(start_out.shape[0]):
-            start_out[b, :sent_first, :] = free_start[b]
         for other, source in enumerate((own_w, other_w)):
             at = pl.ds(pl.multiple_of((sub + other) % 2 * source.shape[0], 64), source.shape[0])
             copies.append(pltpu.make_async_copy(source, whole_w.at[at], sem.at[other]))
@@ -313,7 +311,6 @@
         trig_row = pl.ds(pl.multiple_of(SECTOR * flip + QUAD * side, QUAD), QUAD)
         part_row = pl.ds(pl.multiple_of(group * SECTOR + side * QUAD, QUAD), QUAD)
         sent_row = pl.ds(pl.multiple_of(sector * SECTOR + side * QUAD, QUAD), QUAD)
-        start_row = pl.ds(pl.multiple_of(sent_first + sector * SECTOR + side * QUAD, QUAD), QUAD)
         trig_x, trig_y = tiles(trig[0, trig_row, :]), tiles(trig[1, trig_row, :])
         field = []
         for u in range(halo + chip_rows):
@@ -361,8 +358,9 @@
             core, local, here = where_is(v)
             for half in range(2):
                 value = field[halo + v][half].reshape(QUAD, LANES)
-                start_out[(local * 2 + half) * 2 + core, start_row, :] = value.astype(jnp.bfloat16)
-                field_out[1 - here.astype(jnp.int32), sent_row, lanes_of(local, half)] = value
+                other = 1 - here.astype(jnp.int32)
+                begun[other, local * 2 + half, sent_row, :] = value.astype(jnp.bfloat16)
+                field_out[other, sent_row, lanes_of(local, half)] = value
 
     def both_sides(sector, carry):
         block(sector, 0)
@@ -370,28 +368,43 @@
         return carry
 
     lax.fori_loop(0, half_bins // (2 * SECTOR), both_sides, 0)
+    quarters = begun.shape[1]
+    if dependent:
+        third = half_bins // 2
+        for k in range(quarters):
+            quarter = (lax.axis_index("comp") + k) % quarters
+            sent[k][:third] = kept[quarter]
+            sent[k][third : 2 * third] = crossed[quarter]
+            sent[k][2 * third :] = begun[0, quarter]
+            passed[k] = begun[1, quarter]
+    else:
+        kept[...] = begun[0]
+        passed[...] = begun[1]
     for copy in copies:
         copy.wait()
 
 
 def stencil(sizes, substeps, courant, trig, *fields, operator=None):
     _, half_bins, rows_local, dependent = sizes
-    blocks = 4 * rows_local
+    quarters = 2 * rows_local
     rows = (4 if dependent else 2) * rows_local
     smem = pl.BlockSpec(memory_space=pltpu.SMEM)
     vmem = pl.BlockSpec(memory_space=pltpu.VMEM)
     cells = half_bins // 2 * rows_local * 2 * NLON
     in_specs = [smem] * 2 + [vmem] * (1 + len(fields))
-    out_shape = [
-        pltpu.VMEM((blocks, half_bins // (1 if dependent else 2), LANES), jnp.bfloat16),
-        pltpu.VMEM((2, half_bins // 2, rows_local * NLON), jnp.float32),
+    states = pltpu.VMEM((quarters, half_bins // 2, LANES), jnp.bfloat16)
+    field = pltpu.VMEM((2, half_bins // 2, rows_local * NLON), jnp.float32)
+    scratch = [
+        pltpu.VMEM((rows, 2, 4, TILE, LANES), jnp.float32),
+        pltpu.VMEM((2, quarters, half_bins // 2, LANES), jnp.bfloat16),
     ]
-    scratch = [pltpu.VMEM((rows, 2, 4, TILE, LANES), jnp.float32)]
     args = list(map(off_chip, (substeps, courant, trig))) + list(map(on_chip, fields))
+    out_shape = [states, states, field]
     if dependent:
         in_specs.append(pl.BlockSpec(memory_space=pl.ANY))
         args.append(off_chip(operator))
-        out_shape.append(pltpu.VMEM((2 * operator.shape[0], operator.shape[1]), jnp.bfloat16))
+        out_shape = [states, field, pltpu.VMEM((2 * operator.shape[0], operator.shape[1]), jnp.bfloat16)]
+        out_shape += [pltpu.VMEM((half_bins // 2 * 3, LANES), jnp.bfloat16)] * quarters
         scratch.append(pltpu.SemaphoreType.DMA((2,)))
     return pl.pallas_call(
         functools.partial(stencil_kernel, sizes),
@@ -405,24 +418,32 @@
     )(*args)
 
 
-def integrate_kernel(sizes, arrived, whole_w, *refs):
+def integrate_kernel(sizes, whole_w, *refs):
     bins_local, half_bins, comps = sizes
-    outs, (state, driver) = refs[:comps], refs[comps:]
-    comp, lat = lax.axis_index("comp"), lax.axis_index("lat")
+    large, passed, small = refs[:comps], refs[comps], refs[comps + 1 : 2 * comps]
+    outs, (state, driver) = refs[2 * comps : 3 * comps], refs[3 * comps :]
+    comp, lat, sub = (lax.axis_index(name) for name in ("comp", "lat", "sub"))
     total = comps * bins_local
     sectors = half_bins // (2 * SECTOR)
     groups = bins_local // SECTOR
-    for c in range(comps):
-        first = (c * groups) % 2
-        for s in range(2):
-            for k in range(sectors):
-                for dep in range(2):
-                    parity = (first + lat + dep) % 2
-                    row = c * bins_local + s * half_bins + (2 * k + parity) * SECTOR
-                    row = pl.ds(pl.multiple_of(row, SECTOR), SECTOR)
-                    block = arrived[2 * c + s, (sectors * dep + k) * SECTOR : (sectors * dep + k + 1) * SECTOR, :]
-                    driver[0, row, :] = block
-                    state[row, :] = block.astype(jnp.float32)
+    third = half_bins // 2
+    for k in range(comps):
+        source = (comp + comps - k) % comps
+        free = (source * groups + lat) % 2
+        parts = (
+            (large[k], 0, 0, 0),
+            (large[k], third, 1, 0),
+            (large[k], 2 * third, 0, 1),
+            (small[k - 1] if k else passed.at[0], 0, 1, 1),
+        )
+        for blocks, first, other, dep in parts:
+            for sector in range(sectors):
+                local = (sub + other) % 2 * half_bins + (2 * sector + (free + dep) % 2) * SECTOR
+                row = jnp.where(local < bins_local, source * bins_local + local, total)
+                row = pl.ds(pl.multiple_of(row, SECTOR), SECTOR)
+                block = blocks[first + sector * SECTOR : first + (sector + 1) * SECTOR, :]
+                driver[0, row, :] = block
+                state[row, :] = block.astype(jnp.float32)
     stretch = total // 2
     for step in range(SRC_STEPS):
         read = 0 if step == 0 else 1 + step % 2
@@ -442,7 +463,7 @@
         outs[k][...] = driver[write, at, :]
 
 
-def integrate(sizes, arrived, whole_w):
+def integrate(sizes, whole_w, large, passed, small):
     bins_local, _, comps = sizes
     total = comps * bins_local
     vmem = pl.BlockSpec(memory_space=pltpu.VMEM)
@@ -450,7 +471,7 @@
         functools.partial(integrate_kernel, sizes),
         name="integrate",
         compiler_params=GRANT,
-        in_specs=[vmem] * 2,
+        in_specs=[vmem] * (1 + 2 * comps),
         out_specs=[vmem] * comps,
         out_shape=[pltpu.VMEM((bins_local, LANES), jnp.bfloat16)] * comps,
         scratch_shapes=[
@@ -460,7 +481,7 @@
         cost_estimate=pl.CostEstimate(
             flops=2 * SRC_STEPS * total * total * LANES, bytes_accessed=2 * total * total, transcendentals=0
         ),
-    )(on_chip(arrived), on_chip(whole_w))
+    )(*map(on_chip, (whole_w, *large, passed, *small)))
 
 
 def finish_kernel(sizes, *refs):
@@ -558,16 +579,17 @@
     trig = np.abs(np.stack([np.cos(angles), np.sin(angles)])).astype(np.float32)
     trig = jnp.asarray(np.repeat(trig[:, :, None], LANES, axis=2))
 
-    mine, to_pair, to_near, to_far = pack((bins_local, half_bins, rows_local), spectrum, neighbours, sea_mask)
+    other_w = swap(source_operator, 1)
+    mine, to_pair, to_near, to_far = pack(
+        (bins_local, half_bins, rows_local), spectrum, neighbours, sea_mask
+    )
     pair = swap(to_pair, 1)
     near = swap(to_near, 2)
     far = swap(to_far, 3)
-    source_operator, mine = lax.optimization_barrier((source_operator, mine))
-    other_w = swap(source_operator, 1)
-
-    free_start, free_field = stencil((bins_local, half_bins, rows_local, False), substeps, courant, trig, mine, pair)
-    near, far, other_w, free_start = lax.optimization_barrier((near, far, other_w, free_start))
-    start, dep_field, whole_w = stencil(
+    kept, passed, free_field = stencil((bins_local, half_bins, rows_local, False), substeps, courant, trig, mine, pair)
+    crossed = swap(passed, 1)
+    near, far, other_w, crossed = lax.optimization_barrier((near, far, other_w, crossed))
+    passed, dep_field, whole_w, *sent = stencil(
         (bins_local, half_bins, rows_local, True),
         substeps,
         courant,
@@ -576,16 +598,18 @@
         pair,
         near,
         far,
-        free_start,
+        kept,
+        crossed,
         other_w,
         operator=source_operator,
     )
-    arrived = lax.all_to_all(start, ("comp", "sub"), split_axis=0, concat_axis=0, tiled=True)
-    raised = integrate((bins_local, half_bins, comps), arrived, whole_w)
+    ring = [[(i, (i + k) % comps) for i in range(comps)] for k in range(comps)]
+    passed = swap(passed, 1)
+    large = [sent[0]] + [lax.ppermute(sent[k], "comp", ring[k]) for k in range(1, comps)]
+    small = [lax.ppermute(passed[k], "comp", ring[k]) for k in range(1, comps)]
+    raised = integrate((bins_local, half_bins, comps), whole_w, large, passed, small)
     free_field, dep_field, raised = lax.optimization_barrier((free_field, dep_field, raised))
-    home = [raised[0]] + [
-        lax.ppermute(raised[k], "comp", [(i, (i + k) % comps) for i in range(comps)]) for k in range(1, comps)
-    ]
+    home = [raised[0]] + [lax.ppermute(raised[k], "comp", ring[k]) for k in range(1, comps)]
     got_free = swap(free_field[1:], 1)
     got_dep = swap(dep_field[1:], 1)
     return finish((bins_local, half_bins), (free_field, dep_field, got_free, got_dep), sea_mask, home)

time: 62.2 us -> 57.7 us (0.928)
  blocking collectives: 21.4 us -> 0 us
  starting transfers between devices: 7.94 us -> 21.9 us
  waiting for transfers between devices: 12.6 us -> 15.6 us
    all_to_all x1 -> x0, blocking collectives: 21.4 us -> none  [two_chip_device(): lax.all_to_all(start, ('comp', 'sub'), split_axis=0, concat_axis=0, tiled...]
    ppermute x3 -> x9, starting transfers between devices: 3.83 us -> 16.9 us  [the longest x3 6.64 us: two_chip_device(): lax.ppermute(sent[k], 'comp', ring[k])]
    ppermute x3 -> x9, waiting for transfers between devices: 8.55 us -> 12.7 us  [the longest x3 7.72 us: two_chip_device(): lax.ppermute(raised[k], 'comp', ring[k])]
    ppermute x6 -> x8, waiting for transfers between devices: 4.07 us -> 2.93 us  [swap(): lax.ppermute(values, ('lat', 'sub'), [(i, i ^ bits) for i in range(count)])]
    ppermute x6 -> x8, starting transfers between devices: 4.11 us -> 4.99 us  [swap(): lax.ppermute(values, ('lat', 'sub'), [(i, i ^ bits) for i in range(count)])]
  transfers between devices with their start and end apart: 9 -> 17, of which waited for: 3 -> 9; matrix products, arithmetic and copies ran while one was open for 0% -> 0% of each run, Pallas kernels for 5% -> 9%
where the time goes in v7:
time: 57.7 us; the launch traced here: 57.5 us
  starting transfers between devices  21.9 us (38%)
  Pallas kernels  19.9 us (34%)
  waiting for transfers between devices  15.6 us (27%)
    pallas_call x1, Pallas kernels, integrate(): pl.pallas_call(functools.partial(integrate_kernel, sizes), name='integrat...  8.46 us
    pallas_call x2, Pallas kernels, stencil(): pl.pallas_call(functools.partial(stencil_kernel, sizes), name='stencil_de...  7.75 us
    ppermute x3, waiting for transfers between devices, two_chip_device(): lax.ppermute(raised[k], 'comp', ring[k])  7.72 us
    ppermute x3, starting transfers between devices, two_chip_device(): lax.ppermute(sent[k], 'comp', ring[k])  6.64 us
    ppermute x3, starting transfers between devices, two_chip_device(): small = [lax.ppermute(passed[k], 'comp', ring[k]) for k in range(1, comps)]  5.58 us
    ppermute x8, starting transfers between devices, swap(): lax.ppermute(values, ('lat', 'sub'), [(i, i ^ bits) for i in range(count)])  4.99 us
    ppermute x3, starting transfers between devices, two_chip_device(): lax.ppermute(raised[k], 'comp', ring[k])  4.65 us
    ppermute x3, waiting for transfers between devices, two_chip_device(): small = [lax.ppermute(passed[k], 'comp', ring[k]) for k in range(1, comps)]  4.61 us
  transfers between devices with their start and end apart: 17, of which 9 were waited for; matrix products, arithmetic and copies ran while one was open for 0% of the time, Pallas kernels for 9%

profile of v7, /device:TPU:0, one launch (start us, length us, event | category | flops | bytes accessed | tf_op | source)
XLA Modules:
  0.0 57.5 jit_solution(4821839205591025975)
XLA Ops:
  0.0 0.5 collective-permute-start.3
  0.5 2.0 %pack.1 = (f32[264,512]{1,0:T(8,128)S(1)}, f32[264,512]{1,0:T(8,128)S(1)}, s16[136,512]{1,0:T(8,128)(2,1)S(1)}, s16[136,512]{1,0:T(8,128)(2,1)S(1)}) custom-call(f32[480,512]{1,0:T(8,128)} %spectrum.1, s32[4,512]{1,0:T(4,128)} %neighbours.1, s32[1,512]{1,0:T(1,128)} %bitcast.7), custom_call_target="tpu_custom_call" | custom-call | tf_op jit(solution)/shard_map/pack/pallas_call | solution.py:241
  2.5 0.1 collective-permute-start
  2.6 3.0 %collective-permute-start.1 = (s16[136,512]{1,0:T(8,128)(2,1)S(1)}, s16[136,512]{1,0:T(8,128)(2,1)S(1)}, u32[]{:S(2)}, u32[]{:S(2)}) collective-permute-start(s16[136,512]{1,0:T(8,128)(2,1)S(1)} %get-tuple-element.36), channel_id=1, source_target_pairs={{0,2},{1,3},{2,0},{3,1},{4,6},{5,7},{6,4},{7,5},{8,10},{9,11},{10,... | collective-permute-start | bytes 417800 | tf_op jit(solution)/shard_map/ppermute | solution.py:569
  5.6 0.0 collective-permute-start.2
  5.6 1.9 %collective-permute-done.refs_4_ = f32[264,512]{1,0:T(8,128)S(1)} collective-permute-done((f32[264,512]{1,0:T(8,128)S(1)}, f32[264,512]{1,0:T(8,128)S(1)}, u32[]{:S(2)}, u32[]{:S(2)}) %collective-permute-start) | collective-permute-done | bytes 540704 | tf_op jit(solution)/shard_map/ppermute | solution.py:569
  7.5 3.1 %stencil_free.1 = (bf16[4,128,128]{2,1,0:T(8,128)(2,1)S(1)}, bf16[4,128,128]{2,1,0:T(8,128)(2,1)S(1)}, f32[2,128,512]{2,1,0:T(8,128)S(1)}) custom-call(s32[30]{0:T(128)} %refs_0_.3, f32[30]{0:T(128)} %refs_1_.3, f32[2,64,128]{2,1,0:T(8,128)} %constant.2.clone.refs_2_, f32[264,512]{1,0:T(8,128)S(1)} %get-tuple-element.33.refs_3_, ...), custom_call_target="tpu_custom_call" | custom-call | flops 78643200 | bytes 2097152 | tf_op jit(solution)/shard_map/stencil_free/pallas_call | solution.py:409
  10.6 0.4 collective-permute-start.4
  11.1 0.0 collective-permute-done.1.refs_5_
  11.1 0.8 %collective-permute-done.2.refs_6_ = s16[136,512]{1,0:T(8,128)(2,1)S(1)} collective-permute-done((s16[136,512]{1,0:T(8,128)(2,1)S(1)}, s16[136,512]{1,0:T(8,128)(2,1)S(1)}, u32[]{:S(2)}, u32[]{:S(2)}) %collective-permute-start.2) | collective-permute-done | bytes 139296 | tf_op jit(solution)/shard_map/ppermute | solution.py:569
  11.9 0.2 collective-permute-done.4.refs_8_
  12.1 0.0 collective-permute-done.3.refs_9_
  12.1 4.7 %stencil_dependent.1 = (bf16[4,128,128]{2,1,0:T(8,128)(2,1)S(1)}, f32[2,128,512]{2,1,0:T(8,128)S(1)}, bf16[1920,1920]{1,0:T(8,128)(2,1)S(1)}, bf16[384,128]{1,0:...) custom-call(s32[30]{0:T(128)} %refs_0_.3, f32[30]{0:T(128)} %refs_1_.3, ...), custom_call_target="tpu_custom_call" | custom-call | flops 78643200 | bytes 2097152 | tf_op jit(solution)/shard_map/stencil_dependent/pallas_call | solution.py:409
  16.7 0.4 collective-permute-start.8
  17.2 2.7 %collective-permute-start.5 = (bf16[384,128]{1,0:T(8,128)(2,1)S(1)}, bf16[384,128]{1,0:T(8,128)(2,1)S(1)}, u32[]{:S(2)}, u32[]{:S(2)}) collective-permute-start(bf16[384,128]{1,0:T(8,128)(2,1)S(1)} %get-tuple-element.47), channel_id=1, source_target_pairs={{0,4},{4,8},{8,12},{12,0},{1,5},{5,9},{9,13},{13,1},{2,6},{6,10},{... | collective-permute-start | bytes 294920 | tf_op jit(solution)/shard_map/ppermute | solution.py:608
  19.9 2.6 %collective-permute-start.6 = (bf16[384,128]{1,0:T(8,128)(2,1)S(1)}, bf16[384,128]{1,0:T(8,128)(2,1)S(1)}, u32[]{:S(2)}, u32[]{:S(2)}) collective-permute-start(bf16[384,128]{1,0:T(8,128)(2,1)S(1)} %get-tuple-element.48), channel_id=1, source_target_pairs={{0,8},{4,12},{8,0},{12,4},{1,9},{5,13},{9,1},{13,5},{2,10},{6,14},... | collective-permute-start | bytes 294920 | tf_op jit(solution)/shard_map/ppermute | solution.py:608
  22.5 1.3 %collective-permute-start.7 = (bf16[384,128]{1,0:T(8,128)(2,1)S(1)}, bf16[384,128]{1,0:T(8,128)(2,1)S(1)}, u32[]{:S(2)}, u32[]{:S(2)}) collective-permute-start(bf16[384,128]{1,0:T(8,128)(2,1)S(1)} %get-tuple-element.49), channel_id=1, source_target_pairs={{0,12},{4,0},{8,4},{12,8},{1,13},{5,1},{9,5},{13,9},{2,14},{6,2},{... | collective-permute-start | bytes 294920 | tf_op jit(solution)/shard_map/ppermute | solution.py:608
  23.8 0.0 collective-permute-done.8.refs_4_
  23.8 0.5 collective-permute-start.11
  24.3 1.7 %collective-permute-start.10 = (bf16[128,128]{1,0:T(8,128)(2,1)S(1)}, bf16[128,128]{1,0:T(8,128)(2,1)S(1)}, u32[]{:S(2)}, u32[]{:S(2)}) collective-permute-start(bf16[128,128]{1,0:T(8,128)(2,1)S(1)} %get-tuple-element.62), channel_id=1, source_target_pairs={{0,8},{4,12},{8,0},{12,4},{1,9},{5,13},{9,1},{13,5},{2,10},{6,14},... | collective-permute-start | bytes 98312 | tf_op jit(solution)/shard_map/ppermute | solution.py:609
  26.0 0.0 collective-permute-done.5.refs_1_
  26.0 3.4 %collective-permute-start.9 = (bf16[128,128]{1,0:T(8,128)(2,1)S(1)}, bf16[128,128]{1,0:T(8,128)(2,1)S(1)}, u32[]{:S(2)}, u32[]{:S(2)}) collective-permute-start(bf16[128,128]{1,0:T(8,128)(2,1)S(1)} %get-tuple-element.63), channel_id=1, source_target_pairs={{0,4},{4,8},{8,12},{12,0},{1,5},{5,9},{9,13},{13,1},{2,6},{6,10},{... | collective-permute-start | bytes 98312 | tf_op jit(solution)/shard_map/ppermute | solution.py:609
  29.4 0.1 collective-permute-done.6.refs_2_
  29.5 0.2 collective-permute-done.7.refs_3_
  29.8 0.4 collective-permute-done.11.refs_7_
  30.1 4.3 %collective-permute-done.10.refs_6_ = bf16[128,128]{1,0:T(8,128)(2,1)S(1)} collective-permute-done((bf16[128,128]{1,0:T(8,128)(2,1)S(1)}, bf16[128,128]{1,0:T(8,128)(2,1)S(1)}, u32[]{:S(2)}, u32[]{:S(2)}) %collective-permute-start.10) | collective-permute-done | bytes 32800 | tf_op jit(solution)/shard_map/ppermute | solution.py:609
  34.4 0.0 collective-permute-done.9.refs_5_
  34.4 0.0 copy-start
  34.4 8.5 %integrate.1 = (bf16[480,128]{1,0:T(8,128)(2,1)S(1)}, bf16[480,128]{1,0:T(8,128)(2,1)S(1)}, bf16[480,128]{1,0:T(8,128)(2,1)S(1)}, bf16[480,128]{1,0:T(8,128)(2,1)S(1)}) custom-call(bf16[1920,1920]{1,0:T(8,128)(2,1)S(1)} %get-tuple-element.45.whole_w, bf16[384,128]{1,0:T(8,128)(2,1)S(1)} %get-tuple-element.46.refs_0_, ...), custom_call_target="tpu_custom_call" | custom-call | flops 3774873600 | bytes 7372800 | tf_op jit(solution)/shard_map/integrate/pallas_call | solution.py:470
  42.9 0.1 collective-permute-start.13
  43.0 0.5 collective-permute-start.12
  43.5 0.0 collective-permute-start.14
  43.5 2.1 %collective-permute-start.15 = (bf16[480,128]{1,0:T(8,128)(2,1)S(1)}, bf16[480,128]{1,0:T(8,128)(2,1)S(1)}, u32[]{:S(2)}, u32[]{:S(2)}) collective-permute-start(bf16[480,128]{1,0:T(8,128)(2,1)S(1)} %get-tuple-element.59), channel_id=1, source_target_pairs={{0,8},{4,12},{8,0},{12,4},{1,9},{5,13},{9,1},{13,5},{2,10},{6,14},... | collective-permute-start | bytes 368648 | tf_op jit(solution)/shard_map/ppermute | solution.py:612
  45.6 2.6 %collective-permute-start.16 = (bf16[480,128]{1,0:T(8,128)(2,1)S(1)}, bf16[480,128]{1,0:T(8,128)(2,1)S(1)}, u32[]{:S(2)}, u32[]{:S(2)}) collective-permute-start(bf16[480,128]{1,0:T(8,128)(2,1)S(1)} %get-tuple-element.60), channel_id=1, source_target_pairs={{0,12},{4,0},{8,4},{12,8},{1,13},{5,1},{9,5},{13,9},{2,14},{6,2},{... | collective-permute-start | bytes 368648 | tf_op jit(solution)/shard_map/ppermute | solution.py:612
  48.1 3.5 %collective-permute-done.14.refs_6_ = bf16[480,128]{1,0:T(8,128)(2,1)S(1)} collective-permute-done((bf16[480,128]{1,0:T(8,128)(2,1)S(1)}, bf16[480,128]{1,0:T(8,128)(2,1)S(1)}, u32[]{:S(2)}, u32[]{:S(2)}) %collective-permute-start.14) | collective-permute-done | bytes 122912 | tf_op jit(solution)/shard_map/ppermute | solution.py:612
  51.6 4.3 %collective-permute-done.15.refs_7_ = bf16[480,128]{1,0:T(8,128)(2,1)S(1)} collective-permute-done((bf16[480,128]{1,0:T(8,128)(2,1)S(1)}, bf16[480,128]{1,0:T(8,128)(2,1)S(1)}, u32[]{:S(2)}, u32[]{:S(2)}) %collective-permute-start.15) | collective-permute-done | bytes 122912 | tf_op jit(solution)/shard_map/ppermute | solution.py:612
  55.9 0.0 collective-permute-done.16.refs_8_
  55.9 0.0 collective-permute-done.13.refs_3_
  55.9 0.0 collective-permute-done.12.refs_2_
  55.9 0.0 copy-done
  55.9 1.6 %finish.1 = f32[480,512]{1,0:T(8,128)} custom-call(f32[2,128,512]{2,1,0:T(8,128)S(1)} %get-tuple-element.55.refs_0_, f32[2,128,512]{2,1,0:T(8,128)S(1)} %get-tuple-element.56.refs_1_, f32[1,128,512]{2,1,0:T(8,128)S(1)} %collective-permute-done.12.refs_2_, f32[1,128,512]{2,1,0:T(8,128)S(1)} %collective-permute-done.13.refs_3_, s32[1,512]{1,0:T(1,128)S(1)} %bitcast.8, ...), custom_call_target="tpu_custom_call" | custom-call | tf_op jit(solution)/shard_map/finish/pallas_call | solution.py:544
  (3 shorter events, 0.0 us)
Async XLA Ops:
  0.0 12.1 %collective-permute-start.3 = (bf16[960,1920]{1,0:T(8,128)(2,1)}, bf16[960,1920]{1,0:T(8,128)(2,1)S(1)}, u32[]{:S(2)}, u32[]{:S(2)}) collective-permute-start(bf16[960,1920]{1,0:T(8,128)(2,1)} %refs_10_.1), channel_id=1, source_target_pairs={{0,1},{1,0},{2,3},{3,2},{4,5},{5,4},{6,7},{7,6},{8,9},{9,8},{10,11... | collective-permute-start | bytes 11059208 | tf_op jit(solution)/shard_map/ppermute | solution.py:569
  2.5 5.0 %collective-permute-start = (f32[264,512]{1,0:T(8,128)S(1)}, f32[264,512]{1,0:T(8,128)S(1)}, u32[]{:S(2)}, u32[]{:S(2)}) collective-permute-start(f32[264,512]{1,0:T(8,128)S(1)} %get-tuple-element.34), channel_id=1, source_target_pairs={{0,1},{1,0},{2,3},{3,2},{4,5},{5,4},{6,7},{7,6},{8,9},{9,8},{10,11... | collective-permute-start | bytes 1622024 | tf_op jit(solution)/shard_map/ppermute | solution.py:569
  2.6 8.4 %collective-permute-start.1 = (s16[136,512]{1,0:T(8,128)(2,1)S(1)}, s16[136,512]{1,0:T(8,128)(2,1)S(1)}, u32[]{:S(2)}, u32[]{:S(2)}) collective-permute-start(s16[136,512]{1,0:T(8,128)(2,1)S(1)} %get-tuple-element.36), channel_id=1, source_target_pairs={{0,2},{1,3},{2,0},{3,1},{4,6},{5,7},{6,4},{7,5},{8,10},{9,11},{10,... | collective-permute-start | bytes 417800 | tf_op jit(solution)/shard_map/ppermute | solution.py:569
  5.6 6.3 %collective-permute-start.2 = (s16[136,512]{1,0:T(8,128)(2,1)S(1)}, s16[136,512]{1,0:T(8,128)(2,1)S(1)}, u32[]{:S(2)}, u32[]{:S(2)}) collective-permute-start(s16[136,512]{1,0:T(8,128)(2,1)S(1)} %get-tuple-element.37), channel_id=1, source_target_pairs={{0,3},{1,2},{2,1},{3,0},{4,7},{5,6},{6,5},{7,4},{8,11},{9,10},{10,... | collective-permute-start | bytes 417800 | tf_op jit(solution)/shard_map/ppermute | solution.py:569
  10.6 1.4 %collective-permute-start.4 = (bf16[4,128,128]{2,1,0:T(8,128)(2,1)S(1)}, bf16[4,128,128]{2,1,0:T(8,128)(2,1)S(1)}, u32[]{:S(2)}, u32[]{:S(2)}) collective-permute-start(bf16[4,128,128]{2,1,0:T(8,128)(2,1)S(1)} %get-tuple-element.38), channel_id=1, source_target_pairs={{0,1},{1,0},{2,3},{3,2},{4,5},{5,4},{6,7},{7,6},{8,9},{9,8},{10,11... | collective-permute-start | bytes 393224 | tf_op jit(solution)/shard_map/ppermute | solution.py:569
  16.7 7.1 %collective-permute-start.8 = (bf16[4,128,128]{2,1,0:T(8,128)(2,1)S(1)}, bf16[4,128,128]{2,1,0:T(8,128)(2,1)S(1)}, u32[]{:S(2)}, u32[]{:S(2)}) collective-permute-start(bf16[4,128,128]{2,1,0:T(8,128)(2,1)S(1)} %get-tuple-element.50), channel_id=1, source_target_pairs={{0,1},{1,0},{2,3},{3,2},{4,5},{5,4},{6,7},{7,6},{8,9},{9,8},{10,11... | collective-permute-start | bytes 393224 | tf_op jit(solution)/shard_map/ppermute | solution.py:569
  17.2 8.9 %collective-permute-start.5 = (bf16[384,128]{1,0:T(8,128)(2,1)S(1)}, bf16[384,128]{1,0:T(8,128)(2,1)S(1)}, u32[]{:S(2)}, u32[]{:S(2)}) collective-permute-start(bf16[384,128]{1,0:T(8,128)(2,1)S(1)} %get-tuple-element.47), channel_id=1, source_target_pairs={{0,4},{4,8},{8,12},{12,0},{1,5},{5,9},{9,13},{13,1},{2,6},{6,10},{... | collective-permute-start | bytes 294920 | tf_op jit(solution)/shard_map/ppermute | solution.py:608
  19.9 9.7 %collective-permute-start.6 = (bf16[384,128]{1,0:T(8,128)(2,1)S(1)}, bf16[384,128]{1,0:T(8,128)(2,1)S(1)}, u32[]{:S(2)}, u32[]{:S(2)}) collective-permute-start(bf16[384,128]{1,0:T(8,128)(2,1)S(1)} %get-tuple-element.48), channel_id=1, source_target_pairs={{0,8},{4,12},{8,0},{12,4},{1,9},{5,13},{9,1},{13,5},{2,10},{6,14},... | collective-permute-start | bytes 294920 | tf_op jit(solution)/shard_map/ppermute | solution.py:608
  22.5 7.3 %collective-permute-start.7 = (bf16[384,128]{1,0:T(8,128)(2,1)S(1)}, bf16[384,128]{1,0:T(8,128)(2,1)S(1)}, u32[]{:S(2)}, u32[]{:S(2)}) collective-permute-start(bf16[384,128]{1,0:T(8,128)(2,1)S(1)} %get-tuple-element.49), channel_id=1, source_target_pairs={{0,12},{4,0},{8,4},{12,8},{1,13},{5,1},{9,5},{13,9},{2,14},{6,2},{... | collective-permute-start | bytes 294920 | tf_op jit(solution)/shard_map/ppermute | solution.py:608
  23.8 6.3 %collective-permute-start.11 = (bf16[128,128]{1,0:T(8,128)(2,1)S(1)}, bf16[128,128]{1,0:T(8,128)(2,1)S(1)}, u32[]{:S(2)}, u32[]{:S(2)}) collective-permute-start(bf16[128,128]{1,0:T(8,128)(2,1)S(1)} %get-tuple-element.61), channel_id=1, source_target_pairs={{0,12},{4,0},{8,4},{12,8},{1,13},{5,1},{9,5},{13,9},{2,14},{6,2},{... | collective-permute-start | bytes 98312 | tf_op jit(solution)/shard_map/ppermute | solution.py:609
  24.3 10.1 %collective-permute-start.10 = (bf16[128,128]{1,0:T(8,128)(2,1)S(1)}, bf16[128,128]{1,0:T(8,128)(2,1)S(1)}, u32[]{:S(2)}, u32[]{:S(2)}) collective-permute-start(bf16[128,128]{1,0:T(8,128)(2,1)S(1)} %get-tuple-element.62), channel_id=1, source_target_pairs={{0,8},{4,12},{8,0},{12,4},{1,9},{5,13},{9,1},{13,5},{2,10},{6,14},... | collective-permute-start | bytes 98312 | tf_op jit(solution)/shard_map/ppermute | solution.py:609
  26.0 8.4 %collective-permute-start.9 = (bf16[128,128]{1,0:T(8,128)(2,1)S(1)}, bf16[128,128]{1,0:T(8,128)(2,1)S(1)}, u32[]{:S(2)}, u32[]{:S(2)}) collective-permute-start(bf16[128,128]{1,0:T(8,128)(2,1)S(1)} %get-tuple-element.63), channel_id=1, source_target_pairs={{0,4},{4,8},{8,12},{12,0},{1,5},{5,9},{9,13},{13,1},{2,6},{6,10},{... | collective-permute-start | bytes 98312 | tf_op jit(solution)/shard_map/ppermute | solution.py:609
  34.4 21.5 %copy-start = (s32[512]{0:T(512)S(1)}, s32[512]{0:T(512)}, u32[]{:S(2)}) copy-start(s32[512]{0:T(512)} %param.8) | copy-start | bytes 6148
  42.9 13.0 %collective-permute-start.13 = (f32[1,128,512]{2,1,0:T(8,128)S(1)}, f32[1,128,512]{2,1,0:T(8,128)S(1)}, u32[]{:S(2)}, u32[]{:S(2)}) collective-permute-start(f32[1,128,512]{2,1,0:T(8,128)S(1)} %slice.19), channel_id=1, source_target_pairs={{0,1},{1,0},{2,3},{3,2},{4,5},{5,4},{6,7},{7,6},{8,9},{9,8},{10,11... | collective-permute-start | bytes 786440 | tf_op jit(solution)/shard_map/ppermute | solution.py:569
  43.0 12.9 %collective-permute-start.12 = (f32[1,128,512]{2,1,0:T(8,128)S(1)}, f32[1,128,512]{2,1,0:T(8,128)S(1)}, u32[]{:S(2)}, u32[]{:S(2)}) collective-permute-start(f32[1,128,512]{2,1,0:T(8,128)S(1)} %slice.18), channel_id=1, source_target_pairs={{0,1},{1,0},{2,3},{3,2},{4,5},{5,4},{6,7},{7,6},{8,9},{9,8},{10,11... | collective-permute-start | bytes 786440 | tf_op jit(solution)/shard_map/ppermute | solution.py:569
  43.5 8.1 %collective-permute-start.14 = (bf16[480,128]{1,0:T(8,128)(2,1)S(1)}, bf16[480,128]{1,0:T(8,128)(2,1)S(1)}, u32[]{:S(2)}, u32[]{:S(2)}) collective-permute-start(bf16[480,128]{1,0:T(8,128)(2,1)S(1)} %get-tuple-element.58), channel_id=1, source_target_pairs={{0,4},{4,8},{8,12},{12,0},{1,5},{5,9},{9,13},{13,1},{2,6},{6,10},{... | collective-permute-start | bytes 368648 | tf_op jit(solution)/shard_map/ppermute | solution.py:612
  43.5 12.4 %collective-permute-start.15 = (bf16[480,128]{1,0:T(8,128)(2,1)S(1)}, bf16[480,128]{1,0:T(8,128)(2,1)S(1)}, u32[]{:S(2)}, u32[]{:S(2)}) collective-permute-start(bf16[480,128]{1,0:T(8,128)(2,1)S(1)} %get-tuple-element.59), channel_id=1, source_target_pairs={{0,8},{4,12},{8,0},{12,4},{1,9},{5,13},{9,1},{13,5},{2,10},{6,14},... | collective-permute-start | bytes 368648 | tf_op jit(solution)/shard_map/ppermute | solution.py:612
  45.6 10.3 %collective-permute-start.16 = (bf16[480,128]{1,0:T(8,128)(2,1)S(1)}, bf16[480,128]{1,0:T(8,128)(2,1)S(1)}, u32[]{:S(2)}, u32[]{:S(2)}) collective-permute-start(bf16[480,128]{1,0:T(8,128)(2,1)S(1)} %get-tuple-element.60), channel_id=1, source_target_pairs={{0,12},{4,0},{8,4},{12,8},{1,13},{5,1},{9,5},{13,9},{2,14},{6,2},{... | collective-permute-start | bytes 368648 | tf_op jit(solution)/shard_map/ppermute | solution.py:612

commit v8 on v7

--- a/solution.py
+++ b/solution.py
@@ -190,10 +190,20 @@
     return lat, sub, (first_group + lat) % 2, first_group
 
 
-def pack_kernel(sizes, spectrum, neighbours, sea_mask, mine, to_pair, to_near, to_far):
+def pack_kernel(sizes, spectrum, neighbours, sea_mask, mine, to_pair, to_near, to_far, held, sem):
     bins_local, half_bins, rows_local = sizes
     _, sub, parity, _ = device_place(bins_local)
     sectors = half_bins // (2 * SECTOR)
+    copies = []
+    for other in range(2):
+        base = (sub + other) % 2 * half_bins
+        for k in range(sectors):
+            for rest in range(2):
+                group = (2 * k + (parity + rest) % 2) * SECTOR
+                source = pl.ds(pl.multiple_of(jnp.minimum(base + group, bins_local - SECTOR), SECTOR), SECTOR)
+                index = len(copies)
+                copies.append(pltpu.make_async_copy(spectrum.at[source], held.at[index], sem.at[index]))
+                copies[index].start()
     for row in range(rows_local):
         halves = [slice(row * NLON + h * LANES, row * NLON + (h + 1) * LANES) for h in range(2)]
         sea = [sea_mask[0:1, at].astype(jnp.float32) for at in halves]
@@ -214,24 +224,21 @@
         for j in range(2 * rows_local)
     ]
 
-    for other in range(2):
-        base = (sub + other) % 2 * half_bins
+    for index, copy in enumerate(copies):
+        other, k, rest = index // (2 * sectors), index // 2 % sectors, index % 2
         whole, sent = (to_pair, to_far) if other else (mine, to_near)
-        for k in range(sectors):
-            for rest in range(2):
-                group = (2 * k + (parity + rest) % 2) * SECTOR
-                source = pl.ds(pl.multiple_of(jnp.minimum(base + group, bins_local - SECTOR), SECTOR), SECTOR)
-                target = pl.ds(pl.multiple_of(group, SECTOR), SECTOR)
-                for row in range(rows_local):
-                    pair = [
-                        spectrum[source, (2 * row + h) * LANES : (2 * row + h + 1) * LANES] * sea_rows[2 * row + h]
-                        for h in range(2)
-                    ]
-                    for h, block in enumerate(split_columns(*pair)):
-                        at = slice((2 * row + h) * LANES, (2 * row + h + 1) * LANES)
-                        whole[target, at] = block
-                        if not rest:
-                            sent[k * SECTOR : (k + 1) * SECTOR, at] = encode(block)
+        target = pl.ds(pl.multiple_of((2 * k + (parity + rest) % 2) * SECTOR, SECTOR), SECTOR)
+        copy.wait()
+        for row in range(rows_local):
+            pair = [
+                held[index, :, (2 * row + h) * LANES : (2 * row + h + 1) * LANES] * sea_rows[2 * row + h]
+                for h in range(2)
+            ]
+            for h, block in enumerate(split_columns(*pair)):
+                at = slice((2 * row + h) * LANES, (2 * row + h + 1) * LANES)
+                whole[target, at] = block
+                if not rest:
+                    sent[k * SECTOR : (k + 1) * SECTOR, at] = encode(block)
 
 
 def pack(sizes, spectrum, neighbours, sea_mask):
@@ -242,7 +249,11 @@
         functools.partial(pack_kernel, sizes),
         name="pack",
         compiler_params=GRANT,
-        in_specs=[vmem, vmem, vmem],
+        in_specs=[pl.BlockSpec(memory_space=pl.ANY), vmem, vmem],
+        scratch_shapes=[
+            pltpu.VMEM((2 * half_bins // SECTOR, SECTOR, points), jnp.float32),
+            pltpu.SemaphoreType.DMA((2 * half_bins // SECTOR,)),
+        ],
         out_specs=[vmem] * 4,
         out_shape=[pltpu.VMEM((half_bins + TILE, points), jnp.float32)] * 2
         + [pltpu.VMEM((half_bins // 2 + TILE, points), jnp.int16)] * 2,
@@ -252,9 +263,8 @@
 def stencil_kernel(sizes, *refs):
     bins_local, half_bins, rows_local, dependent = sizes
     if dependent:
-        steps_ref, courant_ref, trig, mine, pair, near, far, kept, crossed, other_w, own_w = refs[:11]
-        passed, field_out, whole_w = refs[11:14]
-        sent, (tab, begun, sem) = refs[14:-3], refs[-3:]
+        steps_ref, courant_ref, trig, mine, pair, near, far, kept, free_passed, passed, field_out = refs[:11]
+        sent, (tab, begun) = refs[11:-2], refs[-2:]
     else:
         steps_ref, courant_ref, trig, mine, pair, kept, passed, field_out, tab, begun = refs
     lat, sub, parity, first_group = device_place(bins_local)
@@ -262,12 +272,6 @@
     first_group = first_group + sub * (half_bins // SECTOR)
     chip_rows = 2 * rows_local
     halo = chip_rows if dependent else 0
-    copies = []
-    if dependent:
-        for other, source in enumerate((own_w, other_w)):
-            at = pl.ds(pl.multiple_of((sub + other) % 2 * source.shape[0], 64), source.shape[0])
-            copies.append(pltpu.make_async_copy(source, whole_w.at[at], sem.at[other]))
-            copies[other].start()
     north = lat == (0 if dependent else 1)
     flip = north.astype(jnp.int32)
 
@@ -370,21 +374,19 @@
     lax.fori_loop(0, half_bins // (2 * SECTOR), both_sides, 0)
     quarters = begun.shape[1]
     if dependent:
-        third = half_bins // 2
+        middle = half_bins // 2
         for k in range(quarters):
             quarter = (lax.axis_index("comp") + k) % quarters
-            sent[k][:third] = kept[quarter]
-            sent[k][third : 2 * third] = crossed[quarter]
-            sent[k][2 * third :] = begun[0, quarter]
-            passed[k] = begun[1, quarter]
+            sent[k][:middle] = kept[quarter]
+            sent[k][middle:] = begun[0, quarter]
+            passed[k, :middle] = free_passed[quarter]
+            passed[k, middle:] = begun[1, quarter]
     else:
         kept[...] = begun[0]
         passed[...] = begun[1]
-    for copy in copies:
-        copy.wait()
-
-
-def stencil(sizes, substeps, courant, trig, *fields, operator=None):
+
+
+def stencil(sizes, substeps, courant, trig, *fields):
     _, half_bins, rows_local, dependent = sizes
     quarters = 2 * rows_local
     rows = (4 if dependent else 2) * rows_local
@@ -401,11 +403,8 @@
     args = list(map(off_chip, (substeps, courant, trig))) + list(map(on_chip, fields))
     out_shape = [states, states, field]
     if dependent:
-        in_specs.append(pl.BlockSpec(memory_space=pl.ANY))
-        args.append(off_chip(operator))
-        out_shape = [states, field, pltpu.VMEM((2 * operator.shape[0], operator.shape[1]), jnp.bfloat16)]
-        out_shape += [pltpu.VMEM((half_bins // 2 * 3, LANES), jnp.bfloat16)] * quarters
-        scratch.append(pltpu.SemaphoreType.DMA((2,)))
+        out_shape = [pltpu.VMEM((quarters, half_bins, LANES), jnp.bfloat16), field]
+        out_shape += [pltpu.VMEM((half_bins, LANES), jnp.bfloat16)] * quarters
     return pl.pallas_call(
         functools.partial(stencil_kernel, sizes),
         name="stencil_dependent" if dependent else "stencil_free",
@@ -418,6 +417,35 @@
     )(*args)
 
 
+def gather_operator_kernel(own_w, other_w, whole_w, sem):
+    sub = lax.axis_index("sub")
+    pieces = sem.shape[1]
+    rows = own_w.shape[0] // pieces
+    copies = []
+    for other, source in enumerate((own_w, other_w)):
+        for p in range(pieces):
+            at = pl.ds(pl.multiple_of((sub + other) % 2 * own_w.shape[0] + p * rows, 64), rows)
+            copy = pltpu.make_async_copy(source.at[pl.ds(p * rows, rows)], whole_w.at[at], sem.at[other, p])
+            copy.start()
+            copies.append(copy)
+    for copy in copies:
+        copy.wait()
+
+
+def gather_operator(own_w, other_w):
+    rows, columns = own_w.shape
+    return pl.pallas_call(
+        gather_operator_kernel,
+        name="gather_operator",
+        compiler_params=GRANT,
+        in_specs=[pl.BlockSpec(memory_space=pl.ANY), pl.BlockSpec(memory_space=pltpu.VMEM)],
+        out_specs=pl.BlockSpec(memory_space=pltpu.VMEM),
+        out_shape=pltpu.VMEM((2 * rows, columns), jnp.bfloat16),
+        scratch_shapes=[pltpu.SemaphoreType.DMA((2, 3))],
+        cost_estimate=pl.CostEstimate(flops=0, bytes_accessed=4 * rows * columns, transcendentals=0),
+    )(off_chip(own_w), on_chip(other_w))
+
+
 def integrate_kernel(sizes, whole_w, *refs):
     bins_local, half_bins, comps = sizes
     large, passed, small = refs[:comps], refs[comps], refs[comps + 1 : 2 * comps]
@@ -426,16 +454,12 @@
     total = comps * bins_local
     sectors = half_bins // (2 * SECTOR)
     groups = bins_local // SECTOR
-    third = half_bins // 2
+    middle = half_bins // 2
     for k in range(comps):
         source = (comp + comps - k) % comps
         free = (source * groups + lat) % 2
-        parts = (
-            (large[k], 0, 0, 0),
-            (large[k], third, 1, 0),
-            (large[k], 2 * third, 0, 1),
-            (small[k - 1] if k else passed.at[0], 0, 1, 1),
-        )
+        crossed = small[k - 1] if k else passed.at[0]
+        parts = ((large[k], 0, 0, 0), (large[k], middle, 0, 1), (crossed, 0, 1, 0), (crossed, middle, 1, 1))
         for blocks, first, other, dep in parts:
             for sector in range(sectors):
                 local = (sub + other) % 2 * half_bins + (2 * sector + (free + dep) % 2) * SECTOR
@@ -579,7 +603,6 @@
     trig = np.abs(np.stack([np.cos(angles), np.sin(angles)])).astype(np.float32)
     trig = jnp.asarray(np.repeat(trig[:, :, None], LANES, axis=2))
 
-    other_w = swap(source_operator, 1)
     mine, to_pair, to_near, to_far = pack(
         (bins_local, half_bins, rows_local), spectrum, neighbours, sea_mask
     )
@@ -587,28 +610,18 @@
     near = swap(to_near, 2)
     far = swap(to_far, 3)
     kept, passed, free_field = stencil((bins_local, half_bins, rows_local, False), substeps, courant, trig, mine, pair)
-    crossed = swap(passed, 1)
-    near, far, other_w, crossed = lax.optimization_barrier((near, far, other_w, crossed))
-    passed, dep_field, whole_w, *sent = stencil(
-        (bins_local, half_bins, rows_local, True),
-        substeps,
-        courant,
-        trig,
-        mine,
-        pair,
-        near,
-        far,
-        kept,
-        crossed,
-        other_w,
-        operator=source_operator,
+    source_operator, kept = lax.optimization_barrier((source_operator, kept))
+    other_w = swap(source_operator, 1)
+    near, far, kept = lax.optimization_barrier((near, far, kept))
+    passed, dep_field, *sent = stencil(
+        (bins_local, half_bins, rows_local, True), substeps, courant, trig, mine, pair, near, far, kept, passed
     )
     ring = [[(i, (i + k) % comps) for i in range(comps)] for k in range(comps)]
     passed = swap(passed, 1)
     large = [sent[0]] + [lax.ppermute(sent[k], "comp", ring[k]) for k in range(1, comps)]
     small = [lax.ppermute(passed[k], "comp", ring[k]) for k in range(1, comps)]
+    whole_w = gather_operator(source_operator, other_w)
     raised = integrate((bins_local, half_bins, comps), whole_w, large, passed, small)
-    free_field, dep_field, raised = lax.optimization_barrier((free_field, dep_field, raised))
     home = [raised[0]] + [lax.ppermute(raised[k], "comp", ring[k]) for k in range(1, comps)]
     got_free = swap(free_field[1:], 1)
     got_dep = swap(dep_field[1:], 1)

time: 57.7 us -> 61 us (1.057)
  starting transfers between devices: 21.9 us -> 18.4 us
  Pallas kernels: 19.9 us -> 23.2 us
  waiting for transfers between devices: 15.6 us -> 18.7 us
    ppermute x8 -> x7, waiting for transfers between devices: 2.93 us -> 8.44 us  [swap(): lax.ppermute(values, ('lat', 'sub'), [(i, i ^ bits) for i in range(count)])]
    ppermute x3, waiting for transfers between devices: 4.61 us -> 2.24 us  [two_chip_device(): small = [lax.ppermute(passed[k], 'comp', ring[k]) for k in range(1, comps)]]
    pallas_call x0 -> x1, Pallas kernels: none -> 2.1 us  [gather_operator(): pl.pallas_call(gather_operator_kernel, name='gather_operator', compiler_p...]
    ppermute x3, starting transfers between devices: 5.58 us -> 3.93 us  [two_chip_device(): small = [lax.ppermute(passed[k], 'comp', ring[k]) for k in range(1, comps)]]
    pallas_call x1, Pallas kernels: 2.05 us -> 3.54 us  [pack(): pl.pallas_call(functools.partial(pack_kernel, sizes), name='pack', compil...]
    ppermute x3, starting transfers between devices: 6.64 us -> 5.76 us  [two_chip_device(): lax.ppermute(sent[k], 'comp', ring[k])]
    ppermute x8 -> x7, starting transfers between devices: 4.99 us -> 4.38 us  [swap(): lax.ppermute(values, ('lat', 'sub'), [(i, i ^ bits) for i in range(count)])]
  transfers between devices with their start and end apart: 17 -> 16, of which waited for: 9 -> 6; matrix products, arithmetic and copies ran while one was open for 0% -> 0% of each run, Pallas kernels for 9% -> 25%
where the time goes in v8:
time: 61 us; the launch traced here: 60.5 us
  Pallas kernels  23.2 us (38%)
  waiting for transfers between devices  18.7 us (31%)
  starting transfers between devices  18.4 us (30%)
    pallas_call x1, Pallas kernels, integrate(): pl.pallas_call(functools.partial(integrate_kernel, sizes), name='integrat...  8.46 us
    ppermute x7, waiting for transfers between devices, swap(): lax.ppermute(values, ('lat', 'sub'), [(i, i ^ bits) for i in range(count)])  8.44 us
    ppermute x3, waiting for transfers between devices, two_chip_device(): lax.ppermute(raised[k], 'comp', ring[k])  7.99 us
    pallas_call x2, Pallas kernels, stencil(): pl.pallas_call(functools.partial(stencil_kernel, sizes), name='stencil_de...  7.45 us
    ppermute x3, starting transfers between devices, two_chip_device(): lax.ppermute(sent[k], 'comp', ring[k])  5.76 us
    ppermute x7, starting transfers between devices, swap(): lax.ppermute(values, ('lat', 'sub'), [(i, i ^ bits) for i in range(count)])  4.38 us
    ppermute x3, starting transfers between devices, two_chip_device(): lax.ppermute(raised[k], 'comp', ring[k])  4.36 us
    ppermute x3, starting transfers between devices, two_chip_device(): small = [lax.ppermute(passed[k], 'comp', ring[k]) for k in range(1, comps)]  3.93 us
  transfers between devices with their start and end apart: 16, of which 6 were waited for; matrix products, arithmetic and copies ran while one was open for 0% of the time, Pallas kernels for 25%

profile of v8, /device:TPU:0, one launch (start us, length us, event | category | flops | bytes accessed | tf_op | source)
XLA Modules:
  0.0 60.5 jit_solution(16158046800309726170)
XLA Ops:
  0.0 3.5 %pack.1 = (f32[264,512]{1,0:T(8,128)S(1)}, f32[264,512]{1,0:T(8,128)S(1)}, s16[136,512]{1,0:T(8,128)(2,1)S(1)}, s16[136,512]{1,0:T(8,128)(2,1)S(1)}) custom-call(f32[480,512]{1,0:T(8,128)} %spectrum.1, s32[4,512]{1,0:T(4,128)} %neighbours.1, s32[1,512]{1,0:T(1,128)} %bitcast.7), custom_call_target="tpu_custom_call" | custom-call | tf_op jit(solution)/shard_map/pack/pallas_call | solution.py:248
  3.5 0.6 collective-permute-start
  4.1 1.6 %collective-permute-done.refs_4_ = f32[264,512]{1,0:T(8,128)S(1)} collective-permute-done((f32[264,512]{1,0:T(8,128)S(1)}, f32[264,512]{1,0:T(8,128)S(1)}, u32[]{:S(2)}, u32[]{:S(2)}) %collective-permute-start) | collective-permute-done | bytes 540704 | tf_op jit(solution)/shard_map/ppermute | solution.py:593
  5.7 3.1 %stencil_free.1 = (bf16[4,128,128]{2,1,0:T(8,128)(2,1)S(1)}, bf16[4,128,128]{2,1,0:T(8,128)(2,1)S(1)}, f32[2,128,512]{2,1,0:T(8,128)S(1)}) custom-call(s32[30]{0:T(128)} %refs_0_.3, f32[30]{0:T(128)} %refs_1_.3, f32[2,64,128]{2,1,0:T(8,128)} %constant.2.clone.refs_2_, f32[264,512]{1,0:T(8,128)S(1)} %get-tuple-element.27.refs_3_, ...), custom_call_target="tpu_custom_call" | custom-call | flops 78643200 | bytes 2097152 | tf_op jit(solution)/shard_map/stencil_free/pallas_call | solution.py:408
  8.8 0.4 collective-permute-start.5
  9.2 2.6 %collective-permute-start.1 = (s16[136,512]{1,0:T(8,128)(2,1)S(1)}, s16[136,512]{1,0:T(8,128)(2,1)S(1)}, u32[]{:S(2)}, u32[]{:S(2)}) collective-permute-start(s16[136,512]{1,0:T(8,128)(2,1)S(1)} %get-tuple-element.30), channel_id=1, source_target_pairs={{0,2},{1,3},{2,0},{3,1},{4,6},{5,7},{6,4},{7,5},{8,10},{9,11},{10,... | collective-permute-start | bytes 417800 | tf_op jit(solution)/shard_map/ppermute | solution.py:593
  11.8 0.0 collective-permute-start.2
  11.8 4.5 %collective-permute-done.1.refs_5_ = s16[136,512]{1,0:T(8,128)(2,1)S(1)} collective-permute-done((s16[136,512]{1,0:T(8,128)(2,1)S(1)}, s16[136,512]{1,0:T(8,128)(2,1)S(1)}, u32[]{:S(2)}, u32[]{:S(2)}) %collective-permute-start.1) | collective-permute-done | bytes 139296 | tf_op jit(solution)/shard_map/ppermute | solution.py:593
  16.3 2.4 %collective-permute-done.2.refs_6_ = s16[136,512]{1,0:T(8,128)(2,1)S(1)} collective-permute-done((s16[136,512]{1,0:T(8,128)(2,1)S(1)}, s16[136,512]{1,0:T(8,128)(2,1)S(1)}, u32[]{:S(2)}, u32[]{:S(2)}) %collective-permute-start.2) | collective-permute-done | bytes 139296 | tf_op jit(solution)/shard_map/ppermute | solution.py:593
  18.7 4.4 %stencil_dependent.1 = (bf16[4,256,128]{2,1,0:T(8,128)(2,1)S(1)}, f32[2,128,512]{2,1,0:T(8,128)S(1)}, bf16[256,128]{1,0:T(8,128)(2,1)S(1)}, bf16[256,128]{1,0:T(...) custom-call(s32[30]{0:T(128)} %refs_0_.3, f32[30]{0:T(128)} %refs_1_.3, ...), custom_call_target="tpu_custom_call" | custom-call | flops 78643200 | bytes 2097152 | tf_op jit(solution)/shard_map/stencil_dependent/pallas_call | solution.py:408
  23.1 0.2 collective-permute-start.9
  23.3 1.8 %collective-permute-start.6 = (bf16[256,128]{1,0:T(8,128)(2,1)S(1)}, bf16[256,128]{1,0:T(8,128)(2,1)S(1)}, u32[]{:S(2)}, u32[]{:S(2)}) collective-permute-start(bf16[256,128]{1,0:T(8,128)(2,1)S(1)} %get-tuple-element.41), channel_id=1, source_target_pairs={{0,4},{4,8},{8,12},{12,0},{1,5},{5,9},{9,13},{13,1},{2,6},{6,10},{... | collective-permute-start | bytes 196616 | tf_op jit(solution)/shard_map/ppermute | solution.py:621
  25.1 2.6 %collective-permute-start.7 = (bf16[256,128]{1,0:T(8,128)(2,1)S(1)}, bf16[256,128]{1,0:T(8,128)(2,1)S(1)}, u32[]{:S(2)}, u32[]{:S(2)}) collective-permute-start(bf16[256,128]{1,0:T(8,128)(2,1)S(1)} %get-tuple-element.42), channel_id=1, source_target_pairs={{0,8},{4,12},{8,0},{12,4},{1,9},{5,13},{9,1},{13,5},{2,10},{6,14},... | collective-permute-start | bytes 196616 | tf_op jit(solution)/shard_map/ppermute | solution.py:621
  27.7 1.3 %collective-permute-start.8 = (bf16[256,128]{1,0:T(8,128)(2,1)S(1)}, bf16[256,128]{1,0:T(8,128)(2,1)S(1)}, u32[]{:S(2)}, u32[]{:S(2)}) collective-permute-start(bf16[256,128]{1,0:T(8,128)(2,1)S(1)} %get-tuple-element.43), channel_id=1, source_target_pairs={{0,12},{4,0},{8,4},{12,8},{1,13},{5,1},{9,5},{13,9},{2,14},{6,2},{... | collective-permute-start | bytes 196616 | tf_op jit(solution)/shard_map/ppermute | solution.py:621
  29.0 0.0 collective-permute-done.9.refs_4_
  29.0 0.7 %collective-permute-start.10 = (bf16[256,128]{1,0:T(8,128)(2,1)S(1)}, bf16[256,128]{1,0:T(8,128)(2,1)S(1)}, u32[]{:S(2)}, u32[]{:S(2)}) collective-permute-start(bf16[256,128]{1,0:T(8,128)(2,1)S(1)} %get-tuple-element.51), channel_id=1, source_target_pairs={{0,4},{4,8},{8,12},{12,0},{1,5},{5,9},{9,13},{13,1},{2,6},{6,10},{... | collective-permute-start | bytes 196616 | tf_op jit(solution)/shard_map/ppermute | solution.py:622
  29.8 0.0 collective-permute-done.6.refs_1_
  29.8 1.1 %collective-permute-start.11 = (bf16[256,128]{1,0:T(8,128)(2,1)S(1)}, bf16[256,128]{1,0:T(8,128)(2,1)S(1)}, u32[]{:S(2)}, u32[]{:S(2)}) collective-permute-start(bf16[256,128]{1,0:T(8,128)(2,1)S(1)} %get-tuple-element.50), channel_id=1, source_target_pairs={{0,8},{4,12},{8,0},{12,4},{1,9},{5,13},{9,1},{13,5},{2,10},{6,14},... | collective-permute-start | bytes 196616 | tf_op jit(solution)/shard_map/ppermute | solution.py:622
  30.9 0.0 collective-permute-done.5.other_w
  30.9 2.1 %collective-permute-start.12 = (bf16[256,128]{1,0:T(8,128)(2,1)S(1)}, bf16[256,128]{1,0:T(8,128)(2,1)S(1)}, u32[]{:S(2)}, u32[]{:S(2)}) collective-permute-start(bf16[256,128]{1,0:T(8,128)(2,1)S(1)} %get-tuple-element.49), channel_id=1, source_target_pairs={{0,12},{4,0},{8,4},{12,8},{1,13},{5,1},{9,5},{13,9},{2,14},{6,2},{... | collective-permute-start | bytes 196616 | tf_op jit(solution)/shard_map/ppermute | solution.py:622
  33.0 2.1 %gather_operator.1.whole_w = bf16[1920,1920]{1,0:T(8,128)(2,1)S(1)} custom-call(bf16[960,1920]{1,0:T(8,128)(2,1)} %own_w, bf16[960,1920]{1,0:T(8,128)(2,1)S(1)} %collective-permute-done.5.other_w), custom_call_target="tpu_custom_call" | custom-call | bytes 7372800 | tf_op jit(solution)/shard_map/gather_operator/pallas_call | solution.py:437
  35.1 0.0 collective-permute-done.7.refs_2_
  35.2 0.1 collective-permute-start.4
  35.2 0.0 collective-permute-done.8.refs_3_
  35.2 0.5 collective-permute-start.3
  35.7 0.0 collective-permute-done.10.refs_5_
  35.7 2.2 %collective-permute-done.11.refs_6_ = bf16[256,128]{1,0:T(8,128)(2,1)S(1)} collective-permute-done((bf16[256,128]{1,0:T(8,128)(2,1)S(1)}, bf16[256,128]{1,0:T(8,128)(2,1)S(1)}, u32[]{:S(2)}, u32[]{:S(2)}) %collective-permute-start.11) | collective-permute-done | bytes 65568 | tf_op jit(solution)/shard_map/ppermute | solution.py:622
  38.0 0.0 collective-permute-done.12.refs_7_
  38.0 0.0 copy-start
  38.0 8.5 %integrate.1 = (bf16[480,128]{1,0:T(8,128)(2,1)S(1)}, bf16[480,128]{1,0:T(8,128)(2,1)S(1)}, bf16[480,128]{1,0:T(8,128)(2,1)S(1)}, bf16[480,128]{1,0:T(8,128)(2,1)S(1)}) custom-call(bf16[1920,1920]{1,0:T(8,128)(2,1)S(1)} %gather_operator.1.whole_w, bf16[256,128]{1,0:T(8,128)(2,1)S(1)} %get-tuple-element.40.refs_0_, ...), custom_call_target="tpu_custom_call" | custom-call | flops 3774873600 | bytes 7372800 | tf_op jit(solution)/shard_map/integrate/pallas_call | solution.py:494
  46.5 1.9 %collective-permute-start.13 = (bf16[480,128]{1,0:T(8,128)(2,1)S(1)}, bf16[480,128]{1,0:T(8,128)(2,1)S(1)}, u32[]{:S(2)}, u32[]{:S(2)}) collective-permute-start(bf16[480,128]{1,0:T(8,128)(2,1)S(1)} %get-tuple-element.46), channel_id=1, source_target_pairs={{0,4},{4,8},{8,12},{12,0},{1,5},{5,9},{9,13},{13,1},{2,6},{6,10},{... | collective-permute-start | bytes 368648 | tf_op jit(solution)/shard_map/ppermute | solution.py:625
  48.4 1.8 %collective-permute-start.14 = (bf16[480,128]{1,0:T(8,128)(2,1)S(1)}, bf16[480,128]{1,0:T(8,128)(2,1)S(1)}, u32[]{:S(2)}, u32[]{:S(2)}) collective-permute-start(bf16[480,128]{1,0:T(8,128)(2,1)S(1)} %get-tuple-element.47), channel_id=1, source_target_pairs={{0,8},{4,12},{8,0},{12,4},{1,9},{5,13},{9,1},{13,5},{2,10},{6,14},... | collective-permute-start | bytes 368648 | tf_op jit(solution)/shard_map/ppermute | solution.py:625
  50.2 0.6 %collective-permute-start.15 = (bf16[480,128]{1,0:T(8,128)(2,1)S(1)}, bf16[480,128]{1,0:T(8,128)(2,1)S(1)}, u32[]{:S(2)}, u32[]{:S(2)}) collective-permute-start(bf16[480,128]{1,0:T(8,128)(2,1)S(1)} %get-tuple-element.48), channel_id=1, source_target_pairs={{0,12},{4,0},{8,4},{12,8},{1,13},{5,1},{9,5},{13,9},{2,14},{6,2},{... | collective-permute-start | bytes 368648 | tf_op jit(solution)/shard_map/ppermute | solution.py:625
  50.8 0.0 collective-permute-done.4.refs_3_
  50.8 0.0 collective-permute-done.3.refs_2_
  50.8 3.8 %collective-permute-done.13.refs_6_ = bf16[480,128]{1,0:T(8,128)(2,1)S(1)} collective-permute-done((bf16[480,128]{1,0:T(8,128)(2,1)S(1)}, bf16[480,128]{1,0:T(8,128)(2,1)S(1)}, u32[]{:S(2)}, u32[]{:S(2)}) %collective-permute-start.13) | collective-permute-done | bytes 122912 | tf_op jit(solution)/shard_map/ppermute | solution.py:625
  54.6 4.2 %collective-permute-done.14.refs_7_ = bf16[480,128]{1,0:T(8,128)(2,1)S(1)} collective-permute-done((bf16[480,128]{1,0:T(8,128)(2,1)S(1)}, bf16[480,128]{1,0:T(8,128)(2,1)S(1)}, u32[]{:S(2)}, u32[]{:S(2)}) %collective-permute-start.14) | collective-permute-done | bytes 122912 | tf_op jit(solution)/shard_map/ppermute | solution.py:625
  58.8 0.0 collective-permute-done.15.refs_8_
  58.8 0.0 copy-done
  58.8 1.6 %finish.1 = f32[480,512]{1,0:T(8,128)} custom-call(f32[2,128,512]{2,1,0:T(8,128)S(1)} %get-tuple-element.29.refs_0_, f32[2,128,512]{2,1,0:T(8,128)S(1)} %get-tuple-element.38.refs_1_, f32[1,128,512]{2,1,0:T(8,128)S(1)} %collective-permute-done.3.refs_2_, f32[1,128,512]{2,1,0:T(8,128)S(1)} %collective-permute-done.4.refs_3_, s32[1,512]{1,0:T(1,128)S(1)} %bitcast.8, ...), custom_call_target="tpu_custom_call" | custom-call | tf_op jit(solution)/shard_map/finish/pallas_call | solution.py:568
  (3 shorter events, 0.1 us)
Async XLA Ops:
  3.5 2.1 %collective-permute-start = (f32[264,512]{1,0:T(8,128)S(1)}, f32[264,512]{1,0:T(8,128)S(1)}, u32[]{:S(2)}, u32[]{:S(2)}) collective-permute-start(f32[264,512]{1,0:T(8,128)S(1)} %get-tuple-element.28), channel_id=1, source_target_pairs={{0,1},{1,0},{2,3},{3,2},{4,5},{5,4},{6,7},{7,6},{8,9},{9,8},{10,11... | collective-permute-start | bytes 1622024 | tf_op jit(solution)/shard_map/ppermute | solution.py:593
  8.8 22.1 %collective-permute-start.5 = (bf16[960,1920]{1,0:T(8,128)(2,1)}, bf16[960,1920]{1,0:T(8,128)(2,1)S(1)}, u32[]{:S(2)}, u32[]{:S(2)}) collective-permute-start(bf16[960,1920]{1,0:T(8,128)(2,1)} %own_w), channel_id=1, source_target_pairs={{0,1},{1,0},{2,3},{3,2},{4,5},{5,4},{6,7},{7,6},{8,9},{9,8},{10,11... | collective-permute-start | bytes 11059208 | tf_op jit(solution)/shard_map/ppermute | solution.py:593
  9.2 7.1 %collective-permute-start.1 = (s16[136,512]{1,0:T(8,128)(2,1)S(1)}, s16[136,512]{1,0:T(8,128)(2,1)S(1)}, u32[]{:S(2)}, u32[]{:S(2)}) collective-permute-start(s16[136,512]{1,0:T(8,128)(2,1)S(1)} %get-tuple-element.30), channel_id=1, source_target_pairs={{0,2},{1,3},{2,0},{3,1},{4,6},{5,7},{6,4},{7,5},{8,10},{9,11},{10,... | collective-permute-start | bytes 417800 | tf_op jit(solution)/shard_map/ppermute | solution.py:593
  11.8 6.9 %collective-permute-start.2 = (s16[136,512]{1,0:T(8,128)(2,1)S(1)}, s16[136,512]{1,0:T(8,128)(2,1)S(1)}, u32[]{:S(2)}, u32[]{:S(2)}) collective-permute-start(s16[136,512]{1,0:T(8,128)(2,1)S(1)} %get-tuple-element.31), channel_id=1, source_target_pairs={{0,3},{1,2},{2,1},{3,0},{4,7},{5,6},{6,5},{7,4},{8,11},{9,10},{10,... | collective-permute-start | bytes 417800 | tf_op jit(solution)/shard_map/ppermute | solution.py:593
  23.1 6.0 %collective-permute-start.9 = (bf16[4,256,128]{2,1,0:T(8,128)(2,1)S(1)}, bf16[4,256,128]{2,1,0:T(8,128)(2,1)S(1)}, u32[]{:S(2)}, u32[]{:S(2)}) collective-permute-start(bf16[4,256,128]{2,1,0:T(8,128)(2,1)S(1)} %get-tuple-element.44), channel_id=1, source_target_pairs={{0,1},{1,0},{2,3},{3,2},{4,5},{5,4},{6,7},{7,6},{8,9},{9,8},{10,11... | collective-permute-start | bytes 786440 | tf_op jit(solution)/shard_map/ppermute | solution.py:593
  23.3 6.5 %collective-permute-start.6 = (bf16[256,128]{1,0:T(8,128)(2,1)S(1)}, bf16[256,128]{1,0:T(8,128)(2,1)S(1)}, u32[]{:S(2)}, u32[]{:S(2)}) collective-permute-start(bf16[256,128]{1,0:T(8,128)(2,1)S(1)} %get-tuple-element.41), channel_id=1, source_target_pairs={{0,4},{4,8},{8,12},{12,0},{1,5},{5,9},{9,13},{13,1},{2,6},{6,10},{... | collective-permute-start | bytes 196616 | tf_op jit(solution)/shard_map/ppermute | solution.py:621
  25.1 10.1 %collective-permute-start.7 = (bf16[256,128]{1,0:T(8,128)(2,1)S(1)}, bf16[256,128]{1,0:T(8,128)(2,1)S(1)}, u32[]{:S(2)}, u32[]{:S(2)}) collective-permute-start(bf16[256,128]{1,0:T(8,128)(2,1)S(1)} %get-tuple-element.42), channel_id=1, source_target_pairs={{0,8},{4,12},{8,0},{12,4},{1,9},{5,13},{9,1},{13,5},{2,10},{6,14},... | collective-permute-start | bytes 196616 | tf_op jit(solution)/shard_map/ppermute | solution.py:621
  27.7 7.6 %collective-permute-start.8 = (bf16[256,128]{1,0:T(8,128)(2,1)S(1)}, bf16[256,128]{1,0:T(8,128)(2,1)S(1)}, u32[]{:S(2)}, u32[]{:S(2)}) collective-permute-start(bf16[256,128]{1,0:T(8,128)(2,1)S(1)} %get-tuple-element.43), channel_id=1, source_target_pairs={{0,12},{4,0},{8,4},{12,8},{1,13},{5,1},{9,5},{13,9},{2,14},{6,2},{... | collective-permute-start | bytes 196616 | tf_op jit(solution)/shard_map/ppermute | solution.py:621
  29.0 6.7 %collective-permute-start.10 = (bf16[256,128]{1,0:T(8,128)(2,1)S(1)}, bf16[256,128]{1,0:T(8,128)(2,1)S(1)}, u32[]{:S(2)}, u32[]{:S(2)}) collective-permute-start(bf16[256,128]{1,0:T(8,128)(2,1)S(1)} %get-tuple-element.51), channel_id=1, source_target_pairs={{0,4},{4,8},{8,12},{12,0},{1,5},{5,9},{9,13},{13,1},{2,6},{6,10},{... | collective-permute-start | bytes 196616 | tf_op jit(solution)/shard_map/ppermute | solution.py:622
  29.8 8.2 %collective-permute-start.11 = (bf16[256,128]{1,0:T(8,128)(2,1)S(1)}, bf16[256,128]{1,0:T(8,128)(2,1)S(1)}, u32[]{:S(2)}, u32[]{:S(2)}) collective-permute-start(bf16[256,128]{1,0:T(8,128)(2,1)S(1)} %get-tuple-element.50), channel_id=1, source_target_pairs={{0,8},{4,12},{8,0},{12,4},{1,9},{5,13},{9,1},{13,5},{2,10},{6,14},... | collective-permute-start | bytes 196616 | tf_op jit(solution)/shard_map/ppermute | solution.py:622
  30.9 7.1 %collective-permute-start.12 = (bf16[256,128]{1,0:T(8,128)(2,1)S(1)}, bf16[256,128]{1,0:T(8,128)(2,1)S(1)}, u32[]{:S(2)}, u32[]{:S(2)}) collective-permute-start(bf16[256,128]{1,0:T(8,128)(2,1)S(1)} %get-tuple-element.49), channel_id=1, source_target_pairs={{0,12},{4,0},{8,4},{12,8},{1,13},{5,1},{9,5},{13,9},{2,14},{6,2},{... | collective-permute-start | bytes 196616 | tf_op jit(solution)/shard_map/ppermute | solution.py:622
  35.2 15.7 %collective-permute-start.4 = (f32[1,128,512]{2,1,0:T(8,128)S(1)}, f32[1,128,512]{2,1,0:T(8,128)S(1)}, u32[]{:S(2)}, u32[]{:S(2)}) collective-permute-start(f32[1,128,512]{2,1,0:T(8,128)S(1)} %slice.16), channel_id=1, source_target_pairs={{0,1},{1,0},{2,3},{3,2},{4,5},{5,4},{6,7},{7,6},{8,9},{9,8},{10,11... | collective-permute-start | bytes 786440 | tf_op jit(solution)/shard_map/ppermute | solution.py:593
  35.2 15.6 %collective-permute-start.3 = (f32[1,128,512]{2,1,0:T(8,128)S(1)}, f32[1,128,512]{2,1,0:T(8,128)S(1)}, u32[]{:S(2)}, u32[]{:S(2)}) collective-permute-start(f32[1,128,512]{2,1,0:T(8,128)S(1)} %slice.15), channel_id=1, source_target_pairs={{0,1},{1,0},{2,3},{3,2},{4,5},{5,4},{6,7},{7,6},{8,9},{9,8},{10,11... | collective-permute-start | bytes 786440 | tf_op jit(solution)/shard_map/ppermute | solution.py:593
  38.0 20.8 %copy-start = (s32[512]{0:T(512)S(1)}, s32[512]{0:T(512)}, u32[]{:S(2)}) copy-start(s32[512]{0:T(512)} %param.8) | copy-start | bytes 6148
  46.5 8.1 %collective-permute-start.13 = (bf16[480,128]{1,0:T(8,128)(2,1)S(1)}, bf16[480,128]{1,0:T(8,128)(2,1)S(1)}, u32[]{:S(2)}, u32[]{:S(2)}) collective-permute-start(bf16[480,128]{1,0:T(8,128)(2,1)S(1)} %get-tuple-element.46), channel_id=1, source_target_pairs={{0,4},{4,8},{8,12},{12,0},{1,5},{5,9},{9,13},{13,1},{2,6},{6,10},{... | collective-permute-start | bytes 368648 | tf_op jit(solution)/shard_map/ppermute | solution.py:625
  48.4 10.4 %collective-permute-start.14 = (bf16[480,128]{1,0:T(8,128)(2,1)S(1)}, bf16[480,128]{1,0:T(8,128)(2,1)S(1)}, u32[]{:S(2)}, u32[]{:S(2)}) collective-permute-start(bf16[480,128]{1,0:T(8,128)(2,1)S(1)} %get-tuple-element.47), channel_id=1, source_target_pairs={{0,8},{4,12},{8,0},{12,4},{1,9},{5,13},{9,1},{13,5},{2,10},{6,14},... | collective-permute-start | bytes 368648 | tf_op jit(solution)/shard_map/ppermute | solution.py:625
  50.2 8.6 %collective-permute-start.15 = (bf16[480,128]{1,0:T(8,128)(2,1)S(1)}, bf16[480,128]{1,0:T(8,128)(2,1)S(1)}, u32[]{:S(2)}, u32[]{:S(2)}) collective-permute-start(bf16[480,128]{1,0:T(8,128)(2,1)S(1)} %get-tuple-element.48), channel_id=1, source_target_pairs={{0,12},{4,0},{8,4},{12,8},{1,13},{5,1},{9,5},{13,9},{2,14},{6,2},{... | collective-permute-start | bytes 368648 | tf_op jit(solution)/shard_map/ppermute | solution.py:625
